TPU v7x, 512 devices: a whole 4x4x16 slice. The times are simulated.
512 devices in a mesh: dp: 16 (over z_lo, y), tensor: 32 (over x, z_hi, core).
Axes of the slice: x: 4, y: 4, z: 16 (z_hi: 4, z_lo: 4; z = z_hi * 4 + z_lo), core: 2. Of those that a mesh axis runs over, the one named last changes fastest.
Arguments:
- tokens_in: bfloat16 [16384, 8192], P('dp', 'tensor'), may hold values from -6 to 6
- out_grad: bfloat16 [16384, 8192], P('dp', 'tensor'), may hold values from -6 to 6
- left_up: bfloat16 [8192, 256], P('tensor'), may hold values from -0.375 to 0.375
- right_up: bfloat16 [8192, 1024], P('tensor'), may hold values from -0.375 to 0.375
- left_down: bfloat16 [32768, 256], P('tensor'), may hold values from -0.1875 to 0.1875
- right_down: bfloat16 [8192, 256], P('tensor'), may hold values from -0.375 to 0.375
Outputs:
- layer_out: bfloat16 [16384, 8192], P('dp', 'tensor')
- input_grad: bfloat16 [16384, 8192], P('dp', 'tensor')
- grad_left_up: bfloat16 [8192, 256], P('tensor')
- grad_right_up: bfloat16 [8192, 1024], P('tensor')
- grad_left_down: bfloat16 [32768, 256], P('tensor')
- grad_right_down: bfloat16 [8192, 256], P('tensor')
All inputs are finite; a program needn't handle non-finite values.
Results may differ from a plain program's by a relative error of at most 0.0075.
Values may be sent and summed in bfloat16 or wider, within the bound.
No kernel may reach another device: no remote copies, remote signals or barrier semaphores. Data moves between devices by JAX's collectives and lax.ppermute only.
A program may use at most 64 MiB of HBM per device.

v0:
```python
import jax
import jax.numpy as jnp
from jax import lax
from jax.sharding import PartitionSpec as P


def gelu_tanh(values):
    return jax.nn.gelu(values, approximate=True)


def on_device(tokens_in, out_grad, left_up, right_up, left_down, right_down):
    blocks = lax.axis_size("tensor")
    tok_rows = tokens_in.shape[0]
    width = tokens_in.shape[1]
    sub_width = width // blocks
    hidden_width = right_up.shape[1]
    f32 = jnp.float32
    bf16 = jnp.bfloat16
    left_up_r = left_up.reshape(width, blocks, sub_width)
    right_up_r = right_up.reshape(blocks, sub_width, hidden_width)
    left_down_r = left_down.reshape(hidden_width, blocks, sub_width)
    right_down_r = right_down.reshape(blocks, sub_width, width)
    first = jnp.einsum("tk,kbs->bts", tokens_in, left_up_r, preferred_element_type=f32).astype(bf16)
    mixed_up = lax.all_to_all(
        first.reshape(blocks, tok_rows * sub_width),
        "tensor",
        split_axis=0,
        concat_axis=0,
        tiled=True,
    )
    mixed_up = mixed_up.reshape(blocks, tok_rows, sub_width)
    pre_act = jnp.einsum("bts,bsf->tf", mixed_up, right_up_r, preferred_element_type=f32)
    hidden = gelu_tanh(pre_act).astype(bf16)
    third = jnp.einsum("tf,fbs->bts", hidden, left_down_r, preferred_element_type=f32).astype(bf16)
    mixed_down = lax.all_to_all(
        third.reshape(blocks, tok_rows * sub_width),
        "tensor",
        split_axis=0,
        concat_axis=0,
        tiled=True,
    )
    mixed_down = mixed_down.reshape(blocks, tok_rows, sub_width)
    layer_out = jnp.einsum(
        "bts,bsk->tk", mixed_down, right_down_r, preferred_element_type=f32
    ).astype(bf16)
    part_right_down = jnp.einsum(
        "bts,tk->bsk", mixed_down, out_grad, preferred_element_type=f32
    ).reshape(width, width)
    back_mixed_down = jnp.einsum(
        "tk,bsk->bts", out_grad, right_down_r, preferred_element_type=f32
    ).astype(bf16)
    back_third = lax.all_to_all(
        back_mixed_down.reshape(blocks, tok_rows * sub_width),
        "tensor",
        split_axis=0,
        concat_axis=0,
        tiled=True,
    )
    back_third = back_third.reshape(blocks, tok_rows, sub_width)
    part_left_down = jnp.einsum(
        "tf,bts->fbs", hidden, back_third, preferred_element_type=f32
    ).reshape(hidden_width, width)
    back_hidden = jnp.einsum("bts,fbs->tf", back_third, left_down_r, preferred_element_type=f32)
    back_pre = jax.vjp(gelu_tanh, pre_act)[1](back_hidden)[0].astype(bf16)
    part_right_up = jnp.einsum(
        "bts,tf->bsf", mixed_up, back_pre, preferred_element_type=f32
    ).reshape(width, hidden_width)
    back_mixed_up = jnp.einsum(
        "tf,bsf->bts", back_pre, right_up_r, preferred_element_type=f32
    ).astype(bf16)
    back_first = lax.all_to_all(
        back_mixed_up.reshape(blocks, tok_rows * sub_width),
        "tensor",
        split_axis=0,
        concat_axis=0,
        tiled=True,
    )
    back_first = back_first.reshape(blocks, tok_rows, sub_width)
    part_left_up = jnp.einsum(
        "tk,bts->kbs", tokens_in, back_first, preferred_element_type=f32
    ).reshape(width, width)
    input_grad = jnp.einsum(
        "bts,kbs->tk", back_first, left_up_r, preferred_element_type=f32
    ).astype(bf16)
    part_left_up, part_right_up, part_left_down, part_right_down = lax.psum(
        (part_left_up, part_right_up, part_left_down, part_right_down), "dp"
    )
    return (
        layer_out,
        input_grad,
        part_left_up.astype(bf16),
        part_right_up.astype(bf16),
        part_left_down.astype(bf16),
        part_right_down.astype(bf16),
    )


def solution(mesh):
    return jax.shard_map(
        on_device,
        mesh=mesh,
        in_specs=(
            P("dp", "tensor"),
            P("dp", "tensor"),
            P("tensor", None),
            P("tensor", None),
            P("tensor", None),
            P("tensor", None),
        ),
        out_specs=(
            P("dp", "tensor"),
            P("dp", "tensor"),
            P("tensor", None),
            P("tensor", None),
            P("tensor", None),
            P("tensor", None),
        ),
        check_vma=False,
    )
```

profile of v0, /device:TPU:6, one launch (start us, length us, event | category | flops | bytes accessed | tf_op | source)
XLA Modules:
  0.0 314.1 jit_solution(4479751208924883557)
XLA Ops:
  0.6 1.5 fusion.30
  2.2 1.8 copy.53
  4.5 3.3 %reduce.2 = bf16[32,8192]{0,1:T(8,128)(2,1)} reduce(bf16[32,1,8192]{0,2,1:T(8,128)(2,1)S(1)} %bitcast.125, bf16[]{:T(256)} %broadcast.25), dimensions={1}, to_apply=%copy.54.reduce_sub_computation | reduce | bytes 1048578 | tf_op jit(solution)/shard_map/all_to_all | solution.py:52
  7.7 1.9 copy.73
  9.7 1.2 reshape.86
  10.8 18.2 %all-to-all-start.2 = ((bf16[32,2,4096]{2,1,0:T(2,128)(2,1)}), bf16[32,2,4096]{2,1,0:T(2,128)(2,1)S(1)}, u32[]{:S(2)}, u32[]{:S(2)}) async-start(bf16[32,2,4096]{2,1,0:T(2,128)(2,1)} %reshape.86), calls=%async_computation.2 | async-start | bytes 1048576 | tf_op jit(solution)/shard_map/all_to_all | solution.py:52
  30.3 2.7 copy.43
  33.1 3.2 %reduce = bf16[32,8192]{0,1:T(8,128)(2,1)} reduce(bf16[32,1,8192]{0,2,1:T(8,128)(2,1)S(1)} %bitcast.127, bf16[]{:T(256)} %broadcast.25), dimensions={1}, to_apply=%copy.44.reduce_sub_computation | reduce | bytes 1048578 | tf_op jit(solution)/shard_map/all_to_all | solution.py:24
  36.3 1.9 copy.71
  38.2 1.2 reshape.82
  39.4 15.9 %all-to-all-done.2 = bf16[32,2,4096]{2,1,0:T(2,128)(2,1)S(1)} async-done(((bf16[32,2,4096]{2,1,0:T(2,128)(2,1)}), bf16[32,2,4096]{2,1,0:T(2,128)(2,1)S(1)}, u32[]{:S(2)}, u32[]{:S(2)}) %all-to-all-start.2) | async-done | bytes 524320 | tf_op jit(solution)/shard_map/all_to_all | solution.py:52
  55.3 10.7 %all-to-all-start = ((bf16[32,2,4096]{2,1,0:T(2,128)(2,1)}), bf16[32,2,4096]{2,1,0:T(2,128)(2,1)}, u32[]{:S(2)}, u32[]{:S(2)}) async-start(bf16[32,2,4096]{2,1,0:T(2,128)(2,1)} %reshape.82), calls=%async_computation | async-start | bytes 1048576 | tf_op jit(solution)/shard_map/all_to_all | solution.py:24
  67.0 1.8 reshape.87
  68.8 2.9 copy.55
  71.7 1.9 copy.56
  73.7 12.8 %all-to-all-done = bf16[32,2,4096]{2,1,0:T(2,128)(2,1)} async-done(((bf16[32,2,4096]{2,1,0:T(2,128)(2,1)}), bf16[32,2,4096]{2,1,0:T(2,128)(2,1)}, u32[]{:S(2)}, u32[]{:S(2)}) %all-to-all-start) | async-done | bytes 524320 | tf_op jit(solution)/shard_map/all_to_all | solution.py:24
  86.5 4.4 %reshape.83 = bf16[32,1,8192]{2,1,0:T(2,128)(2,1)} reshape(bf16[32,2,4096]{2,1,0:T(2,128)(2,1)} %all-to-all-done) | data formatting | bytes 1048576
  90.9 4.0 %copy.45 = bf16[32,1,8192]{0,2,1:T(8,128)(2,1)} copy(bf16[32,1,8192]{2,1,0:T(2,128)(2,1)} %reshape.83) | data formatting | bytes 1048576 | tf_op jit(solution)/shard_map/all_to_all | solution.py:24
  94.9 3.7 %copy.46 = bf16[32,1024,8]{1,2,0:T(8,128)(2,1)} copy(bf16[32,1024,8]{0,2,1:T(8,128)(2,1)} %bitcast.120) | data formatting | bytes 1048576 | tf_op jit(solution)/shard_map/reshape | solution.py:31
  98.7 4.0 %fusion.10 = (bf16[1024,1024]{1,0:T(8,128)(2,1)}, f32[1024,1024,1]{1,0,2:T(8,128)S(1)}) fusion(bf16[32,1024,8]{1,2,0:T(8,128)(2,1)} %copy.46, bf16[256,1024]{1,0:T(8,128)(2,1)S(1)} %copy-done), kind=kOutput, calls=%fused_computation.15 | convolution fusion | flops 546308096 | bytes 7340032 | tf_op jit(solution)/shard_map/bts,bsf->tf/dot_general | solution.py:32
  102.7 3.3 %fusion.6 = bf16[1024,1024]{1,0:T(8,128)(2,1)S(1)} fusion(f32[1024,1024,1]{1,0,2:T(8,128)S(1)} %get-tuple-element.11, bf16[32,1024,8]{1,2,0:T(8,128)(2,1)S(1)} %copy.56, bf16[1024,256]{0,1:T(8,128)(2,1)S(1)} %copy-done.6), kind=kOutput, calls=%fused_computation.8 | convolution fusion | flops 557842432 | bytes 7340032 | tf_op jit(solution)/shard_map/bts,fbs->tf/dot_general | solution.py:63
  106.0 1.3 copy-done.2
  108.3 2.5 copy.58
  110.8 4.8 %reduce.3 = bf16[32,8192]{0,1:T(8,128)(2,1)} reduce(bf16[32,1,8192]{0,2,1:T(8,128)(2,1)} %bitcast.128, bf16[]{:T(256)} %broadcast.25), dimensions={1}, to_apply=%copy.59.reduce_sub_computation | reduce | bytes 1048578 | tf_op jit(solution)/shard_map/all_to_all | solution.py:71
  115.6 1.9 copy.74
  117.5 1.2 reshape.88
  118.7 17.7 %all-to-all-start.3 = ((bf16[32,2,4096]{2,1,0:T(2,128)(2,1)}), bf16[32,2,4096]{2,1,0:T(2,128)(2,1)S(1)}, u32[]{:S(2)}, u32[]{:S(2)}) async-start(bf16[32,2,4096]{2,1,0:T(2,128)(2,1)} %reshape.88), calls=%async_computation.3 | async-start | bytes 1048576 | tf_op jit(solution)/shard_map/all_to_all | solution.py:71
  136.4 3.5 %fusion.26 = bf16[32,1024,8]{1,0,2:T(8,128)(2,1)} fusion(bf16[1024,1024]{1,0:T(8,128)(2,1)} %get-tuple-element.10, bf16[1024,32,8]{0,2,1:T(8,128)(2,1)} %bitcast.129), kind=kOutput, calls=%fused_computation.29 | convolution fusion | flops 537133056 | bytes 3145728 | tf_op jit(solution)/shard_map/tf,fbs->bts/dot_general | solution.py:34
  139.8 3.4 %copy.49 = bf16[32,1024,8]{0,2,1:T(8,128)(2,1)} copy(bf16[32,1024,8]{1,0,2:T(8,128)(2,1)} %fusion.26) | data formatting | bytes 1048576 | tf_op jit(solution)/shard_map/convert_element_type | solution.py:34
  143.2 4.8 %reduce.1 = bf16[32,8192]{0,1:T(8,128)(2,1)} reduce(bf16[32,1,8192]{0,2,1:T(8,128)(2,1)} %bitcast.126, bf16[]{:T(256)} %broadcast.25), dimensions={1}, to_apply=%copy.50.reduce_sub_computation | reduce | bytes 1048578 | tf_op jit(solution)/shard_map/all_to_all | solution.py:35
  148.0 2.6 copy.72
  150.6 2.2 reshape.84
  152.8 4.0 %all-to-all-done.3 = bf16[32,2,4096]{2,1,0:T(2,128)(2,1)S(1)} async-done(((bf16[32,2,4096]{2,1,0:T(2,128)(2,1)}), bf16[32,2,4096]{2,1,0:T(2,128)(2,1)S(1)}, u32[]{:S(2)}, u32[]{:S(2)}) %all-to-all-start.3) | async-done | bytes 524320 | tf_op jit(solution)/shard_map/all_to_all | solution.py:71
  156.8 17.8 %all-to-all-start.1 = ((bf16[32,2,4096]{2,1,0:T(2,128)(2,1)}), bf16[32,2,4096]{2,1,0:T(2,128)(2,1)}, u32[]{:S(2)}, u32[]{:S(2)}) async-start(bf16[32,2,4096]{2,1,0:T(2,128)(2,1)} %reshape.84), calls=%async_computation.1 | async-start | bytes 1048576 | tf_op jit(solution)/shard_map/all_to_all | solution.py:35
  174.6 1.9 copy.65
  176.6 3.9 %copy.64 = bf16[32,8,1024]{2,1,0:T(8,128)(2,1)} copy(bf16[32,8,1024]{0,1,2:T(8,128)(2,1)} %bitcast.121) | data formatting | bytes 1048576 | tf_op jit(solution)/shard_map/bts,tf->bsf/dot_general | solution.py:65
  180.5 3.5 %fusion.35 = f32[256,1024]{1,0:T(8,128)} fusion(bf16[1024,1024]{1,0:T(8,128)(2,1)} %copy-done.2, bf16[32,8,1024]{2,1,0:T(8,128)(2,1)} %copy.64), kind=kOutput, calls=%fused_computation.37 | convolution fusion | flops 536870912 | bytes 3670016 | tf_op jit(solution)/shard_map/bts,tf->bsf/dot_general | solution.py:65
  183.9 1.7 fusion.33
  185.7 4.5 %reshape.89 = bf16[32,1,8192]{2,1,0:T(2,128)(2,1)} reshape(bf16[32,2,4096]{2,1,0:T(2,128)(2,1)} %copy-done.3) | data formatting | bytes 1048576
  190.1 2.9 copy.60
  193.0 1.9 copy.61
  195.0 1.3 convolution_bitcast_fusion.2
  197.5 4.5 %reshape.85 = bf16[32,1,8192]{2,1,0:T(2,128)(2,1)} reshape(bf16[32,2,4096]{2,1,0:T(2,128)(2,1)} %all-to-all-done.1) | data formatting | bytes 1048576
  202.0 2.9 copy.51
  204.9 1.9 copy.52
  208.0 1.9 copy.66
  210.0 1.3 fusion.31
  211.5 102.7 %all-reduce.2 = (bf16[256,256]{1,0:T(8,128)(2,1)}, bf16[256,1024]{1,0:T(8,128)(2,1)}, bf16[1024,256]{1,0:T(8,128)(2,1)}, bf16[256,256]{1,0:T(8,128)(2,1)}) all-reduce(f32[256,256]{1,0:T(8,128)S(1)} %copy.63, f32[256,1024]{1,0:T(8,128)} %fusion.35, f32[1024,256]{1,0:T(8,128)} %fusion.33, ...), channel_id=1, replica_groups=mesh['dp'=16,'tensor'=32] {'dp'}, use_global_device_ids=true, to_apply=%region_0.0 | all-reduce | flops 655360 | bytes 3932160 | tf_op jit(solution)/shard_map/psum | solution.py:85
  (26 shorter events, 6.2 us)
Async XLA Ops:
  0.6 98.0 %copy-start = (bf16[256,1024]{1,0:T(8,128)(2,1)S(1)}, bf16[256,1024]{1,0:T(8,128)(2,1)}, u32[]{:S(2)}) copy-start(bf16[256,1024]{1,0:T(8,128)(2,1)} %param.9) | copy-start | bytes 1572868
  4.5 24.6 %copy-start.8 = (bf16[256,256]{1,0:T(8,128)(2,1)S(1)}, bf16[256,256]{1,0:T(8,128)(2,1)}, u32[]{:S(2)}) copy-start(bf16[256,256]{1,0:T(8,128)(2,1)} %param.8) | copy-start | bytes 393220
  7.7 21.5 %copy-start.4 = (bf16[1024,256]{1,0:T(8,128)(2,1)S(1)}, bf16[1024,256]{1,0:T(8,128)(2,1)}, u32[]{:S(2)}) copy-start(bf16[1024,256]{1,0:T(8,128)(2,1)} %param.6) | copy-start | bytes 1572868
  10.8 44.5 %all-to-all-start.2 = ((bf16[32,2,4096]{2,1,0:T(2,128)(2,1)}), bf16[32,2,4096]{2,1,0:T(2,128)(2,1)S(1)}, u32[]{:S(2)}, u32[]{:S(2)}) async-start(bf16[32,2,4096]{2,1,0:T(2,128)(2,1)} %reshape.86), calls=%async_computation.2 | async-start | bytes 1048576 | tf_op jit(solution)/shard_map/all_to_all | solution.py:52
  36.3 29.7 %copy-start.5 = (bf16[1024,256]{1,0:T(8,128)(2,1)S(1)}, bf16[1024,256]{1,0:T(8,128)(2,1)}, u32[]{:S(2)}) copy-start(bf16[1024,256]{1,0:T(8,128)(2,1)} %param.10) | copy-start | bytes 1572868
  55.3 31.2 %all-to-all-start = ((bf16[32,2,4096]{2,1,0:T(2,128)(2,1)}), bf16[32,2,4096]{2,1,0:T(2,128)(2,1)}, u32[]{:S(2)}, u32[]{:S(2)}) async-start(bf16[32,2,4096]{2,1,0:T(2,128)(2,1)} %reshape.82), calls=%async_computation | async-start | bytes 1048576 | tf_op jit(solution)/shard_map/all_to_all | solution.py:24
  98.7 4.0 %copy-start.6 = (bf16[1024,256]{0,1:T(8,128)(2,1)S(1)}, bf16[1024,256]{0,1:T(8,128)(2,1)}, u32[]{:S(2)}) copy-start(bf16[1024,256]{0,1:T(8,128)(2,1)} %copy.47) | copy-start | bytes 1572868
  106.0 1.3 copy-start.2
  118.7 38.1 %all-to-all-start.3 = ((bf16[32,2,4096]{2,1,0:T(2,128)(2,1)}), bf16[32,2,4096]{2,1,0:T(2,128)(2,1)S(1)}, u32[]{:S(2)}, u32[]{:S(2)}) async-start(bf16[32,2,4096]{2,1,0:T(2,128)(2,1)} %reshape.88), calls=%async_computation.3 | async-start | bytes 1048576 | tf_op jit(solution)/shard_map/all_to_all | solution.py:71
  156.8 17.8 %copy-start.3 = (bf16[32,2,4096]{2,1,0:T(2,128)(2,1)}, bf16[32,2,4096]{2,1,0:T(2,128)(2,1)S(1)}, u32[]{:S(2)}) copy-start(bf16[32,2,4096]{2,1,0:T(2,128)(2,1)S(1)} %all-to-all-done.3) | copy-start | bytes 1572868
  156.8 40.7 %all-to-all-start.1 = ((bf16[32,2,4096]{2,1,0:T(2,128)(2,1)}), bf16[32,2,4096]{2,1,0:T(2,128)(2,1)}, u32[]{:S(2)}, u32[]{:S(2)}) async-start(bf16[32,2,4096]{2,1,0:T(2,128)(2,1)} %reshape.84), calls=%async_computation.1 | async-start | bytes 1048576 | tf_op jit(solution)/shard_map/all_to_all | solution.py:35
  176.6 7.4 %copy-start.1 = (bf16[1024,1024]{1,0:T(8,128)(2,1)S(1)}, bf16[1024,1024]{1,0:T(8,128)(2,1)}, u32[]{:S(2)}) copy-start(bf16[1024,1024]{1,0:T(8,128)(2,1)} %get-tuple-element.10) | copy-start | bytes 6291460
  197.5 9.4 %copy-start.7 = (bf16[256,256]{1,0:T(8,128)(2,1)S(1)}, bf16[256,256]{1,0:T(8,128)(2,1)}, u32[]{:S(2)}) copy-start(bf16[256,256]{1,0:T(8,128)(2,1)} %param.11) | copy-start | bytes 393220
where the time goes:
time: 319 us; the launch traced here: 314 us
  blocking collectives  103 us (32%)
  local copies, waits for them, and re-layouts  72.7 us (23%)
  starting transfers between devices  64.4 us (20%)
  waiting for transfers between devices  32.7 us (10%)
  matrix products  24.6 us (8%)
  other arithmetic  16.1 us (5%)
    psum x1, blocking collectives, on_device(): lax.psum((part_left_up, part_right_up, part_left_down, part_right_down),...  103 us
    unnamed x32, local copies, waits for them, and re-layouts  31.6 us
    all_to_all x1, starting transfers between devices, on_device(): lax.all_to_all(back_mixed_down.reshape(blocks, tok_rows * sub_width), 'te...  18.2 us
    all_to_all x1, starting transfers between devices, on_device(): lax.all_to_all(third.reshape(blocks, tok_rows * sub_width), 'tensor', spl...  17.8 us
    all_to_all x1, starting transfers between devices, on_device(): lax.all_to_all(back_mixed_up.reshape(blocks, tok_rows * sub_width), 'tens...  17.7 us
    all_to_all x1, waiting for transfers between devices, on_device(): lax.all_to_all(back_mixed_down.reshape(blocks, tok_rows * sub_width), 'te...  15.9 us
    all_to_all x1, waiting for transfers between devices, on_device(): lax.all_to_all(first.reshape(blocks, tok_rows * sub_width), 'tensor', spl...  12.8 us
    all_to_all x1, starting transfers between devices, on_device(): lax.all_to_all(first.reshape(blocks, tok_rows * sub_width), 'tensor', spl...  10.7 us
  transfers between devices with their start and end apart: 4, of which 3 were waited for; matrix products, arithmetic and copies ran while one was open for 18% of the time, Pallas kernels for 0%

commit v1 on v0

v1 whole, which is shorter than its diff:
```python
import jax
import jax.numpy as jnp
from jax import lax
from jax.experimental import pallas as pl
from jax.experimental.pallas import tpu as pltpu
from jax.sharding import PartitionSpec as P

F32 = jnp.float32
BF16 = jnp.bfloat16
GELU_C = 0.7978845608028654
GELU_A = 0.044715
NT = (((1,), (1,)), ((), ()))
NN = (((1,), (0,)), ((), ()))
TN = (((0,), (0,)), ((), ()))
PARAMS = pltpu.CompilerParams(vmem_limit_bytes=40 * 1024 * 1024)


def dot(left, right, dims=NN):
    return lax.dot_general(left, right, dims, preferred_element_type=F32)


def weave(upper, lower):
    tok = upper.shape[1]
    both = jnp.concatenate([upper.reshape(-1, 8, tok), lower.reshape(-1, 8, tok)], axis=1)
    return both.astype(BF16)


def unweave(both):
    tok = both.shape[2]
    wide = both.astype(F32)
    upper = wide[:, :8].reshape(-1, tok).astype(BF16)
    lower = wide[:, 8:].reshape(-1, tok).astype(BF16)
    return upper, lower


def entry_kernel(tok_ref, grad_ref, left_up_ref, right_down_ref, send_ref):
    left_up_t = left_up_ref[...].astype(F32).T.astype(BF16)
    first = dot(left_up_t, tok_ref[...], NT)
    back = dot(right_down_ref[...], grad_ref[...], NT)
    send_ref[...] = weave(first, back)


def middle_kernel(recv_ref, right_up_ref, right_up_t_ref, left_down_ref, left_down_t_ref,
                  send_ref, hidden_ref, back_pre_ref, mixed_ref, back_third_ref):
    mixed, back_third = unweave(recv_ref[...])
    mixed_ref[...] = mixed
    back_third_ref[...] = back_third
    pre = dot(right_up_t_ref[...], mixed)
    back_hidden = dot(left_down_ref[...], back_third)
    square = pre * pre
    tanh = jnp.tanh(GELU_C * (pre + GELU_A * (pre * square)))
    cdf = 0.5 * (1.0 + tanh)
    hidden = (pre * cdf).astype(BF16)
    slope = cdf + (0.5 * pre) * (1.0 - tanh * tanh) * (GELU_C * (1.0 + (3.0 * GELU_A) * square))
    back_pre = (back_hidden * slope).astype(BF16)
    hidden_ref[...] = hidden
    back_pre_ref[...] = back_pre
    third = dot(left_down_t_ref[...], hidden)
    back_mixed = dot(right_up_ref[...], back_pre)
    send_ref[...] = weave(third, back_mixed)


def middle_grads_kernel(hidden_ref, back_pre_ref, mixed_ref, back_third_ref, out_ref):
    out_ref[0, :256] = dot(hidden_ref[...], back_third_ref[...], NT).astype(BF16)
    out_ref[0, 256:] = dot(mixed_ref[...], back_pre_ref[...], NT).astype(BF16)


def exit_grads_kernel(recv_ref, tok_ref, grad_ref, out_ref, mixed_ref, back_first_ref):
    mixed, back_first = unweave(recv_ref[...])
    mixed_ref[...] = mixed
    back_first_ref[...] = back_first
    out_ref[:256] = dot(mixed, grad_ref[...]).astype(BF16)
    out_ref[256:] = dot(back_first, tok_ref[...]).T.astype(BF16)


def exit_kernel(mixed_ref, back_first_ref, left_up_ref, right_down_ref, out_ref, in_grad_ref):
    left_up_t = left_up_ref[...].astype(F32).T.astype(BF16)
    out_ref[...] = dot(mixed_ref[...], right_down_ref[...], TN).astype(BF16)
    in_grad_ref[...] = dot(back_first_ref[...], left_up_t, TN).astype(BF16)


def shape(dims, dtype=BF16):
    return jax.ShapeDtypeStruct(dims, dtype)


def shift_pairs(inner, step):
    pairs = []
    for z_lo in range(4):
        for y in range(4):
            to = (z_lo * 4 + (y + step) % 4) if inner else (((z_lo + step) % 4) * 4 + y)
            pairs.append((z_lo * 4 + y, to))
    return pairs


def scatter_sum(parts, place, inner):
    total = lax.dynamic_index_in_dim(parts, place, 0, keepdims=False).astype(F32)
    got = []
    for step in (2, 1, 3):
        chunk = lax.dynamic_index_in_dim(parts, (place + step) % 4, 0, keepdims=False)
        got.append(lax.ppermute(chunk, "dp", shift_pairs(inner, step)))
    for piece in got:
        total = total + piece.astype(F32)
    return total.astype(BF16)


def gather_parts(part, place, inner):
    got = [(step, lax.ppermute(part, "dp", shift_pairs(inner, step))) for step in (2, 1, 3)]
    whole = jnp.zeros((4,) + part.shape, part.dtype)
    whole = lax.dynamic_update_index_in_dim(whole, part, place, 0)
    for step, piece in got:
        whole = lax.dynamic_update_index_in_dim(whole, piece, (place + 4 - step) % 4, 0)
    return whole


def exchange(parts, axis):
    return lax.all_to_all(parts, axis, split_axis=0, concat_axis=0, tiled=True)


def on_device(tokens_in, out_grad, left_up, right_up, left_down, right_down):
    tok = tokens_in.shape[0]
    tile = 256
    dp_index = lax.axis_index("dp")
    y, z_lo = dp_index % 4, dp_index // 4

    send = pl.pallas_call(entry_kernel, out_shape=shape((32, 16, tok)), compiler_params=PARAMS)(
        tokens_in, out_grad, left_up, right_down)
    recv = exchange(send, "tensor")

    weight = lambda rows, cols: pl.BlockSpec((rows, cols), lambda i: (0, 0))
    column = lambda rows: pl.BlockSpec((rows, tile), lambda i: (0, i))
    woven = pl.BlockSpec((32, 16, tile), lambda i: (0, 0, i))
    send, hidden, back_pre, mixed_up, back_third = pl.pallas_call(
        middle_kernel,
        grid=(tok // tile,),
        in_specs=[woven, weight(256, 1024), weight(1024, 256), weight(1024, 256), weight(256, 1024)],
        out_specs=[woven, column(1024), column(1024), column(256), column(256)],
        out_shape=[shape((32, 16, tok)), shape((1024, tok)), shape((1024, tok)),
                   shape((256, tok)), shape((256, tok))],
        compiler_params=PARAMS,
    )(recv, right_up, right_up.T, left_down, left_down.T)
    recv = exchange(send, "tensor")

    parts = pl.pallas_call(
        middle_grads_kernel,
        grid=(4,),
        in_specs=[pl.BlockSpec((256, tok), lambda i: (i, 0)), pl.BlockSpec((256, tok), lambda i: (i, 0)),
                  weight(256, tok), weight(256, tok)],
        out_specs=pl.BlockSpec((1, 512, 256), lambda i: (i, 0, 0)),
        out_shape=shape((4, 512, 256)),
        compiler_params=PARAMS,
    )(hidden, back_pre, mixed_up, back_third)
    part = scatter_sum(parts, y, True)
    part = scatter_sum(part.reshape(4, 128, 256), z_lo, False)
    part = gather_parts(part, z_lo, False).reshape(512, 256)
    whole = gather_parts(part, y, True)
    grad_left_down = whole[:, :256].reshape(1024, 256)
    grad_right_up = whole[:, 256:].transpose(1, 0, 2).reshape(256, 1024)

    late, mixed_down, back_first = pl.pallas_call(
        exit_grads_kernel,
        out_shape=[shape((512, 256)), shape((256, tok)), shape((256, tok))],
        compiler_params=PARAMS,
    )(recv, tokens_in, out_grad)
    late = exchange(late.reshape(16, 32, 256), "dp")
    late = jnp.sum(late.astype(F32), axis=0).astype(BF16)
    late = exchange(jnp.broadcast_to(late[None], (16, 32, 256)), "dp").reshape(512, 256)

    layer_out, input_grad = pl.pallas_call(
        exit_kernel,
        out_shape=[shape((tok, 256)), shape((tok, 256))],
        compiler_params=PARAMS,
    )(mixed_down, back_first, left_up, right_down)
    return layer_out, input_grad, late[256:], grad_right_up, grad_left_down, late[:256]


def solution(mesh):
    rows = P("tensor", None)
    return jax.shard_map(
        on_device,
        mesh=mesh,
        in_specs=(P("dp", "tensor"), P("dp", "tensor"), rows, rows, rows, rows),
        out_specs=(P("dp", "tensor"), P("dp", "tensor"), rows, rows, rows, rows),
        check_vma=False,
    )
```

time: 319 us -> 206 us (0.65)
  blocking collectives: 103 us -> 0 us
  local copies, waits for them, and re-layouts: 72.7 us -> 17.8 us
  starting transfers between devices: 64.4 us -> 108 us
  waiting for transfers between devices: 32.7 us -> 63.1 us
  matrix products: 24.6 us -> 0 us
  other arithmetic: 16.1 us -> 2.17 us
  Pallas kernels: 0 us -> 11.7 us
    psum x1 -> x0, blocking collectives: 103 us -> none  [on_device(): lax.psum((part_left_up, part_right_up, part_left_down, part_right_down),...]
    ppermute x0 -> x12, starting transfers between devices: none -> 48.6 us  [the longest x6 24.3 us: gather_parts(): lax.ppermute(part, 'dp', shift_pairs(inner, step))]
    dot_general x12 -> x0, matrix products: 24.6 us -> none  [the longest x1 4 us: on_device(): jnp.einsum('bts,bsf->tf', mixed_up, right_up_r, preferred_element_type=f32)]
    all_to_all x4, waiting for transfers between devices: 32.7 us -> 55.5 us  [exchange(): return lax.all_to_all(parts, axis, split_axis=0, concat_axis=0, tiled=True)]
    unnamed x32 -> x42, local copies, waits for them, and re-layouts: 31.6 us -> 12.8 us
    all_to_all x4 -> x0, other arithmetic: 16.1 us -> none  [the longest x1 4.81 us: on_device(): lax.all_to_all(back_mixed_up.reshape(blocks, tok_rows * sub_width), 'tens...]
    all_to_all x5 -> x0, local copies, waits for them, and re-layouts: 13.3 us -> none  [the longest x2 4.53 us: on_device(): lax.all_to_all(first.reshape(blocks, tok_rows * sub_width), 'tensor', spl...]
    pallas_call x0 -> x5, Pallas kernels: none -> 11.7 us  [the longest x1 5.61 us: on_device(): pl.pallas_call(middle_kernel, grid=(tok // tile,), in_specs=[woven, weigh...]
  transfers between devices with their start and end apart: 4 -> 16, of which waited for: 3 -> 7; matrix products, arithmetic and copies ran while one was open for 18% -> 3% of each run, Pallas kernels for 0% -> 2%
where the time goes in v1:
time: 206 us; the launch traced here: 204 us
  starting transfers between devices  108 us (52%)
  waiting for transfers between devices  63.1 us (31%)
  local copies, waits for them, and re-layouts  17.8 us (9%)
  Pallas kernels  11.7 us (6%)
  other arithmetic  2.17 us (1%)
    all_to_all x4, starting transfers between devices, exchange(): return lax.all_to_all(parts, axis, split_axis=0, concat_axis=0, tiled=True)  59.3 us
    all_to_all x4, waiting for transfers between devices, exchange(): return lax.all_to_all(parts, axis, split_axis=0, concat_axis=0, tiled=True)  55.5 us
    ppermute x6, starting transfers between devices, gather_parts(): lax.ppermute(part, 'dp', shift_pairs(inner, step))  24.3 us
    ppermute x6, starting transfers between devices, scatter_sum(): got.append(lax.ppermute(chunk, 'dp', shift_pairs(inner, step)))  24.3 us
    unnamed x42, local copies, waits for them, and re-layouts  12.8 us
    ppermute x6, waiting for transfers between devices, scatter_sum(): got.append(lax.ppermute(chunk, 'dp', shift_pairs(inner, step)))  5.77 us
    pallas_call x1, Pallas kernels, on_device(): pl.pallas_call(middle_kernel, grid=(tok // tile,), in_specs=[woven, weigh...  5.61 us
  transfers between devices with their start and end apart: 16, of which 7 were waited for; matrix products, arithmetic and copies ran while one was open for 3% of the time, Pallas kernels for 2%

profile of v1, /device:TPU:6, one launch (start us, length us, event | category | flops | bytes accessed | tf_op | source)
XLA Modules:
  0.0 203.9 jit_solution(5655661136364562516)
XLA Ops:
  0.7 1.1 copy-done.6
  1.7 1.0 copy-done.8
  2.8 0.9 copy-done.15
  3.7 0.9 copy-done.17
  4.6 1.5 shard_map.109
  6.1 18.4 %all-to-all-start = ((bf16[32,16,1024]{2,1,0:T(8,128)(2,1)}), bf16[32,16,1024]{2,1,0:T(8,128)(2,1)S(1)}, u32[]{:S(2)}, u32[]{:S(2)}) async-start(bf16[32,16,1024]{2,1,0:T(8,128)(2,1)} %shard_map.109), calls=%async_computation | async-start | bytes 2097152 | tf_op jit(solution)/shard_map/all_to_all | solution.py:116
  24.7 0.2 copy.13
  24.9 49.0 %all-to-all-done.recv_ref = bf16[32,16,1024]{2,1,0:T(8,128)(2,1)S(1)} async-done(((bf16[32,16,1024]{2,1,0:T(8,128)(2,1)}), bf16[32,16,1024]{2,1,0:T(8,128)(2,1)S(1)}, u32[]{:S(2)}, u32[]{:S(2)}) %all-to-all-start) | async-done | bytes 1048608 | tf_op jit(solution)/shard_map/all_to_all | solution.py:116
  73.8 5.6 %shard_map.110 = (bf16[32,16,1024]{2,1,0:T(8,128)(2,1)S(1)}, bf16[1024,1024]{1,0:T(8,128)(2,1)S(1)}, bf16[1024,1024]{1,0:T(8,128)(2,1)S(1)}, bf16[256,1024]{1,0:T(8,128)(2,1)S(1)}, bf16[256,1024]{1,0:T(8,128)(2,1)S(1)}) custom-call(bf16[32,16,1024]{2,1,0:T(8,128)(2,1)S(1)} %all-to-all-done.recv_ref, bf16[256,1024]{1,0:T(8,128)(2,1)S(1)} %copy-done.4, ...), custom_call_target="tpu_custom_call" | custom-call | tf_op jit(solution)/shard_map/pallas_call | solution.py:132
  79.5 1.3 copy-done
  80.8 1.3 copy-done.2
  82.2 1.0 copy-done.10
  83.2 0.8 copy-done.11
  84.0 0.8 copy-done.13
  84.7 11.0 %all-to-all-start.1 = ((bf16[32,16,1024]{2,1,0:T(8,128)(2,1)}), bf16[32,16,1024]{2,1,0:T(8,128)(2,1)S(1)}, u32[]{:S(2)}, u32[]{:S(2)}) async-start(bf16[32,16,1024]{2,1,0:T(8,128)(2,1)} %copy-done.10), calls=%async_computation.1 | async-start | bytes 2097152 | tf_op jit(solution)/shard_map/all_to_all | solution.py:116
  95.9 1.6 copy-done.1
  97.4 1.6 copy-done.3
  99.0 1.9 shard_map.113
  101.0 0.9 dynamic-slice_bitcast_fusion.2
  101.9 5.1 %collective-permute-start = (bf16[512,256]{1,0:T(8,128)(2,1)}, bf16[512,256]{1,0:T(8,128)(2,1)S(1)}, u32[]{:S(2)}, u32[]{:S(2)}) collective-permute-start(bf16[512,256]{1,0:T(8,128)(2,1)} %get-tuple-element.30), channel_id=1, source_target_pairs={{0,64},{32,96},{64,0},{96,32},{128,192},{160,224},{192,128},{224,1... | collective-permute-start | bytes 786440 | tf_op jit(solution)/shard_map/ppermute | solution.py:100
  107.0 2.6 %collective-permute-start.1 = (bf16[512,256]{1,0:T(8,128)(2,1)}, bf16[512,256]{1,0:T(8,128)(2,1)}, u32[]{:S(2)}, u32[]{:S(2)}) collective-permute-start(bf16[512,256]{1,0:T(8,128)(2,1)} %get-tuple-element.32), channel_id=1, source_target_pairs={{0,32},{32,64},{64,96},{96,0},{128,160},{160,192},{192,224},{224,1... | collective-permute-start | bytes 786440 | tf_op jit(solution)/shard_map/ppermute | solution.py:100
  109.6 4.5 %collective-permute-start.2 = (bf16[512,256]{1,0:T(8,128)(2,1)}, bf16[512,256]{1,0:T(8,128)(2,1)}, u32[]{:S(2)}, u32[]{:S(2)}) collective-permute-start(bf16[512,256]{1,0:T(8,128)(2,1)} %get-tuple-element.31), channel_id=1, source_target_pairs={{0,96},{32,0},{64,32},{96,64},{128,224},{160,128},{192,160},{224,1... | collective-permute-start | bytes 786440 | tf_op jit(solution)/shard_map/ppermute | solution.py:100
  114.1 0.5 collective-permute-done
  114.6 4.9 %collective-permute-done.1 = bf16[512,256]{1,0:T(8,128)(2,1)} collective-permute-done((bf16[512,256]{1,0:T(8,128)(2,1)}, bf16[512,256]{1,0:T(8,128)(2,1)}, u32[]{:S(2)}, u32[]{:S(2)}) %collective-permute-start.1) | collective-permute-done | bytes 262176 | tf_op jit(solution)/shard_map/ppermute | solution.py:100
  119.6 0.3 collective-permute-done.2
  119.9 1.2 fusion.2
  121.1 0.7 dynamic-slice_bitcast_fusion.5
  121.8 4.5 %collective-permute-start.3 = (bf16[128,256]{1,0:T(8,128)(2,1)}, bf16[128,256]{1,0:T(8,128)(2,1)S(1)}, u32[]{:S(2)}, u32[]{:S(2)}) collective-permute-start(bf16[128,256]{1,0:T(8,128)(2,1)} %get-tuple-element.35), channel_id=1, source_target_pairs={{0,256},{32,288},{64,320},{96,352},{128,384},{160,416},{192,448},{... | collective-permute-start | bytes 196616 | tf_op jit(solution)/shard_map/ppermute | solution.py:100
  126.3 2.1 %collective-permute-start.4 = (bf16[128,256]{1,0:T(8,128)(2,1)}, bf16[128,256]{1,0:T(8,128)(2,1)S(1)}, u32[]{:S(2)}, u32[]{:S(2)}) collective-permute-start(bf16[128,256]{1,0:T(8,128)(2,1)} %get-tuple-element.37), channel_id=1, source_target_pairs={{0,128},{32,160},{64,192},{96,224},{128,256},{160,288},{192,320},{... | collective-permute-start | bytes 196616 | tf_op jit(solution)/shard_map/ppermute | solution.py:100
  128.5 5.5 %collective-permute-start.5 = (bf16[128,256]{1,0:T(8,128)(2,1)}, bf16[128,256]{1,0:T(8,128)(2,1)}, u32[]{:S(2)}, u32[]{:S(2)}) collective-permute-start(bf16[128,256]{1,0:T(8,128)(2,1)} %get-tuple-element.36), channel_id=1, source_target_pairs={{0,384},{32,416},{64,448},{96,480},{128,0},{160,32},{192,64},{224,... | collective-permute-start | bytes 196616 | tf_op jit(solution)/shard_map/ppermute | solution.py:100
  134.0 1.2 shard_map.111
  135.3 24.4 %all-to-all-start.2 = ((bf16[16,32,256]{2,1,0:T(8,128)(2,1)}), bf16[16,32,256]{2,1,0:T(8,128)(2,1)S(1)}, u32[]{:S(2)}, u32[]{:S(2)}) async-start(bf16[16,32,256]{2,1,0:T(8,128)(2,1)} %bitcast.2), calls=%async_computation.2 | async-start | bytes 524288 | tf_op jit(solution)/shard_map/all_to_all | solution.py:116
  159.7 0.9 bitcast_dynamic-update-slice_fusion.7
  160.6 4.7 %collective-permute-start.6 = (bf16[128,256]{1,0:T(8,128)(2,1)S(1)}, bf16[128,256]{1,0:T(8,128)(2,1)S(1)}, u32[]{:S(2)}, u32[]{:S(2)}) collective-permute-start(bf16[128,256]{1,0:T(8,128)(2,1)S(1)} %get-tuple-element.27), channel_id=1, source_target_pairs={{0,256},{32,288},{64,320},{96,352},{128,384},{160,416},{192,448},{... | collective-permute-start | bytes 196616 | tf_op jit(solution)/shard_map/ppermute | solution.py:107
  165.4 3.4 %collective-permute-start.7 = (bf16[128,256]{1,0:T(8,128)(2,1)S(1)}, bf16[128,256]{1,0:T(8,128)(2,1)S(1)}, u32[]{:S(2)}, u32[]{:S(2)}) collective-permute-start(bf16[128,256]{1,0:T(8,128)(2,1)S(1)} %get-tuple-element.27), channel_id=1, source_target_pairs={{0,128},{32,160},{64,192},{96,224},{128,256},{160,288},{192,320},{... | collective-permute-start | bytes 196616 | tf_op jit(solution)/shard_map/ppermute | solution.py:107
  168.7 4.3 %collective-permute-start.8 = (bf16[128,256]{1,0:T(8,128)(2,1)S(1)}, bf16[128,256]{1,0:T(8,128)(2,1)S(1)}, u32[]{:S(2)}, u32[]{:S(2)}) collective-permute-start(bf16[128,256]{1,0:T(8,128)(2,1)S(1)} %get-tuple-element.27), channel_id=1, source_target_pairs={{0,384},{32,416},{64,448},{96,480},{128,0},{160,32},{192,64},{224,... | collective-permute-start | bytes 196616 | tf_op jit(solution)/shard_map/ppermute | solution.py:107
  173.0 0.3 collective-permute-done.7
  173.3 1.6 collective-permute-done.8
  174.9 4.9 %collective-permute-start.9 = (bf16[512,256]{1,0:T(8,128)(2,1)S(1)}, bf16[512,256]{1,0:T(8,128)(2,1)S(1)}, u32[]{:S(2)}, u32[]{:S(2)}) collective-permute-start(bf16[512,256]{1,0:T(8,128)(2,1)S(1)} %bitcast.52), channel_id=1, source_target_pairs={{0,64},{32,96},{64,0},{96,32},{128,192},{160,224},{192,128},{224,1... | collective-permute-start | bytes 786440 | tf_op jit(solution)/shard_map/ppermute | solution.py:107
  179.8 2.5 %collective-permute-start.10 = (bf16[512,256]{1,0:T(8,128)(2,1)S(1)}, bf16[512,256]{1,0:T(8,128)(2,1)S(1)}, u32[]{:S(2)}, u32[]{:S(2)}) collective-permute-start(bf16[512,256]{1,0:T(8,128)(2,1)S(1)} %bitcast.53), channel_id=1, source_target_pairs={{0,32},{32,64},{64,96},{96,0},{128,160},{160,192},{192,224},{224,1... | collective-permute-start | bytes 786440 | tf_op jit(solution)/shard_map/ppermute | solution.py:107
  182.3 4.6 %collective-permute-start.11 = (bf16[512,256]{1,0:T(8,128)(2,1)S(1)}, bf16[512,256]{1,0:T(8,128)(2,1)S(1)}, u32[]{:S(2)}, u32[]{:S(2)}) collective-permute-start(bf16[512,256]{1,0:T(8,128)(2,1)S(1)} %bitcast.54), channel_id=1, source_target_pairs={{0,96},{32,0},{64,32},{96,64},{128,224},{160,128},{192,160},{224,1... | collective-permute-start | bytes 786440 | tf_op jit(solution)/shard_map/ppermute | solution.py:107
  186.9 0.7 broadcast_in_dim.38
  187.7 5.5 %all-to-all-start.3 = ((bf16[16,32,256]{2,1,0:T(8,128)(2,1)}), bf16[16,32,256]{2,1,0:T(8,128)(2,1)S(1)}, u32[]{:S(2)}, u32[]{:S(2)}) async-start(bf16[16,32,256]{2,1,0:T(8,128)(2,1)} %broadcast_in_dim.38), calls=%async_computation.3 | async-start | bytes 524288 | tf_op jit(solution)/shard_map/all_to_all | solution.py:116
  193.5 0.9 fusion.7
  194.3 0.9 copy.15
  195.2 1.5 shard_map.112
  196.7 6.5 %all-to-all-done.3 = bf16[16,32,256]{2,1,0:T(8,128)(2,1)S(1)} async-done(((bf16[16,32,256]{2,1,0:T(8,128)(2,1)}), bf16[16,32,256]{2,1,0:T(8,128)(2,1)S(1)}, u32[]{:S(2)}, u32[]{:S(2)}) %all-to-all-start.3) | async-done | bytes 262176 | tf_op jit(solution)/shard_map/all_to_all | solution.py:116
  203.2 0.7 fusion.8
  (49 shorter events, 0.6 us)
Async XLA Ops:
  0.6 23.8 %copy-start.4 = (bf16[256,1024]{1,0:T(8,128)(2,1)S(1)}, bf16[256,1024]{1,0:T(8,128)(2,1)}, u32[]{:S(2)}) copy-start(bf16[256,1024]{1,0:T(8,128)(2,1)} %right_up_ref.1) | copy-start | bytes 1572868
  0.6 1.1 copy-start.6
  1.7 1.0 copy-start.8
  2.8 0.9 copy-start.15
  3.7 0.9 copy-start.17
  6.1 18.6 %copy-start.5 = (bf16[1024,256]{1,0:T(8,128)(2,1)S(1)}, bf16[1024,256]{1,0:T(8,128)(2,1)}, u32[]{:S(2)}) copy-start(bf16[1024,256]{1,0:T(8,128)(2,1)} %left_down_ref.1) | copy-start | bytes 1572868
  6.1 67.8 %all-to-all-start = ((bf16[32,16,1024]{2,1,0:T(8,128)(2,1)}), bf16[32,16,1024]{2,1,0:T(8,128)(2,1)S(1)}, u32[]{:S(2)}, u32[]{:S(2)}) async-start(bf16[32,16,1024]{2,1,0:T(8,128)(2,1)} %shard_map.109), calls=%async_computation | async-start | bytes 2097152 | tf_op jit(solution)/shard_map/all_to_all | solution.py:116
  79.5 1.4 copy-start
  80.8 1.3 copy-start.2
  82.2 1.0 copy-start.10
  83.2 0.8 copy-start.11
  83.9 0.8 copy-start.13
  84.7 11.1 %copy-start.12 = (bf16[256,1024]{1,0:T(8,128)(2,1)S(1)}, bf16[256,1024]{1,0:T(8,128)(2,1)}, u32[]{:S(2)}) copy-start(bf16[256,1024]{1,0:T(8,128)(2,1)} %copy-done.11) | copy-start | bytes 1572868
  84.7 11.1 %copy-start.14 = (bf16[256,1024]{1,0:T(8,128)(2,1)S(1)}, bf16[256,1024]{1,0:T(8,128)(2,1)}, u32[]{:S(2)}) copy-start(bf16[256,1024]{1,0:T(8,128)(2,1)} %copy-done.13) | copy-start | bytes 1572868
  84.7 49.3 %all-to-all-start.1 = ((bf16[32,16,1024]{2,1,0:T(8,128)(2,1)}), bf16[32,16,1024]{2,1,0:T(8,128)(2,1)S(1)}, u32[]{:S(2)}, u32[]{:S(2)}) async-start(bf16[32,16,1024]{2,1,0:T(8,128)(2,1)} %copy-done.10), calls=%async_computation.1 | async-start | bytes 2097152 | tf_op jit(solution)/shard_map/all_to_all | solution.py:116
  95.8 1.6 copy-start.1
  97.4 1.6 copy-start.3
  101.0 33.1 %copy-start.7 = (bf16[1024,256]{1,0:T(8,128)(2,1)S(1)}, bf16[1024,256]{1,0:T(8,128)(2,1)}, u32[]{:S(2)}) copy-start(bf16[1024,256]{1,0:T(8,128)(2,1)} %tok_ref.3) | copy-start | bytes 1572868
  101.0 33.0 %copy-start.9 = (bf16[1024,256]{1,0:T(8,128)(2,1)S(1)}, bf16[1024,256]{1,0:T(8,128)(2,1)}, u32[]{:S(2)}) copy-start(bf16[1024,256]{1,0:T(8,128)(2,1)} %grad_ref.3) | copy-start | bytes 1572868
  101.9 12.7 %collective-permute-start = (bf16[512,256]{1,0:T(8,128)(2,1)}, bf16[512,256]{1,0:T(8,128)(2,1)S(1)}, u32[]{:S(2)}, u32[]{:S(2)}) collective-permute-start(bf16[512,256]{1,0:T(8,128)(2,1)} %get-tuple-element.30), channel_id=1, source_target_pairs={{0,64},{32,96},{64,0},{96,32},{128,192},{160,224},{192,128},{224,1... | collective-permute-start | bytes 786440 | tf_op jit(solution)/shard_map/ppermute | solution.py:100
  107.0 12.6 %collective-permute-start.1 = (bf16[512,256]{1,0:T(8,128)(2,1)}, bf16[512,256]{1,0:T(8,128)(2,1)}, u32[]{:S(2)}, u32[]{:S(2)}) collective-permute-start(bf16[512,256]{1,0:T(8,128)(2,1)} %get-tuple-element.32), channel_id=1, source_target_pairs={{0,32},{32,64},{64,96},{96,0},{128,160},{160,192},{192,224},{224,1... | collective-permute-start | bytes 786440 | tf_op jit(solution)/shard_map/ppermute | solution.py:100
  109.6 10.3 %collective-permute-start.2 = (bf16[512,256]{1,0:T(8,128)(2,1)}, bf16[512,256]{1,0:T(8,128)(2,1)}, u32[]{:S(2)}, u32[]{:S(2)}) collective-permute-start(bf16[512,256]{1,0:T(8,128)(2,1)} %get-tuple-element.31), channel_id=1, source_target_pairs={{0,96},{32,0},{64,32},{96,64},{128,224},{160,128},{192,160},{224,1... | collective-permute-start | bytes 786440 | tf_op jit(solution)/shard_map/ppermute | solution.py:100
  114.6 4.9 %copy-start.19 = (bf16[512,256]{1,0:T(8,128)(2,1)}, bf16[512,256]{1,0:T(8,128)(2,1)S(1)}, u32[]{:S(2)}) copy-start(bf16[512,256]{1,0:T(8,128)(2,1)S(1)} %collective-permute-done) | copy-start | bytes 786436
  121.8 37.8 %collective-permute-start.3 = (bf16[128,256]{1,0:T(8,128)(2,1)}, bf16[128,256]{1,0:T(8,128)(2,1)S(1)}, u32[]{:S(2)}, u32[]{:S(2)}) collective-permute-start(bf16[128,256]{1,0:T(8,128)(2,1)} %get-tuple-element.35), channel_id=1, source_target_pairs={{0,256},{32,288},{64,320},{96,352},{128,384},{160,416},{192,448},{... | collective-permute-start | bytes 196616 | tf_op jit(solution)/shard_map/ppermute | solution.py:100
  126.3 33.4 %collective-permute-start.4 = (bf16[128,256]{1,0:T(8,128)(2,1)}, bf16[128,256]{1,0:T(8,128)(2,1)S(1)}, u32[]{:S(2)}, u32[]{:S(2)}) collective-permute-start(bf16[128,256]{1,0:T(8,128)(2,1)} %get-tuple-element.37), channel_id=1, source_target_pairs={{0,128},{32,160},{64,192},{96,224},{128,256},{160,288},{192,320},{... | collective-permute-start | bytes 196616 | tf_op jit(solution)/shard_map/ppermute | solution.py:100
  128.5 31.2 %collective-permute-start.5 = (bf16[128,256]{1,0:T(8,128)(2,1)}, bf16[128,256]{1,0:T(8,128)(2,1)}, u32[]{:S(2)}, u32[]{:S(2)}) collective-permute-start(bf16[128,256]{1,0:T(8,128)(2,1)} %get-tuple-element.36), channel_id=1, source_target_pairs={{0,384},{32,416},{64,448},{96,480},{128,0},{160,32},{192,64},{224,... | collective-permute-start | bytes 196616 | tf_op jit(solution)/shard_map/ppermute | solution.py:100
  135.3 51.6 %all-to-all-start.2 = ((bf16[16,32,256]{2,1,0:T(8,128)(2,1)}), bf16[16,32,256]{2,1,0:T(8,128)(2,1)S(1)}, u32[]{:S(2)}, u32[]{:S(2)}) async-start(bf16[16,32,256]{2,1,0:T(8,128)(2,1)} %bitcast.2), calls=%async_computation.2 | async-start | bytes 524288 | tf_op jit(solution)/shard_map/all_to_all | solution.py:116
  160.6 12.4 %collective-permute-start.6 = (bf16[128,256]{1,0:T(8,128)(2,1)S(1)}, bf16[128,256]{1,0:T(8,128)(2,1)S(1)}, u32[]{:S(2)}, u32[]{:S(2)}) collective-permute-start(bf16[128,256]{1,0:T(8,128)(2,1)S(1)} %get-tuple-element.27), channel_id=1, source_target_pairs={{0,256},{32,288},{64,320},{96,352},{128,384},{160,416},{192,448},{... | collective-permute-start | bytes 196616 | tf_op jit(solution)/shard_map/ppermute | solution.py:107
  165.4 8.0 %collective-permute-start.7 = (bf16[128,256]{1,0:T(8,128)(2,1)S(1)}, bf16[128,256]{1,0:T(8,128)(2,1)S(1)}, u32[]{:S(2)}, u32[]{:S(2)}) collective-permute-start(bf16[128,256]{1,0:T(8,128)(2,1)S(1)} %get-tuple-element.27), channel_id=1, source_target_pairs={{0,128},{32,160},{64,192},{96,224},{128,256},{160,288},{192,320},{... | collective-permute-start | bytes 196616 | tf_op jit(solution)/shard_map/ppermute | solution.py:107
  168.7 6.2 %collective-permute-start.8 = (bf16[128,256]{1,0:T(8,128)(2,1)S(1)}, bf16[128,256]{1,0:T(8,128)(2,1)S(1)}, u32[]{:S(2)}, u32[]{:S(2)}) collective-permute-start(bf16[128,256]{1,0:T(8,128)(2,1)S(1)} %get-tuple-element.27), channel_id=1, source_target_pairs={{0,384},{32,416},{64,448},{96,480},{128,0},{160,32},{192,64},{224,... | collective-permute-start | bytes 196616 | tf_op jit(solution)/shard_map/ppermute | solution.py:107
  174.9 18.4 %collective-permute-start.9 = (bf16[512,256]{1,0:T(8,128)(2,1)S(1)}, bf16[512,256]{1,0:T(8,128)(2,1)S(1)}, u32[]{:S(2)}, u32[]{:S(2)}) collective-permute-start(bf16[512,256]{1,0:T(8,128)(2,1)S(1)} %bitcast.52), channel_id=1, source_target_pairs={{0,64},{32,96},{64,0},{96,32},{128,192},{160,224},{192,128},{224,1... | collective-permute-start | bytes 786440 | tf_op jit(solution)/shard_map/ppermute | solution.py:107
  179.8 13.6 %collective-permute-start.10 = (bf16[512,256]{1,0:T(8,128)(2,1)S(1)}, bf16[512,256]{1,0:T(8,128)(2,1)S(1)}, u32[]{:S(2)}, u32[]{:S(2)}) collective-permute-start(bf16[512,256]{1,0:T(8,128)(2,1)S(1)} %bitcast.53), channel_id=1, source_target_pairs={{0,32},{32,64},{64,96},{96,0},{128,160},{160,192},{192,224},{224,1... | collective-permute-start | bytes 786440 | tf_op jit(solution)/shard_map/ppermute | solution.py:107
  182.3 11.1 %collective-permute-start.11 = (bf16[512,256]{1,0:T(8,128)(2,1)S(1)}, bf16[512,256]{1,0:T(8,128)(2,1)S(1)}, u32[]{:S(2)}, u32[]{:S(2)}) collective-permute-start(bf16[512,256]{1,0:T(8,128)(2,1)S(1)} %bitcast.54), channel_id=1, source_target_pairs={{0,96},{32,0},{64,32},{96,64},{128,224},{160,128},{192,160},{224,1... | collective-permute-start | bytes 786440 | tf_op jit(solution)/shard_map/ppermute | solution.py:107
  187.7 15.5 %all-to-all-start.3 = ((bf16[16,32,256]{2,1,0:T(8,128)(2,1)}), bf16[16,32,256]{2,1,0:T(8,128)(2,1)S(1)}, u32[]{:S(2)}, u32[]{:S(2)}) async-start(bf16[16,32,256]{2,1,0:T(8,128)(2,1)} %broadcast_in_dim.38), calls=%async_computation.3 | async-start | bytes 524288 | tf_op jit(solution)/shard_map/all_to_all | solution.py:116
  193.4 1.8 copy-start.16
  193.4 1.8 copy-start.18

commit v2 on v1

--- a/solution.py
+++ b/solution.py
@@ -79,8 +79,20 @@
     in_grad_ref[...] = dot(back_first_ref[...], left_up_t, TN).astype(BF16)
 
 
-def shape(dims, dtype=BF16):
-    return jax.ShapeDtypeStruct(dims, dtype)
+def unpack_kernel(place_ref, own_ref, far_ref, near_ref, last_ref, left_down_ref, right_up_ref):
+    place = place_ref[0] & 3
+    for step, ref in ((0, own_ref), (2, far_ref), (1, near_ref), (3, last_ref)):
+        start = pl.multiple_of(((place + 4 - step) & 3) * 256, 256)
+        left_down_ref[pl.ds(start, 256), :] = ref[:256]
+        right_up_ref[:, pl.ds(start, 256)] = ref[256:]
+
+
+def hbm(dims):
+    return pltpu.HBM(dims, BF16)
+
+
+def in_hbm(array):
+    return pltpu.with_memory_space_constraint(array, pltpu.HBM)
 
 
 def shift_pairs(inner, step):
@@ -92,24 +104,23 @@
     return pairs
 
 
-def scatter_sum(parts, place, inner):
-    total = lax.dynamic_index_in_dim(parts, place, 0, keepdims=False).astype(F32)
-    got = []
-    for step in (2, 1, 3):
-        chunk = lax.dynamic_index_in_dim(parts, (place + step) % 4, 0, keepdims=False)
-        got.append(lax.ppermute(chunk, "dp", shift_pairs(inner, step)))
-    for piece in got:
-        total = total + piece.astype(F32)
-    return total.astype(BF16)
-
-
-def gather_parts(part, place, inner):
-    got = [(step, lax.ppermute(part, "dp", shift_pairs(inner, step))) for step in (2, 1, 3)]
-    whole = jnp.zeros((4,) + part.shape, part.dtype)
-    whole = lax.dynamic_update_index_in_dim(whole, part, place, 0)
-    for step, piece in got:
-        whole = lax.dynamic_update_index_in_dim(whole, piece, (place + 4 - step) % 4, 0)
-    return whole
+def permute(array, inner, step):
+    return lax.ppermute(array, "dp", shift_pairs(inner, step))
+
+
+def four_sum(own, near, far, last):
+    return ((own.astype(F32) + far.astype(F32)) + (near.astype(F32) + last.astype(F32))).astype(BF16)
+
+
+def scatter_sum_y(parts, y):
+    chunk = lambda step: lax.dynamic_index_in_dim(parts, (y + step) & 3, 0, keepdims=False)
+    far, near, last = (permute(chunk(step), True, step) for step in (2, 1, 3))
+    return four_sum(chunk(0), near, far, last)
+
+
+def all_sum_z(part):
+    far, near, last = (permute(part, False, step) for step in (2, 1, 3))
+    return four_sum(part, near, far, last)
 
 
 def exchange(parts, axis):
@@ -119,23 +130,29 @@
 def on_device(tokens_in, out_grad, left_up, right_up, left_down, right_down):
     tok = tokens_in.shape[0]
     tile = 256
-    dp_index = lax.axis_index("dp")
-    y, z_lo = dp_index % 4, dp_index // 4
-
-    send = pl.pallas_call(entry_kernel, out_shape=shape((32, 16, tok)), compiler_params=PARAMS)(
-        tokens_in, out_grad, left_up, right_down)
-    recv = exchange(send, "tensor")
+    y = lax.axis_index("dp") & 3
 
     weight = lambda rows, cols: pl.BlockSpec((rows, cols), lambda i: (0, 0))
+    row = pl.BlockSpec((tile, 256), lambda i: (i, 0))
     column = lambda rows: pl.BlockSpec((rows, tile), lambda i: (0, i))
     woven = pl.BlockSpec((32, 16, tile), lambda i: (0, 0, i))
+    send = pl.pallas_call(
+        entry_kernel,
+        grid=(tok // tile,),
+        in_specs=[row, row, weight(256, 256), weight(256, 256)],
+        out_specs=woven,
+        out_shape=hbm((32, 16, tok)),
+        compiler_params=PARAMS,
+    )(in_hbm(tokens_in), in_hbm(out_grad), in_hbm(left_up), in_hbm(right_down))
+    recv = exchange(send, "tensor")
+
     send, hidden, back_pre, mixed_up, back_third = pl.pallas_call(
         middle_kernel,
         grid=(tok // tile,),
         in_specs=[woven, weight(256, 1024), weight(1024, 256), weight(1024, 256), weight(256, 1024)],
         out_specs=[woven, column(1024), column(1024), column(256), column(256)],
-        out_shape=[shape((32, 16, tok)), shape((1024, tok)), shape((1024, tok)),
-                   shape((256, tok)), shape((256, tok))],
+        out_shape=[hbm((32, 16, tok)), hbm((1024, tok)), hbm((1024, tok)),
+                   hbm((256, tok)), hbm((256, tok))],
         compiler_params=PARAMS,
     )(recv, right_up, right_up.T, left_down, left_down.T)
     recv = exchange(send, "tensor")
@@ -146,30 +163,37 @@
         in_specs=[pl.BlockSpec((256, tok), lambda i: (i, 0)), pl.BlockSpec((256, tok), lambda i: (i, 0)),
                   weight(256, tok), weight(256, tok)],
         out_specs=pl.BlockSpec((1, 512, 256), lambda i: (i, 0, 0)),
-        out_shape=shape((4, 512, 256)),
-        compiler_params=PARAMS,
-    )(hidden, back_pre, mixed_up, back_third)
-    part = scatter_sum(parts, y, True)
-    part = scatter_sum(part.reshape(4, 128, 256), z_lo, False)
-    part = gather_parts(part, z_lo, False).reshape(512, 256)
-    whole = gather_parts(part, y, True)
-    grad_left_down = whole[:, :256].reshape(1024, 256)
-    grad_right_up = whole[:, 256:].transpose(1, 0, 2).reshape(256, 1024)
-
+        out_shape=hbm((4, 512, 256)),
+        compiler_params=PARAMS,
+    )(in_hbm(hidden), in_hbm(back_pre), in_hbm(mixed_up), in_hbm(back_third))
+    part = all_sum_z(scatter_sum_y(parts, y))
+    recv, part = lax.optimization_barrier((recv, part))
+    pieces = [part] + [permute(part, True, step) for step in (2, 1, 3)]
     late, mixed_down, back_first = pl.pallas_call(
         exit_grads_kernel,
-        out_shape=[shape((512, 256)), shape((256, tok)), shape((256, tok))],
+        out_shape=[hbm((512, 256)), hbm((256, tok)), hbm((256, tok))],
         compiler_params=PARAMS,
     )(recv, tokens_in, out_grad)
     late = exchange(late.reshape(16, 32, 256), "dp")
+    late, pieces = lax.optimization_barrier((late, pieces))
     late = jnp.sum(late.astype(F32), axis=0).astype(BF16)
     late = exchange(jnp.broadcast_to(late[None], (16, 32, 256)), "dp").reshape(512, 256)
 
+    grad_left_down, grad_right_up = pl.pallas_call(
+        unpack_kernel,
+        in_specs=[pl.BlockSpec(memory_space=pltpu.SMEM)] + [pl.BlockSpec(memory_space=pltpu.VMEM)] * 4,
+        out_shape=[hbm((1024, 256)), hbm((256, 1024))],
+        compiler_params=PARAMS,
+    )(y.astype(jnp.int32).reshape(1), *pieces)
+
     layer_out, input_grad = pl.pallas_call(
         exit_kernel,
-        out_shape=[shape((tok, 256)), shape((tok, 256))],
-        compiler_params=PARAMS,
-    )(mixed_down, back_first, left_up, right_down)
+        grid=(tok // tile,),
+        in_specs=[column(256), column(256), weight(256, 256), weight(256, 256)],
+        out_specs=[row, row],
+        out_shape=[hbm((tok, 256)), hbm((tok, 256))],
+        compiler_params=PARAMS,
+    )(in_hbm(mixed_down), in_hbm(back_first), in_hbm(left_up), in_hbm(right_down))
     return layer_out, input_grad, late[256:], grad_right_up, grad_left_down, late[:256]
 
 

time: 206 us -> 206 us (level)
  waiting for transfers between devices: 63.1 us -> 101 us
  starting transfers between devices: 108 us -> 76.8 us
  local copies, waits for them, and re-layouts: 17.8 us -> 3.13 us
  Pallas kernels: 11.7 us -> 21.7 us
    ppermute x12 -> x9, waiting for transfers between devices: 7.62 us -> 47.1 us  [permute(): return lax.ppermute(array, 'dp', shift_pairs(inner, step))]
    all_to_all x4, starting transfers between devices: 59.3 us -> 43.1 us  [exchange(): return lax.all_to_all(parts, axis, split_axis=0, concat_axis=0, tiled=True)]
    ppermute x12 -> x9, starting transfers between devices: 48.6 us -> 33.7 us  [permute(): return lax.ppermute(array, 'dp', shift_pairs(inner, step))]
    unnamed x42 -> x10, local copies, waits for them, and re-layouts: 12.8 us -> 0.42 us
    pallas_call x3 -> x4, Pallas kernels: 4.21 us -> 10.7 us  [the longest x1 4.17 us: on_device(): pl.pallas_call(exit_kernel, grid=(tok // tile,), in_specs=[column(256), c...]
    pallas_call x1, Pallas kernels: 1.93 us -> 5.16 us  [on_device(): pl.pallas_call(middle_grads_kernel, grid=(4,), in_specs=[pl.BlockSpec((25...]
  transfers between devices with their start and end apart: 16 -> 13, of which waited for: 7 -> 8; matrix products, arithmetic and copies ran while one was open for 3% -> 1% of each run, Pallas kernels for 2% -> 5%
where the time goes in v2:
time: 206 us; the launch traced here: 205 us
  waiting for transfers between devices  101 us (49%)
  starting transfers between devices  76.8 us (37%)
  Pallas kernels  21.7 us (11%)
  local copies, waits for them, and re-layouts  3.13 us (2%)
    all_to_all x4, waiting for transfers between devices, exchange(): return lax.all_to_all(parts, axis, split_axis=0, concat_axis=0, tiled=True)  53.8 us
    ppermute x9, waiting for transfers between devices, permute(): return lax.ppermute(array, 'dp', shift_pairs(inner, step))  47.1 us
    all_to_all x4, starting transfers between devices, exchange(): return lax.all_to_all(parts, axis, split_axis=0, concat_axis=0, tiled=True)  43.1 us
    ppermute x9, starting transfers between devices, permute(): return lax.ppermute(array, 'dp', shift_pairs(inner, step))  33.7 us
    pallas_call x1, Pallas kernels, on_device(): pl.pallas_call(middle_kernel, grid=(tok // tile,), in_specs=[woven, weigh...  5.83 us
    pallas_call x1, Pallas kernels, on_device(): pl.pallas_call(middle_grads_kernel, grid=(4,), in_specs=[pl.BlockSpec((25...  5.16 us
    pallas_call x1, Pallas kernels, on_device(): pl.pallas_call(exit_kernel, grid=(tok // tile,), in_specs=[column(256), c...  4.17 us
    pallas_call x1, Pallas kernels, on_device(): pl.pallas_call(entry_kernel, grid=(tok // tile,), in_specs=[row, row, wei...  4.15 us
  transfers between devices with their start and end apart: 13, of which 8 were waited for; matrix products, arithmetic and copies ran while one was open for 1% of the time, Pallas kernels for 5%

profile of v2, /device:TPU:6, one launch (start us, length us, event | category | flops | bytes accessed | tf_op | source)
XLA Modules:
  0.0 204.7 jit_solution(6182396365751815104)
XLA Ops:
  0.6 0.0 copy-start
  0.6 4.1 %shard_map.109 = bf16[32,16,1024]{2,1,0:T(8,128)(2,1)} custom-call(bf16[1024,256]{1,0:T(8,128)(2,1)} %tok_ref.3, bf16[1024,256]{1,0:T(8,128)(2,1)} %grad_ref.3, bf16[256,256]{1,0:T(8,128)(2,1)} %left_up_ref.3, bf16[256,256]{1,0:T(8,128)(2,1)} %right_down_ref.3), custom_call_target="tpu_custom_call" | custom-call | tf_op jit(solution)/shard_map/pallas_call | solution.py:139
  4.8 0.0 copy-start.1
  4.8 18.4 %all-to-all-start = ((bf16[32,16,1024]{2,1,0:T(8,128)(2,1)}), bf16[32,16,1024]{2,1,0:T(8,128)(2,1)S(1)}, u32[]{:S(2)}, u32[]{:S(2)}) async-start(bf16[32,16,1024]{2,1,0:T(8,128)(2,1)} %shard_map.109), calls=%async_computation | async-start | bytes 2097152 | tf_op jit(solution)/shard_map/all_to_all | solution.py:127
  23.2 0.0 copy-done
  23.2 0.2 copy.12
  23.4 0.0 copy-done.1
  23.4 0.2 copy.13
  23.6 49.0 %all-to-all-done.recv_ref = bf16[32,16,1024]{2,1,0:T(8,128)(2,1)S(1)} async-done(((bf16[32,16,1024]{2,1,0:T(8,128)(2,1)}), bf16[32,16,1024]{2,1,0:T(8,128)(2,1)S(1)}, u32[]{:S(2)}, u32[]{:S(2)}) %all-to-all-start) | async-done | bytes 1048608 | tf_op jit(solution)/shard_map/all_to_all | solution.py:127
  72.6 5.8 %shard_map.110 = (bf16[32,16,1024]{2,1,0:T(8,128)(2,1)}, bf16[1024,1024]{1,0:T(8,128)(2,1)}, bf16[1024,1024]{1,0:T(8,128)(2,1)}, bf16[256,1024]{1,0:T(8,128)(2,1)}, bf16[256,1024]{1,0:T(8,128)(2,1)}) custom-call(bf16[32,16,1024]{2,1,0:T(8,128)(2,1)S(1)} %all-to-all-done.recv_ref, bf16[256,1024]{1,0:T(8,128)(2,1)S(1)} %copy-done, ...), custom_call_target="tpu_custom_call" | custom-call | tf_op jit(solution)/shard_map/pallas_call | solution.py:149
  78.4 10.8 %all-to-all-start.1 = ((bf16[32,16,1024]{2,1,0:T(8,128)(2,1)}), bf16[32,16,1024]{2,1,0:T(8,128)(2,1)S(1)}, u32[]{:S(2)}, u32[]{:S(2)}) async-start(bf16[32,16,1024]{2,1,0:T(8,128)(2,1)} %get-tuple-element.25), calls=%async_computation.1 | async-start | bytes 2097152 | tf_op jit(solution)/shard_map/all_to_all | solution.py:127
  89.3 5.2 %shard_map.111 = bf16[4,512,256]{2,1,0:T(8,128)(2,1)} custom-call(bf16[1024,1024]{1,0:T(8,128)(2,1)} %get-tuple-element.26.hidden_ref, bf16[1024,1024]{1,0:T(8,128)(2,1)} %get-tuple-element.27.back_pre_ref, bf16[256,1024]{1,0:T(8,128)(2,1)} %get-tuple-element.28.mixed_ref, bf16[256,1024]{1,0:T(8,128)(2,1)} %get-tuple-element.29.back_third_ref), custom_call_target="tpu_custom_call" | custom-call | tf_op jit(solution)/shard_map/pallas_call | solution.py:160
  94.4 0.0 copy-start.2
  94.4 0.0 copy-start.3
  94.5 1.3 dynamic-slice_bitcast_fusion.2
  95.7 4.9 %collective-permute-start.2 = (bf16[512,256]{1,0:T(8,128)(2,1)S(1)}, bf16[512,256]{1,0:T(8,128)(2,1)S(1)}, u32[]{:S(2)}, u32[]{:S(2)}) collective-permute-start(bf16[512,256]{1,0:T(8,128)(2,1)S(1)} %get-tuple-element.45), channel_id=1, source_target_pairs={{0,96},{32,0},{64,32},{96,64},{128,224},{160,128},{192,160},{224,1... | collective-permute-start | bytes 786440 | tf_op jit(solution)/shard_map/ppermute | solution.py:108
  100.6 1.9 collective-permute-start.1
  102.5 4.1 %collective-permute-start = (bf16[512,256]{1,0:T(8,128)(2,1)S(1)}, bf16[512,256]{1,0:T(8,128)(2,1)}, u32[]{:S(2)}, u32[]{:S(2)}) collective-permute-start(bf16[512,256]{1,0:T(8,128)(2,1)S(1)} %get-tuple-element.44), channel_id=1, source_target_pairs={{0,64},{32,96},{64,0},{96,32},{128,192},{160,224},{192,128},{224,1... | collective-permute-start | bytes 786440 | tf_op jit(solution)/shard_map/ppermute | solution.py:108
  106.6 0.0 collective-permute-done.2
  106.6 10.8 %collective-permute-done.1 = bf16[512,256]{1,0:T(8,128)(2,1)S(1)} collective-permute-done((bf16[512,256]{1,0:T(8,128)(2,1)S(1)}, bf16[512,256]{1,0:T(8,128)(2,1)S(1)}, u32[]{:S(2)}, u32[]{:S(2)}) %collective-permute-start.1) | collective-permute-done | bytes 262176 | tf_op jit(solution)/shard_map/ppermute | solution.py:108
  117.4 0.0 collective-permute-done
  117.4 1.2 fusion.1
  118.5 4.2 %collective-permute-start.5 = (bf16[512,256]{1,0:T(8,128)(2,1)S(1)}, bf16[512,256]{1,0:T(8,128)(2,1)S(1)}, u32[]{:S(2)}, u32[]{:S(2)}) collective-permute-start(bf16[512,256]{1,0:T(8,128)(2,1)S(1)} %fusion.1), channel_id=1, source_target_pairs={{0,384},{32,416},{64,448},{96,480},{128,0},{160,32},{192,64},{224,... | collective-permute-start | bytes 786440 | tf_op jit(solution)/shard_map/ppermute | solution.py:108
  122.7 1.9 collective-permute-start.4
  124.7 4.4 %collective-permute-start.3 = (bf16[512,256]{1,0:T(8,128)(2,1)S(1)}, bf16[512,256]{1,0:T(8,128)(2,1)S(1)}, u32[]{:S(2)}, u32[]{:S(2)}) collective-permute-start(bf16[512,256]{1,0:T(8,128)(2,1)S(1)} %fusion.1), channel_id=1, source_target_pairs={{0,256},{32,288},{64,320},{96,352},{128,384},{160,416},{192,448},{... | collective-permute-start | bytes 786440 | tf_op jit(solution)/shard_map/ppermute | solution.py:108
  129.0 16.6 %collective-permute-done.5 = bf16[512,256]{1,0:T(8,128)(2,1)S(1)} collective-permute-done((bf16[512,256]{1,0:T(8,128)(2,1)S(1)}, bf16[512,256]{1,0:T(8,128)(2,1)S(1)}, u32[]{:S(2)}, u32[]{:S(2)}) %collective-permute-start.5) | collective-permute-done | bytes 262176 | tf_op jit(solution)/shard_map/ppermute | solution.py:108
  145.6 7.5 %collective-permute-done.4 = bf16[512,256]{1,0:T(8,128)(2,1)S(1)} collective-permute-done((bf16[512,256]{1,0:T(8,128)(2,1)S(1)}, bf16[512,256]{1,0:T(8,128)(2,1)S(1)}, u32[]{:S(2)}, u32[]{:S(2)}) %collective-permute-start.4) | collective-permute-done | bytes 262176 | tf_op jit(solution)/shard_map/ppermute | solution.py:108
  153.1 7.0 %collective-permute-done.3 = bf16[512,256]{1,0:T(8,128)(2,1)S(1)} collective-permute-done((bf16[512,256]{1,0:T(8,128)(2,1)S(1)}, bf16[512,256]{1,0:T(8,128)(2,1)S(1)}, u32[]{:S(2)}, u32[]{:S(2)}) %collective-permute-start.3) | collective-permute-done | bytes 262176 | tf_op jit(solution)/shard_map/ppermute | solution.py:108
  160.1 0.1 add_convert_fusion.own_ref
  160.3 0.0 all-to-all-done.1.recv_ref
  160.3 0.0 copy-done.2
  160.3 0.0 copy-done.3
  160.3 1.3 shard_map.112
  161.6 7.5 %all-to-all-start.2 = ((bf16[16,32,256]{2,1,0:T(8,128)(2,1)}), bf16[16,32,256]{2,1,0:T(8,128)(2,1)S(1)}, u32[]{:S(2)}, u32[]{:S(2)}) async-start(bf16[16,32,256]{2,1,0:T(8,128)(2,1)} %bitcast.17), calls=%async_computation.2 | async-start | bytes 524288 | tf_op jit(solution)/shard_map/all_to_all | solution.py:127
  169.1 5.3 %collective-permute-start.6 = (bf16[512,256]{1,0:T(8,128)(2,1)S(1)}, bf16[512,256]{1,0:T(8,128)(2,1)S(1)}, u32[]{:S(2)}, u32[]{:S(2)}) collective-permute-start(bf16[512,256]{1,0:T(8,128)(2,1)S(1)} %add_convert_fusion.own_ref), channel_id=1, source_target_pairs={{0,64},{32,96},{64,0},{96,32},{128,192},{160,224},{192,128},{224,1... | collective-permute-start | bytes 786440 | tf_op jit(solution)/shard_map/ppermute | solution.py:108
  174.5 2.5 %collective-permute-start.7 = (bf16[512,256]{1,0:T(8,128)(2,1)S(1)}, bf16[512,256]{1,0:T(8,128)(2,1)S(1)}, u32[]{:S(2)}, u32[]{:S(2)}) collective-permute-start(bf16[512,256]{1,0:T(8,128)(2,1)S(1)} %add_convert_fusion.own_ref), channel_id=1, source_target_pairs={{0,32},{32,64},{64,96},{96,0},{128,160},{160,192},{192,224},{224,1... | collective-permute-start | bytes 786440 | tf_op jit(solution)/shard_map/ppermute | solution.py:108
  176.9 4.6 %collective-permute-start.8 = (bf16[512,256]{1,0:T(8,128)(2,1)S(1)}, bf16[512,256]{1,0:T(8,128)(2,1)S(1)}, u32[]{:S(2)}, u32[]{:S(2)}) collective-permute-start(bf16[512,256]{1,0:T(8,128)(2,1)S(1)} %add_convert_fusion.own_ref), channel_id=1, source_target_pairs={{0,96},{32,0},{64,32},{96,64},{128,224},{160,128},{192,160},{224,1... | collective-permute-start | bytes 786440 | tf_op jit(solution)/shard_map/ppermute | solution.py:108
  181.5 1.3 collective-permute-done.6.far_ref
  182.8 3.9 %collective-permute-done.7.near_ref = bf16[512,256]{1,0:T(8,128)(2,1)S(1)} collective-permute-done((bf16[512,256]{1,0:T(8,128)(2,1)S(1)}, bf16[512,256]{1,0:T(8,128)(2,1)S(1)}, u32[]{:S(2)}, u32[]{:S(2)}) %collective-permute-start.7) | collective-permute-done | bytes 262176 | tf_op jit(solution)/shard_map/ppermute | solution.py:108
  186.7 0.0 collective-permute-done.8.last_ref
  186.7 0.0 all-to-all-done.2
  186.8 0.7 broadcast_in_dim.2
  187.5 6.4 %all-to-all-start.3 = ((bf16[16,32,256]{2,1,0:T(8,128)(2,1)}), bf16[16,32,256]{2,1,0:T(8,128)(2,1)S(1)}, u32[]{:S(2)}, u32[]{:S(2)}) async-start(bf16[16,32,256]{2,1,0:T(8,128)(2,1)} %broadcast_in_dim.2), calls=%async_computation.3 | async-start | bytes 524288 | tf_op jit(solution)/shard_map/all_to_all | solution.py:127
  194.0 4.2 %shard_map.113 = (bf16[1024,256]{1,0:T(8,128)(2,1)}, bf16[1024,256]{1,0:T(8,128)(2,1)}) custom-call(bf16[256,1024]{1,0:T(8,128)(2,1)} %get-tuple-element.31.mixed_ref, bf16[256,1024]{1,0:T(8,128)(2,1)} %get-tuple-element.32.back_first_ref, bf16[256,256]{1,0:T(8,128)(2,1)} %left_up_ref.3, bf16[256,256]{1,0:T(8,128)(2,1)} %right_down_ref.3), custom_call_target="tpu_custom_call" | custom-call | tf_op jit(solution)/shard_map/pallas_call | solution.py:189
  198.1 1.1 shard_map.114
  199.2 4.8 %all-to-all-done.3 = bf16[16,32,256]{2,1,0:T(8,128)(2,1)S(1)} async-done(((bf16[16,32,256]{2,1,0:T(8,128)(2,1)}), bf16[16,32,256]{2,1,0:T(8,128)(2,1)S(1)}, u32[]{:S(2)}, u32[]{:S(2)}) %all-to-all-start.3) | async-done | bytes 262176 | tf_op jit(solution)/shard_map/all_to_all | solution.py:127
  204.0 0.7 fusion.2
  (1 shorter events, 0.0 us)
Async XLA Ops:
  0.6 22.5 %copy-start = (bf16[256,1024]{1,0:T(8,128)(2,1)S(1)}, bf16[256,1024]{1,0:T(8,128)(2,1)}, u32[]{:S(2)}) copy-start(bf16[256,1024]{1,0:T(8,128)(2,1)} %right_up_ref.1) | copy-start | bytes 1572868
  4.8 18.6 %copy-start.1 = (bf16[1024,256]{1,0:T(8,128)(2,1)S(1)}, bf16[1024,256]{1,0:T(8,128)(2,1)}, u32[]{:S(2)}) copy-start(bf16[1024,256]{1,0:T(8,128)(2,1)} %left_down_ref.1) | copy-start | bytes 1572868
  4.8 67.8 %all-to-all-start = ((bf16[32,16,1024]{2,1,0:T(8,128)(2,1)}), bf16[32,16,1024]{2,1,0:T(8,128)(2,1)S(1)}, u32[]{:S(2)}, u32[]{:S(2)}) async-start(bf16[32,16,1024]{2,1,0:T(8,128)(2,1)} %shard_map.109), calls=%async_computation | async-start | bytes 2097152 | tf_op jit(solution)/shard_map/all_to_all | solution.py:127
  78.4 81.8 %all-to-all-start.1 = ((bf16[32,16,1024]{2,1,0:T(8,128)(2,1)}), bf16[32,16,1024]{2,1,0:T(8,128)(2,1)S(1)}, u32[]{:S(2)}, u32[]{:S(2)}) async-start(bf16[32,16,1024]{2,1,0:T(8,128)(2,1)} %get-tuple-element.25), calls=%async_computation.1 | async-start | bytes 2097152 | tf_op jit(solution)/shard_map/all_to_all | solution.py:127
  94.4 65.8 %copy-start.2 = (bf16[1024,256]{1,0:T(8,128)(2,1)S(1)}, bf16[1024,256]{1,0:T(8,128)(2,1)}, u32[]{:S(2)}) copy-start(bf16[1024,256]{1,0:T(8,128)(2,1)} %tok_ref.3) | copy-start | bytes 1572868
  94.4 65.9 %copy-start.3 = (bf16[1024,256]{1,0:T(8,128)(2,1)S(1)}, bf16[1024,256]{1,0:T(8,128)(2,1)}, u32[]{:S(2)}) copy-start(bf16[1024,256]{1,0:T(8,128)(2,1)} %grad_ref.3) | copy-start | bytes 1572868
  95.7 10.9 %collective-permute-start.2 = (bf16[512,256]{1,0:T(8,128)(2,1)S(1)}, bf16[512,256]{1,0:T(8,128)(2,1)S(1)}, u32[]{:S(2)}, u32[]{:S(2)}) collective-permute-start(bf16[512,256]{1,0:T(8,128)(2,1)S(1)} %get-tuple-element.45), channel_id=1, source_target_pairs={{0,96},{32,0},{64,32},{96,64},{128,224},{160,128},{192,160},{224,1... | collective-permute-start | bytes 786440 | tf_op jit(solution)/shard_map/ppermute | solution.py:108
  100.6 16.8 %collective-permute-start.1 = (bf16[512,256]{1,0:T(8,128)(2,1)S(1)}, bf16[512,256]{1,0:T(8,128)(2,1)S(1)}, u32[]{:S(2)}, u32[]{:S(2)}) collective-permute-start(bf16[512,256]{1,0:T(8,128)(2,1)S(1)} %get-tuple-element.46), channel_id=1, source_target_pairs={{0,32},{32,64},{64,96},{96,0},{128,160},{160,192},{192,224},{224,1... | collective-permute-start | bytes 786440 | tf_op jit(solution)/shard_map/ppermute | solution.py:108
  102.5 14.9 %collective-permute-start = (bf16[512,256]{1,0:T(8,128)(2,1)S(1)}, bf16[512,256]{1,0:T(8,128)(2,1)}, u32[]{:S(2)}, u32[]{:S(2)}) collective-permute-start(bf16[512,256]{1,0:T(8,128)(2,1)S(1)} %get-tuple-element.44), channel_id=1, source_target_pairs={{0,64},{32,96},{64,0},{96,32},{128,192},{160,224},{192,128},{224,1... | collective-permute-start | bytes 786440 | tf_op jit(solution)/shard_map/ppermute | solution.py:108
  118.5 27.1 %collective-permute-start.5 = (bf16[512,256]{1,0:T(8,128)(2,1)S(1)}, bf16[512,256]{1,0:T(8,128)(2,1)S(1)}, u32[]{:S(2)}, u32[]{:S(2)}) collective-permute-start(bf16[512,256]{1,0:T(8,128)(2,1)S(1)} %fusion.1), channel_id=1, source_target_pairs={{0,384},{32,416},{64,448},{96,480},{128,0},{160,32},{192,64},{224,... | collective-permute-start | bytes 786440 | tf_op jit(solution)/shard_map/ppermute | solution.py:108
  122.7 30.4 %collective-permute-start.4 = (bf16[512,256]{1,0:T(8,128)(2,1)S(1)}, bf16[512,256]{1,0:T(8,128)(2,1)S(1)}, u32[]{:S(2)}, u32[]{:S(2)}) collective-permute-start(bf16[512,256]{1,0:T(8,128)(2,1)S(1)} %fusion.1), channel_id=1, source_target_pairs={{0,128},{32,160},{64,192},{96,224},{128,256},{160,288},{192,320},{... | collective-permute-start | bytes 786440 | tf_op jit(solution)/shard_map/ppermute | solution.py:108
  124.7 35.5 %collective-permute-start.3 = (bf16[512,256]{1,0:T(8,128)(2,1)S(1)}, bf16[512,256]{1,0:T(8,128)(2,1)S(1)}, u32[]{:S(2)}, u32[]{:S(2)}) collective-permute-start(bf16[512,256]{1,0:T(8,128)(2,1)S(1)} %fusion.1), channel_id=1, source_target_pairs={{0,256},{32,288},{64,320},{96,352},{128,384},{160,416},{192,448},{... | collective-permute-start | bytes 786440 | tf_op jit(solution)/shard_map/ppermute | solution.py:108
  161.6 25.1 %all-to-all-start.2 = ((bf16[16,32,256]{2,1,0:T(8,128)(2,1)}), bf16[16,32,256]{2,1,0:T(8,128)(2,1)S(1)}, u32[]{:S(2)}, u32[]{:S(2)}) async-start(bf16[16,32,256]{2,1,0:T(8,128)(2,1)} %bitcast.17), calls=%async_computation.2 | async-start | bytes 524288 | tf_op jit(solution)/shard_map/all_to_all | solution.py:127
  169.1 13.7 %collective-permute-start.6 = (bf16[512,256]{1,0:T(8,128)(2,1)S(1)}, bf16[512,256]{1,0:T(8,128)(2,1)S(1)}, u32[]{:S(2)}, u32[]{:S(2)}) collective-permute-start(bf16[512,256]{1,0:T(8,128)(2,1)S(1)} %add_convert_fusion.own_ref), channel_id=1, source_target_pairs={{0,64},{32,96},{64,0},{96,32},{128,192},{160,224},{192,128},{224,1... | collective-permute-start | bytes 786440 | tf_op jit(solution)/shard_map/ppermute | solution.py:108
  174.5 12.3 %collective-permute-start.7 = (bf16[512,256]{1,0:T(8,128)(2,1)S(1)}, bf16[512,256]{1,0:T(8,128)(2,1)S(1)}, u32[]{:S(2)}, u32[]{:S(2)}) collective-permute-start(bf16[512,256]{1,0:T(8,128)(2,1)S(1)} %add_convert_fusion.own_ref), channel_id=1, source_target_pairs={{0,32},{32,64},{64,96},{96,0},{128,160},{160,192},{192,224},{224,1... | collective-permute-start | bytes 786440 | tf_op jit(solution)/shard_map/ppermute | solution.py:108
  176.9 9.8 %collective-permute-start.8 = (bf16[512,256]{1,0:T(8,128)(2,1)S(1)}, bf16[512,256]{1,0:T(8,128)(2,1)S(1)}, u32[]{:S(2)}, u32[]{:S(2)}) collective-permute-start(bf16[512,256]{1,0:T(8,128)(2,1)S(1)} %add_convert_fusion.own_ref), channel_id=1, source_target_pairs={{0,96},{32,0},{64,32},{96,64},{128,224},{160,128},{192,160},{224,1... | collective-permute-start | bytes 786440 | tf_op jit(solution)/shard_map/ppermute | solution.py:108
  187.5 16.4 %all-to-all-start.3 = ((bf16[16,32,256]{2,1,0:T(8,128)(2,1)}), bf16[16,32,256]{2,1,0:T(8,128)(2,1)S(1)}, u32[]{:S(2)}, u32[]{:S(2)}) async-start(bf16[16,32,256]{2,1,0:T(8,128)(2,1)} %broadcast_in_dim.2), calls=%async_computation.3 | async-start | bytes 524288 | tf_op jit(solution)/shard_map/all_to_all | solution.py:127

commit v3 on v2

v3 whole, which is shorter than its diff:
```python
import jax
import jax.numpy as jnp
from jax import lax
from jax.experimental import pallas as pl
from jax.experimental.pallas import tpu as pltpu
from jax.sharding import PartitionSpec as P

F32 = jnp.float32
BF16 = jnp.bfloat16
GELU_C = 0.7978845608028654
GELU_A = 0.044715
NT = (((1,), (1,)), ((), ()))
NN = (((1,), (0,)), ((), ()))
TN = (((0,), (0,)), ((), ()))
PARAMS = pltpu.CompilerParams(vmem_limit_bytes=24 * 1024 * 1024)
ALONG_Y = [[z_lo * 4 + y for y in range(4)] for z_lo in range(4)]
ALONG_Z = [[z_lo * 4 + y for z_lo in range(4)] for y in range(4)]


def dot(left, right, dims=NN):
    return lax.dot_general(left, right, dims, preferred_element_type=F32)


def weave(upper, lower):
    tok = upper.shape[1]
    both = jnp.concatenate([upper.reshape(-1, 8, tok), lower.reshape(-1, 8, tok)], axis=1)
    return both.astype(BF16)


def unweave(both):
    tok = both.shape[2]
    wide = both.astype(F32)
    upper = wide[:, :8].reshape(-1, tok).astype(BF16)
    lower = wide[:, 8:].reshape(-1, tok).astype(BF16)
    return upper, lower


def entry_kernel(tok_ref, grad_ref, left_up_ref, right_down_ref, send_ref):
    left_up_t = left_up_ref[...].astype(F32).T.astype(BF16)
    first = dot(left_up_t, tok_ref[...], NT)
    back = dot(right_down_ref[...], grad_ref[...], NT)
    send_ref[...] = weave(first, back)


def middle_kernel(recv_ref, right_up_ref, right_up_t_ref, left_down_ref, left_down_t_ref,
                  send_ref, hidden_ref, back_pre_ref, mixed_ref, back_third_ref):
    mixed, back_third = unweave(recv_ref[...])
    mixed_ref[...] = mixed
    back_third_ref[...] = back_third
    pre = dot(right_up_t_ref[...], mixed)
    back_hidden = dot(left_down_ref[...], back_third)
    square = pre * pre
    tanh = jnp.tanh(GELU_C * (pre + GELU_A * (pre * square)))
    cdf = 0.5 * (1.0 + tanh)
    hidden = (pre * cdf).astype(BF16)
    slope = cdf + (0.5 * pre) * (1.0 - tanh * tanh) * (GELU_C * (1.0 + (3.0 * GELU_A) * square))
    back_pre = (back_hidden * slope).astype(BF16)
    hidden_ref[...] = hidden
    back_pre_ref[...] = back_pre
    third = dot(left_down_t_ref[...], hidden)
    back_mixed = dot(right_up_ref[...], back_pre)
    send_ref[...] = weave(third, back_mixed)


def middle_grads_kernel(place_ref, hidden_ref, back_pre_ref, mixed_ref, back_third_ref, *out_refs):
    for step, out_ref in enumerate(out_refs):
        start = pl.multiple_of(((place_ref[0] + step) & 3) * 256, 256)
        block = pl.ds(start, 256)
        out_ref[:256] = dot(hidden_ref[block, :], back_third_ref[...], NT).astype(BF16)
        out_ref[256:] = dot(mixed_ref[...], back_pre_ref[block, :], NT).astype(BF16)


def fold_kernel(place_ref, own_ref, near_ref, far_ref, last_ref, *rest):
    total_ref = rest[-1]
    total_ref[...] = four_sum(own_ref[...], near_ref[...], far_ref[...], last_ref[...])
    for step, out_ref in enumerate(rest[:-1]):
        start = pl.multiple_of(((place_ref[0] + step) & 3) * 128, 128)
        out_ref[...] = total_ref[pl.ds(start, 128), :]


def exit_grads_kernel(recv_ref, tok_ref, grad_ref, out_ref, mixed_ref, back_first_ref):
    mixed, back_first = unweave(recv_ref[...])
    mixed_ref[...] = mixed
    back_first_ref[...] = back_first
    out_ref[:256] = dot(mixed, grad_ref[...]).astype(BF16)
    out_ref[256:] = dot(back_first, tok_ref[...]).T.astype(BF16)


def exit_kernel(mixed_ref, back_first_ref, left_up_ref, right_down_ref, out_ref, in_grad_ref):
    left_up_t = left_up_ref[...].astype(F32).T.astype(BF16)
    out_ref[...] = dot(mixed_ref[...], right_down_ref[...], TN).astype(BF16)
    in_grad_ref[...] = dot(back_first_ref[...], left_up_t, TN).astype(BF16)


def sum_spread_kernel(parts_ref, out_ref):
    total = jnp.sum(parts_ref[...].astype(F32), axis=0).astype(BF16)
    out_ref[...] = jnp.broadcast_to(total[None], out_ref.shape)


def pack_kernel(place_ref, late_ref, own_ref, near_ref, far_ref, last_ref, out_ref):
    late = jnp.sum(late_ref[...].astype(F32), axis=0).astype(BF16)
    place = place_ref[0] & 3
    for peer in range(4):
        out_ref[peer, :128] = late
        for step, ref in ((0, own_ref), (1, near_ref), (2, far_ref), (3, last_ref)):
            start = pl.multiple_of(128 + ((place + 4 - step) & 3) * 128, 128)
            out_ref[peer, pl.ds(start, 128), :] = ref[...]


def unpack_kernel(all_ref, left_up_ref, right_up_ref, left_down_ref, right_down_ref):
    for y in range(4):
        late_ref = right_down_ref if y < 2 else left_up_ref
        late_ref[y % 2 * 128:y % 2 * 128 + 128] = all_ref[y, :128]
        left_down_ref[y * 256:y * 256 + 256] = all_ref[y, 128:384]
        right_up_ref[:, y * 256:y * 256 + 256] = all_ref[y, 384:]


def hbm(dims):
    return pltpu.HBM(dims, BF16)


def plain(dims):
    return jax.ShapeDtypeStruct(dims, BF16)


def in_hbm(array):
    return pltpu.with_memory_space_constraint(array, pltpu.HBM)


def shift_pairs(inner, step):
    pairs = []
    for z_lo in range(4):
        for y in range(4):
            to = (z_lo * 4 + (y + step) % 4) if inner else (((z_lo + step) % 4) * 4 + y)
            pairs.append((z_lo * 4 + y, to))
    return pairs


def permute(array, inner, step):
    return lax.ppermute(array, "dp", shift_pairs(inner, step))


def four_sum(own, near, far, last):
    return ((own.astype(F32) + far.astype(F32)) + (near.astype(F32) + last.astype(F32))).astype(BF16)


def send_on(chunks, inner):
    far = permute(chunks[2], inner, 2)
    near = permute(chunks[1], inner, 1)
    return [chunks[0], near, far, permute(chunks[3], inner, 3)]


def exchange(parts, axis, groups=None):
    return lax.all_to_all(parts, axis, 0, 0, axis_index_groups=groups, tiled=True)


def whole_call(kernel, outs, *args):
    return pl.pallas_call(kernel, out_shape=outs, compiler_params=PARAMS)(*args)


def on_device(tokens_in, out_grad, left_up, right_up, left_down, right_down):
    tok = tokens_in.shape[0]
    tile = 256
    dp_index = lax.axis_index("dp")
    y, z_lo = dp_index & 3, dp_index >> 2

    weight = lambda rows, cols: pl.BlockSpec((rows, cols), lambda i: (0, 0))
    column = lambda rows: pl.BlockSpec((rows, tile), lambda i: (0, i))
    woven = lambda cols: pl.BlockSpec((32, 16, cols), lambda i: (0, 0, i))
    half = pl.BlockSpec((tok // 2, 256), lambda i: (i, 0))
    send = pl.pallas_call(
        entry_kernel,
        grid=(2,),
        in_specs=[half, half, weight(256, 256), weight(256, 256)],
        out_specs=woven(tok // 2),
        out_shape=hbm((32, 16, tok)),
        compiler_params=PARAMS,
    )(in_hbm(tokens_in), in_hbm(out_grad), in_hbm(left_up), in_hbm(right_down))
    recv = exchange(send, "tensor")

    send, hidden, back_pre, mixed_up, back_third = pl.pallas_call(
        middle_kernel,
        grid=(tok // tile,),
        in_specs=[woven(tile), weight(256, 1024), weight(1024, 256), weight(1024, 256), weight(256, 1024)],
        out_specs=[woven(tile), column(1024), column(1024), column(256), column(256)],
        out_shape=[hbm((32, 16, tok)), plain((1024, tok)), plain((1024, tok)),
                   plain((256, tok)), plain((256, tok))],
        compiler_params=PARAMS,
    )(recv, right_up, right_up.T, left_down, left_down.T)
    vmem = pl.BlockSpec(memory_space=pltpu.VMEM)
    smem = pl.BlockSpec(memory_space=pltpu.SMEM)
    y_place = y.astype(jnp.int32).reshape(1)
    z_place = z_lo.astype(jnp.int32).reshape(1)
    parts = pl.pallas_call(
        middle_grads_kernel,
        in_specs=[smem] + [vmem] * 4,
        out_shape=[hbm((512, 256))] * 4,
        compiler_params=PARAMS,
    )(y_place, hidden, back_pre, mixed_up, back_third)
    send, parts = lax.optimization_barrier((send, parts))
    recv = exchange(send, "tensor")

    parts = pl.pallas_call(
        fold_kernel,
        in_specs=[smem] + [vmem] * 4,
        out_shape=[plain((128, 256))] * 4,
        scratch_shapes=[pltpu.VMEM((512, 256), BF16)],
        compiler_params=PARAMS,
    )(z_place, *send_on(parts, True))
    part = four_sum(*send_on(parts, False))
    pieces = send_on([part] * 4, False)
    recv, pieces = lax.optimization_barrier((recv, pieces))

    late, mixed_down, back_first = whole_call(
        exit_grads_kernel, [hbm((512, 256)), plain((256, tok)), plain((256, tok))],
        recv, tokens_in, out_grad)
    late = exchange(late.reshape(4, 128, 256), "dp", ALONG_Y)
    late = whole_call(sum_spread_kernel, hbm((4, 128, 256)), late)
    late = exchange(late, "dp", ALONG_Z)
    packed = pl.pallas_call(
        pack_kernel,
        in_specs=[smem] + [vmem] * 5,
        out_shape=hbm((4, 640, 256)),
        compiler_params=PARAMS,
    )(z_place, late, *pieces)
    packed = exchange(packed, "dp", ALONG_Y)
    layer_out, input_grad = whole_call(
        exit_kernel, [hbm((tok, 256)), hbm((tok, 256))], mixed_down, back_first, left_up, right_down)
    grads = whole_call(
        unpack_kernel, [hbm((256, 256)), hbm((256, 1024)), hbm((1024, 256)), hbm((256, 256))], packed)
    return (layer_out, input_grad, *grads)


def solution(mesh):
    rows = P("tensor", None)
    return jax.shard_map(
        on_device,
        mesh=mesh,
        in_specs=(P("dp", "tensor"), P("dp", "tensor"), rows, rows, rows, rows),
        out_specs=(P("dp", "tensor"), P("dp", "tensor"), rows, rows, rows, rows),
        check_vma=False,
    )
```

time: 206 us -> 201 us (0.976)
  blocking collectives: 0 us -> 23 us
  starting transfers between devices: 76.8 us -> 67.2 us
  waiting for transfers between devices: 101 us -> 92.1 us
  Pallas kernels: 21.7 us -> 16.9 us
  local copies, waits for them, and re-layouts: 3.13 us -> 0.44 us
    all_to_all x0 -> x2, blocking collectives: none -> 23 us  [exchange(): lax.all_to_all(parts, axis, 0, 0, axis_index_groups=groups, tiled=True)]
    ppermute x9, waiting for transfers between devices: 47.1 us -> 30.5 us  [permute(): return lax.ppermute(array, 'dp', shift_pairs(inner, step))]
    all_to_all x4 -> x3, starting transfers between devices: 43.1 us -> 32.9 us  [exchange(): lax.all_to_all(parts, axis, 0, 0, axis_index_groups=groups, tiled=True)]
    all_to_all x4 -> x3, waiting for transfers between devices: 53.8 us -> 61.6 us  [exchange(): lax.all_to_all(parts, axis, 0, 0, axis_index_groups=groups, tiled=True)]
    pallas_call x6 -> x9, Pallas kernels: 21.7 us -> 16.9 us  [the longest x1 6.04 us: on_device(): pl.pallas_call(middle_kernel, grid=(tok // tile,), in_specs=[woven(tile),...]
  transfers between devices with their start and end apart: 13 -> 12, of which waited for: 8 -> 9; matrix products, arithmetic and copies ran while one was open for 1% -> 0% of each run, Pallas kernels for 5% -> 1%
where the time goes in v3:
time: 201 us; the launch traced here: 200 us
  waiting for transfers between devices  92.1 us (46%)
  starting transfers between devices  67.2 us (33%)
  blocking collectives  23 us (11%)
  Pallas kernels  16.9 us (8%)
    all_to_all x3, waiting for transfers between devices, exchange(): lax.all_to_all(parts, axis, 0, 0, axis_index_groups=groups, tiled=True)  61.6 us
    ppermute x9, starting transfers between devices, permute(): return lax.ppermute(array, 'dp', shift_pairs(inner, step))  34.4 us
    all_to_all x3, starting transfers between devices, exchange(): lax.all_to_all(parts, axis, 0, 0, axis_index_groups=groups, tiled=True)  32.9 us
    ppermute x9, waiting for transfers between devices, permute(): return lax.ppermute(array, 'dp', shift_pairs(inner, step))  30.5 us
    all_to_all x2, blocking collectives, exchange(): lax.all_to_all(parts, axis, 0, 0, axis_index_groups=groups, tiled=True)  23 us
    pallas_call x1, Pallas kernels, on_device(): pl.pallas_call(middle_kernel, grid=(tok // tile,), in_specs=[woven(tile),...  6.04 us
    pallas_call x4, Pallas kernels, whole_call(): return pl.pallas_call(kernel, out_shape=outs, compiler_params=PARAMS)(*args)  4.62 us
  transfers between devices with their start and end apart: 12, of which 9 were waited for; matrix products, arithmetic and copies ran while one was open for 0% of the time, Pallas kernels for 1%

profile of v3, /device:TPU:6, one launch (start us, length us, event | category | flops | bytes accessed | tf_op | source)
XLA Modules:
  0.0 200.5 jit_solution(7878542810351189319)
XLA Ops:
  0.6 0.0 copy-start
  0.6 2.7 %shard_map.109 = bf16[32,16,1024]{2,1,0:T(8,128)(2,1)} custom-call(bf16[1024,256]{1,0:T(8,128)(2,1)} %tok_ref.3, bf16[1024,256]{1,0:T(8,128)(2,1)} %grad_ref.3, bf16[256,256]{1,0:T(8,128)(2,1)} %left_up_ref.3, bf16[256,256]{1,0:T(8,128)(2,1)} %right_down_ref.3), custom_call_target="tpu_custom_call" | custom-call | tf_op jit(solution)/shard_map/pallas_call | solution.py:171
  3.3 0.0 copy-start.1
  3.3 18.4 %all-to-all-start = ((bf16[32,16,1024]{2,1,0:T(8,128)(2,1)}), bf16[32,16,1024]{2,1,0:T(8,128)(2,1)S(1)}, u32[]{:S(2)}, u32[]{:S(2)}) async-start(bf16[32,16,1024]{2,1,0:T(8,128)(2,1)} %shard_map.109), calls=%async_computation | async-start | bytes 2097152 | tf_op jit(solution)/shard_map/all_to_all | solution.py:154
  21.7 0.0 copy-done
  21.7 0.2 copy.12
  21.9 0.0 copy-done.1
  21.9 0.2 copy.13
  22.2 49.0 %all-to-all-done.recv_ref = bf16[32,16,1024]{2,1,0:T(8,128)(2,1)S(1)} async-done(((bf16[32,16,1024]{2,1,0:T(8,128)(2,1)}), bf16[32,16,1024]{2,1,0:T(8,128)(2,1)S(1)}, u32[]{:S(2)}, u32[]{:S(2)}) %all-to-all-start) | async-done | bytes 1048608 | tf_op jit(solution)/shard_map/all_to_all | solution.py:154
  71.2 6.0 %shard_map.110 = (bf16[32,16,1024]{2,1,0:T(8,128)(2,1)}, bf16[1024,1024]{1,0:T(8,128)(2,1)S(1)}, bf16[1024,1024]{1,0:T(8,128)(2,1)S(1)}, bf16[256,1024]{1,0:T(8,128)(2,1)S(1)}, bf16[256,1024]{1,0:T(8,128)(2,1)S(1)}) custom-call(bf16[32,16,1024]{2,1,0:T(8,128)(2,1)S(1)} %all-to-all-done.recv_ref, bf16[256,1024]{1,0:T(8,128)(2,1)S(1)} %copy-done, ...), custom_call_target="tpu_custom_call" | custom-call | tf_op jit(solution)/shard_map/pallas_call | solution.py:181
  77.2 2.1 %shard_map.111 = (bf16[512,256]{1,0:T(8,128)(2,1)}, bf16[512,256]{1,0:T(8,128)(2,1)}, bf16[512,256]{1,0:T(8,128)(2,1)}, bf16[512,256]{1,0:T(8,128)(2,1)}) custom-call(s32[1]{0:T(128)} %bitcast.2.place_ref, bf16[1024,1024]{1,0:T(8,128)(2,1)S(1)} %get-tuple-element.39.hidden_ref, bf16[1024,1024]{1,0:T(8,128)(2,1)S(1)} %get-tuple-element.40.back_pre_ref, ...), custom_call_target="tpu_custom_call" | custom-call | tf_op jit(solution)/shard_map/pallas_call | solution.py:194
  79.3 0.0 copy-start.7
  79.3 11.0 %all-to-all-start.1 = ((bf16[32,16,1024]{2,1,0:T(8,128)(2,1)}), bf16[32,16,1024]{2,1,0:T(8,128)(2,1)S(1)}, u32[]{:S(2)}, u32[]{:S(2)}) async-start(bf16[32,16,1024]{2,1,0:T(8,128)(2,1)} %get-tuple-element.47), calls=%async_computation.1 | async-start | bytes 2097152 | tf_op jit(solution)/shard_map/all_to_all | solution.py:154
  90.3 3.5 %collective-permute-start = (bf16[512,256]{1,0:T(8,128)(2,1)}, bf16[512,256]{1,0:T(8,128)(2,1)S(1)}, u32[]{:S(2)}, u32[]{:S(2)}) collective-permute-start(bf16[512,256]{1,0:T(8,128)(2,1)} %get-tuple-element.49), channel_id=1, source_target_pairs={{0,32},{32,64},{64,96},{96,0},{128,160},{160,192},{192,224},{224,1... | collective-permute-start | bytes 786440 | tf_op jit(solution)/shard_map/ppermute | solution.py:140
  93.8 4.8 %collective-permute-start.1 = (bf16[512,256]{1,0:T(8,128)(2,1)}, bf16[512,256]{1,0:T(8,128)(2,1)S(1)}, u32[]{:S(2)}, u32[]{:S(2)}) collective-permute-start(bf16[512,256]{1,0:T(8,128)(2,1)} %get-tuple-element.50), channel_id=1, source_target_pairs={{0,64},{32,96},{64,0},{96,32},{128,192},{160,224},{192,128},{224,1... | collective-permute-start | bytes 786440 | tf_op jit(solution)/shard_map/ppermute | solution.py:140
  98.6 0.0 copy-done.7
  98.6 3.3 %collective-permute-start.2 = (bf16[512,256]{1,0:T(8,128)(2,1)S(1)}, bf16[512,256]{1,0:T(8,128)(2,1)S(1)}, u32[]{:S(2)}, u32[]{:S(2)}) collective-permute-start(bf16[512,256]{1,0:T(8,128)(2,1)S(1)} %copy-done.7), channel_id=1, source_target_pairs={{0,96},{32,0},{64,32},{96,64},{128,224},{160,128},{192,160},{224,1... | collective-permute-start | bytes 786440 | tf_op jit(solution)/shard_map/ppermute | solution.py:140
  101.9 0.2 collective-permute-done.near_ref
  102.0 6.8 %collective-permute-done.1.far_ref = bf16[512,256]{1,0:T(8,128)(2,1)S(1)} collective-permute-done((bf16[512,256]{1,0:T(8,128)(2,1)}, bf16[512,256]{1,0:T(8,128)(2,1)S(1)}, u32[]{:S(2)}, u32[]{:S(2)}) %collective-permute-start.1) | collective-permute-done | bytes 262176 | tf_op jit(solution)/shard_map/ppermute | solution.py:140
  108.8 1.3 collective-permute-done.2.last_ref
  110.1 0.0 copy-done.6
  110.1 0.2 shard_map.112
  110.4 4.5 %collective-permute-start.3 = (bf16[128,256]{1,0:T(8,128)(2,1)S(1)}, bf16[128,256]{1,0:T(8,128)(2,1)S(1)}, u32[]{:S(2)}, u32[]{:S(2)}) collective-permute-start(bf16[128,256]{1,0:T(8,128)(2,1)S(1)} %get-tuple-element.53), channel_id=1, source_target_pairs={{0,256},{32,288},{64,320},{96,352},{128,384},{160,416},{192,448},{... | collective-permute-start | bytes 196616 | tf_op jit(solution)/shard_map/ppermute | solution.py:140
  114.9 2.1 %collective-permute-start.4 = (bf16[128,256]{1,0:T(8,128)(2,1)S(1)}, bf16[128,256]{1,0:T(8,128)(2,1)S(1)}, u32[]{:S(2)}, u32[]{:S(2)}) collective-permute-start(bf16[128,256]{1,0:T(8,128)(2,1)S(1)} %get-tuple-element.54), channel_id=1, source_target_pairs={{0,128},{32,160},{64,192},{96,224},{128,256},{160,288},{192,320},{... | collective-permute-start | bytes 196616 | tf_op jit(solution)/shard_map/ppermute | solution.py:140
  117.0 5.6 %collective-permute-start.5 = (bf16[128,256]{1,0:T(8,128)(2,1)S(1)}, bf16[128,256]{1,0:T(8,128)(2,1)S(1)}, u32[]{:S(2)}, u32[]{:S(2)}) collective-permute-start(bf16[128,256]{1,0:T(8,128)(2,1)S(1)} %get-tuple-element.55), channel_id=1, source_target_pairs={{0,384},{32,416},{64,448},{96,480},{128,0},{160,32},{192,64},{224,... | collective-permute-start | bytes 196616 | tf_op jit(solution)/shard_map/ppermute | solution.py:140
  122.6 19.4 %collective-permute-done.3 = bf16[128,256]{1,0:T(8,128)(2,1)S(1)} collective-permute-done((bf16[128,256]{1,0:T(8,128)(2,1)S(1)}, bf16[128,256]{1,0:T(8,128)(2,1)S(1)}, u32[]{:S(2)}, u32[]{:S(2)}) %collective-permute-start.3) | collective-permute-done | bytes 65568 | tf_op jit(solution)/shard_map/ppermute | solution.py:140
  142.0 0.0 collective-permute-done.4
  142.0 0.3 collective-permute-done.5
  142.3 4.5 %collective-permute-start.6 = (bf16[128,256]{1,0:T(8,128)(2,1)S(1)}, bf16[128,256]{1,0:T(8,128)(2,1)S(1)}, u32[]{:S(2)}, u32[]{:S(2)}) collective-permute-start(bf16[128,256]{1,0:T(8,128)(2,1)S(1)} %add_convert_fusion.own_ref), channel_id=1, source_target_pairs={{0,128},{32,160},{64,192},{96,224},{128,256},{160,288},{192,320},{... | collective-permute-start | bytes 196616 | tf_op jit(solution)/shard_map/ppermute | solution.py:140
  146.7 1.9 collective-permute-start.7
  148.7 4.3 %collective-permute-start.8 = (bf16[128,256]{1,0:T(8,128)(2,1)S(1)}, bf16[128,256]{1,0:T(8,128)(2,1)S(1)}, u32[]{:S(2)}, u32[]{:S(2)}) collective-permute-start(bf16[128,256]{1,0:T(8,128)(2,1)S(1)} %add_convert_fusion.own_ref), channel_id=1, source_target_pairs={{0,384},{32,416},{64,448},{96,480},{128,0},{160,32},{192,64},{224,... | collective-permute-start | bytes 196616 | tf_op jit(solution)/shard_map/ppermute | solution.py:140
  152.9 0.0 collective-permute-done.6.near_ref
  153.0 1.7 collective-permute-done.7.far_ref
  154.7 0.8 collective-permute-done.8.last_ref
  155.5 0.0 all-to-all-done.1.recv_ref
  155.5 0.0 copy-done.2
  155.5 0.0 copy-done.3
  155.5 1.2 shard_map.113
  156.8 11.2 %all_to_all.25.parts_ref = bf16[4,128,256]{2,1,0:T(8,128)(2,1)S(1)} all-to-all(bf16[4,128,256]{2,1,0:T(8,128)(2,1)} %bitcast.7), channel_id=1, replica_groups={{0,32,64,96},{128,160,192,224},{256,288,320,352},{384,416,448,480},{1,3..., dimensions={0} | all-to-all | bytes 524288 | tf_op jit(solution)/shard_map/all_to_all | solution.py:154
  167.9 0.7 shard_map.115
  168.7 11.8 %all_to_all.26.late_ref = bf16[4,128,256]{2,1,0:T(8,128)(2,1)S(1)} all-to-all(bf16[4,128,256]{2,1,0:T(8,128)(2,1)} %shard_map.115), channel_id=1, replica_groups={{0,128,256,384},{32,160,288,416},{64,192,320,448},{96,224,352,480},{1,1..., dimensions={0} | all-to-all | bytes 524288 | tf_op jit(solution)/shard_map/all_to_all | solution.py:154
  180.5 1.2 shard_map.116
  181.7 3.5 %all-to-all-start.4 = ((bf16[4,640,256]{2,1,0:T(8,128)(2,1)}), bf16[4,640,256]{2,1,0:T(8,128)(2,1)S(1)}, u32[]{:S(2)}, u32[]{:S(2)}) async-start(bf16[4,640,256]{2,1,0:T(8,128)(2,1)} %shard_map.116), calls=%async_computation.4 | async-start | bytes 2621440 | tf_op jit(solution)/shard_map/all_to_all | solution.py:154
  185.2 0.0 copy-done.4
  185.2 0.0 copy-done.5
  185.2 1.5 shard_map.114
  186.8 12.6 %all-to-all-done.4.all_ref = bf16[4,640,256]{2,1,0:T(8,128)(2,1)S(1)} async-done(((bf16[4,640,256]{2,1,0:T(8,128)(2,1)}), bf16[4,640,256]{2,1,0:T(8,128)(2,1)S(1)}, u32[]{:S(2)}, u32[]{:S(2)}) %all-to-all-start.4) | async-done | bytes 1310752 | tf_op jit(solution)/shard_map/all_to_all | solution.py:154
  199.3 1.2 shard_map.117
  (6 shorter events, 0.0 us)
Async XLA Ops:
  0.6 21.1 %copy-start = (bf16[256,1024]{1,0:T(8,128)(2,1)S(1)}, bf16[256,1024]{1,0:T(8,128)(2,1)}, u32[]{:S(2)}) copy-start(bf16[256,1024]{1,0:T(8,128)(2,1)} %right_up_ref.1) | copy-start | bytes 1572868
  3.3 18.6 %copy-start.1 = (bf16[1024,256]{1,0:T(8,128)(2,1)S(1)}, bf16[1024,256]{1,0:T(8,128)(2,1)}, u32[]{:S(2)}) copy-start(bf16[1024,256]{1,0:T(8,128)(2,1)} %left_down_ref.1) | copy-start | bytes 1572868
  3.3 67.8 %all-to-all-start = ((bf16[32,16,1024]{2,1,0:T(8,128)(2,1)}), bf16[32,16,1024]{2,1,0:T(8,128)(2,1)S(1)}, u32[]{:S(2)}, u32[]{:S(2)}) async-start(bf16[32,16,1024]{2,1,0:T(8,128)(2,1)} %shard_map.109), calls=%async_computation | async-start | bytes 2097152 | tf_op jit(solution)/shard_map/all_to_all | solution.py:154
  79.3 19.3 %copy-start.7 = (bf16[512,256]{1,0:T(8,128)(2,1)S(1)}, bf16[512,256]{1,0:T(8,128)(2,1)}, u32[]{:S(2)}) copy-start(bf16[512,256]{1,0:T(8,128)(2,1)} %get-tuple-element.51) | copy-start | bytes 786436
  79.3 30.9 %copy-start.6 = (bf16[512,256]{1,0:T(8,128)(2,1)S(1)}, bf16[512,256]{1,0:T(8,128)(2,1)}, u32[]{:S(2)}) copy-start(bf16[512,256]{1,0:T(8,128)(2,1)} %get-tuple-element.48.own_ref) | copy-start | bytes 786436
  79.3 76.3 %copy-start.2 = (bf16[1024,256]{1,0:T(8,128)(2,1)S(1)}, bf16[1024,256]{1,0:T(8,128)(2,1)}, u32[]{:S(2)}) copy-start(bf16[1024,256]{1,0:T(8,128)(2,1)} %tok_ref.3) | copy-start | bytes 1572868
  79.3 76.3 %copy-start.3 = (bf16[1024,256]{1,0:T(8,128)(2,1)S(1)}, bf16[1024,256]{1,0:T(8,128)(2,1)}, u32[]{:S(2)}) copy-start(bf16[1024,256]{1,0:T(8,128)(2,1)} %grad_ref.3) | copy-start | bytes 1572868
  79.3 76.2 %all-to-all-start.1 = ((bf16[32,16,1024]{2,1,0:T(8,128)(2,1)}), bf16[32,16,1024]{2,1,0:T(8,128)(2,1)S(1)}, u32[]{:S(2)}, u32[]{:S(2)}) async-start(bf16[32,16,1024]{2,1,0:T(8,128)(2,1)} %get-tuple-element.47), calls=%async_computation.1 | async-start | bytes 2097152 | tf_op jit(solution)/shard_map/all_to_all | solution.py:154
  90.3 11.7 %collective-permute-start = (bf16[512,256]{1,0:T(8,128)(2,1)}, bf16[512,256]{1,0:T(8,128)(2,1)S(1)}, u32[]{:S(2)}, u32[]{:S(2)}) collective-permute-start(bf16[512,256]{1,0:T(8,128)(2,1)} %get-tuple-element.49), channel_id=1, source_target_pairs={{0,32},{32,64},{64,96},{96,0},{128,160},{160,192},{192,224},{224,1... | collective-permute-start | bytes 786440 | tf_op jit(solution)/shard_map/ppermute | solution.py:140
  93.8 15.0 %collective-permute-start.1 = (bf16[512,256]{1,0:T(8,128)(2,1)}, bf16[512,256]{1,0:T(8,128)(2,1)S(1)}, u32[]{:S(2)}, u32[]{:S(2)}) collective-permute-start(bf16[512,256]{1,0:T(8,128)(2,1)} %get-tuple-element.50), channel_id=1, source_target_pairs={{0,64},{32,96},{64,0},{96,32},{128,192},{160,224},{192,128},{224,1... | collective-permute-start | bytes 786440 | tf_op jit(solution)/shard_map/ppermute | solution.py:140
  98.6 11.5 %collective-permute-start.2 = (bf16[512,256]{1,0:T(8,128)(2,1)S(1)}, bf16[512,256]{1,0:T(8,128)(2,1)S(1)}, u32[]{:S(2)}, u32[]{:S(2)}) collective-permute-start(bf16[512,256]{1,0:T(8,128)(2,1)S(1)} %copy-done.7), channel_id=1, source_target_pairs={{0,96},{32,0},{64,32},{96,64},{128,224},{160,128},{192,160},{224,1... | collective-permute-start | bytes 786440 | tf_op jit(solution)/shard_map/ppermute | solution.py:140
  110.4 31.6 %collective-permute-start.3 = (bf16[128,256]{1,0:T(8,128)(2,1)S(1)}, bf16[128,256]{1,0:T(8,128)(2,1)S(1)}, u32[]{:S(2)}, u32[]{:S(2)}) collective-permute-start(bf16[128,256]{1,0:T(8,128)(2,1)S(1)} %get-tuple-element.53), channel_id=1, source_target_pairs={{0,256},{32,288},{64,320},{96,352},{128,384},{160,416},{192,448},{... | collective-permute-start | bytes 196616 | tf_op jit(solution)/shard_map/ppermute | solution.py:140
  114.9 27.0 %collective-permute-start.4 = (bf16[128,256]{1,0:T(8,128)(2,1)S(1)}, bf16[128,256]{1,0:T(8,128)(2,1)S(1)}, u32[]{:S(2)}, u32[]{:S(2)}) collective-permute-start(bf16[128,256]{1,0:T(8,128)(2,1)S(1)} %get-tuple-element.54), channel_id=1, source_target_pairs={{0,128},{32,160},{64,192},{96,224},{128,256},{160,288},{192,320},{... | collective-permute-start | bytes 196616 | tf_op jit(solution)/shard_map/ppermute | solution.py:140
  117.0 25.2 %collective-permute-start.5 = (bf16[128,256]{1,0:T(8,128)(2,1)S(1)}, bf16[128,256]{1,0:T(8,128)(2,1)S(1)}, u32[]{:S(2)}, u32[]{:S(2)}) collective-permute-start(bf16[128,256]{1,0:T(8,128)(2,1)S(1)} %get-tuple-element.55), channel_id=1, source_target_pairs={{0,384},{32,416},{64,448},{96,480},{128,0},{160,32},{192,64},{224,... | collective-permute-start | bytes 196616 | tf_op jit(solution)/shard_map/ppermute | solution.py:140
  142.3 10.7 %collective-permute-start.6 = (bf16[128,256]{1,0:T(8,128)(2,1)S(1)}, bf16[128,256]{1,0:T(8,128)(2,1)S(1)}, u32[]{:S(2)}, u32[]{:S(2)}) collective-permute-start(bf16[128,256]{1,0:T(8,128)(2,1)S(1)} %add_convert_fusion.own_ref), channel_id=1, source_target_pairs={{0,128},{32,160},{64,192},{96,224},{128,256},{160,288},{192,320},{... | collective-permute-start | bytes 196616 | tf_op jit(solution)/shard_map/ppermute | solution.py:140
  146.7 8.0 %collective-permute-start.7 = (bf16[128,256]{1,0:T(8,128)(2,1)S(1)}, bf16[128,256]{1,0:T(8,128)(2,1)S(1)}, u32[]{:S(2)}, u32[]{:S(2)}) collective-permute-start(bf16[128,256]{1,0:T(8,128)(2,1)S(1)} %add_convert_fusion.own_ref), channel_id=1, source_target_pairs={{0,256},{32,288},{64,320},{96,352},{128,384},{160,416},{192,448},{... | collective-permute-start | bytes 196616 | tf_op jit(solution)/shard_map/ppermute | solution.py:140
  148.7 6.9 %collective-permute-start.8 = (bf16[128,256]{1,0:T(8,128)(2,1)S(1)}, bf16[128,256]{1,0:T(8,128)(2,1)S(1)}, u32[]{:S(2)}, u32[]{:S(2)}) collective-permute-start(bf16[128,256]{1,0:T(8,128)(2,1)S(1)} %add_convert_fusion.own_ref), channel_id=1, source_target_pairs={{0,384},{32,416},{64,448},{96,480},{128,0},{160,32},{192,64},{224,... | collective-permute-start | bytes 196616 | tf_op jit(solution)/shard_map/ppermute | solution.py:140
  180.5 4.7 %copy-start.4 = (bf16[256,256]{1,0:T(8,128)(2,1)S(1)}, bf16[256,256]{1,0:T(8,128)(2,1)}, u32[]{:S(2)}) copy-start(bf16[256,256]{1,0:T(8,128)(2,1)} %left_up_ref.3) | copy-start | bytes 393220
  180.5 4.7 %copy-start.5 = (bf16[256,256]{1,0:T(8,128)(2,1)S(1)}, bf16[256,256]{1,0:T(8,128)(2,1)}, u32[]{:S(2)}) copy-start(bf16[256,256]{1,0:T(8,128)(2,1)} %right_down_ref.3) | copy-start | bytes 393220
  181.7 17.6 %all-to-all-start.4 = ((bf16[4,640,256]{2,1,0:T(8,128)(2,1)}), bf16[4,640,256]{2,1,0:T(8,128)(2,1)S(1)}, u32[]{:S(2)}, u32[]{:S(2)}) async-start(bf16[4,640,256]{2,1,0:T(8,128)(2,1)} %shard_map.116), calls=%async_computation.4 | async-start | bytes 2621440 | tf_op jit(solution)/shard_map/all_to_all | solution.py:154

commit v4 on v3

--- a/solution.py
+++ b/solution.py
@@ -92,19 +92,20 @@
     in_grad_ref[...] = dot(back_first_ref[...], left_up_t, TN).astype(BF16)
 
 
-def sum_spread_kernel(parts_ref, out_ref):
-    total = jnp.sum(parts_ref[...].astype(F32), axis=0).astype(BF16)
-    out_ref[...] = jnp.broadcast_to(total[None], out_ref.shape)
-
-
-def pack_kernel(place_ref, late_ref, own_ref, near_ref, far_ref, last_ref, out_ref):
+def spread_kernel(late_ref, own_ref, near_ref, far_ref, last_ref, out_ref):
     late = jnp.sum(late_ref[...].astype(F32), axis=0).astype(BF16)
-    place = place_ref[0] & 3
+    early = four_sum(own_ref[...], near_ref[...], far_ref[...], last_ref[...])
     for peer in range(4):
         out_ref[peer, :128] = late
-        for step, ref in ((0, own_ref), (1, near_ref), (2, far_ref), (3, last_ref)):
-            start = pl.multiple_of(128 + ((place + 4 - step) & 3) * 128, 128)
-            out_ref[peer, pl.ds(start, 128), :] = ref[...]
+        out_ref[peer, 128:] = early
+
+
+def pack_kernel(parts_ref, out_ref):
+    late = jnp.sum(parts_ref[:, :128].astype(F32), axis=0).astype(BF16)
+    for peer in range(4):
+        out_ref[peer, :128] = late
+        for z_lo in range(4):
+            out_ref[peer, 128 + z_lo * 128:256 + z_lo * 128] = parts_ref[z_lo, 128:]
 
 
 def unpack_kernel(all_ref, left_up_ref, right_up_ref, left_down_ref, right_down_ref):
@@ -207,22 +208,16 @@
         scratch_shapes=[pltpu.VMEM((512, 256), BF16)],
         compiler_params=PARAMS,
     )(z_place, *send_on(parts, True))
-    part = four_sum(*send_on(parts, False))
-    pieces = send_on([part] * 4, False)
+    pieces = send_on(parts, False)
     recv, pieces = lax.optimization_barrier((recv, pieces))
 
     late, mixed_down, back_first = whole_call(
         exit_grads_kernel, [hbm((512, 256)), plain((256, tok)), plain((256, tok))],
         recv, tokens_in, out_grad)
     late = exchange(late.reshape(4, 128, 256), "dp", ALONG_Y)
-    late = whole_call(sum_spread_kernel, hbm((4, 128, 256)), late)
+    late = whole_call(spread_kernel, hbm((4, 256, 256)), late, *pieces)
     late = exchange(late, "dp", ALONG_Z)
-    packed = pl.pallas_call(
-        pack_kernel,
-        in_specs=[smem] + [vmem] * 5,
-        out_shape=hbm((4, 640, 256)),
-        compiler_params=PARAMS,
-    )(z_place, late, *pieces)
+    packed = whole_call(pack_kernel, hbm((4, 640, 256)), late)
     packed = exchange(packed, "dp", ALONG_Y)
     layer_out, input_grad = whole_call(
         exit_kernel, [hbm((tok, 256)), hbm((tok, 256))], mixed_down, back_first, left_up, right_down)

time: 201 us -> 202 us (level)
  blocking collectives: 23 us -> 34.6 us
  starting transfers between devices: 67.2 us -> 55.7 us
    all_to_all x2, blocking collectives: 23 us -> 34.6 us  [exchange(): lax.all_to_all(parts, axis, 0, 0, axis_index_groups=groups, tiled=True)]
    ppermute x9 -> x6, starting transfers between devices: 34.4 us -> 22.8 us  [permute(): return lax.ppermute(array, 'dp', shift_pairs(inner, step))]
    all_to_all x3, waiting for transfers between devices: 61.6 us -> 64.9 us  [exchange(): lax.all_to_all(parts, axis, 0, 0, axis_index_groups=groups, tiled=True)]
    ppermute x9 -> x6, waiting for transfers between devices: 30.5 us -> 27.6 us  [permute(): return lax.ppermute(array, 'dp', shift_pairs(inner, step))]
    pallas_call x4 -> x5, Pallas kernels: 4.62 us -> 5.91 us  [whole_call(): return pl.pallas_call(kernel, out_shape=outs, compiler_params=PARAMS)(*args)]
  transfers between devices with their start and end apart: 12 -> 9, of which waited for: 9 -> 7; matrix products, arithmetic and copies ran while one was open for 0% -> 0% of each run, Pallas kernels for 1% -> 1%
where the time goes in v4:
time: 202 us; the launch traced here: 201 us
  waiting for transfers between devices  92.4 us (46%)
  starting transfers between devices  55.7 us (28%)
  blocking collectives  34.6 us (17%)
  Pallas kernels  17 us (8%)
    all_to_all x3, waiting for transfers between devices, exchange(): lax.all_to_all(parts, axis, 0, 0, axis_index_groups=groups, tiled=True)  64.9 us
    all_to_all x2, blocking collectives, exchange(): lax.all_to_all(parts, axis, 0, 0, axis_index_groups=groups, tiled=True)  34.6 us
    all_to_all x3, starting transfers between devices, exchange(): lax.all_to_all(parts, axis, 0, 0, axis_index_groups=groups, tiled=True)  32.8 us
    ppermute x6, waiting for transfers between devices, permute(): return lax.ppermute(array, 'dp', shift_pairs(inner, step))  27.6 us
    ppermute x6, starting transfers between devices, permute(): return lax.ppermute(array, 'dp', shift_pairs(inner, step))  22.8 us
    pallas_call x1, Pallas kernels, on_device(): pl.pallas_call(middle_kernel, grid=(tok // tile,), in_specs=[woven(tile),...  6.07 us
    pallas_call x5, Pallas kernels, whole_call(): return pl.pallas_call(kernel, out_shape=outs, compiler_params=PARAMS)(*args)  5.91 us
  transfers between devices with their start and end apart: 9, of which 7 were waited for; matrix products, arithmetic and copies ran while one was open for 0% of the time, Pallas kernels for 1%

profile of v4, /device:TPU:6, one launch (start us, length us, event | category | flops | bytes accessed | tf_op | source)
XLA Modules:
  0.0 201.0 jit_solution(16880807241384792286)
XLA Ops:
  0.6 0.0 copy-start
  0.6 2.7 %shard_map.109 = bf16[32,16,1024]{2,1,0:T(8,128)(2,1)} custom-call(bf16[1024,256]{1,0:T(8,128)(2,1)} %tok_ref.3, bf16[1024,256]{1,0:T(8,128)(2,1)} %grad_ref.3, bf16[256,256]{1,0:T(8,128)(2,1)} %left_up_ref.3, bf16[256,256]{1,0:T(8,128)(2,1)} %right_down_ref.3), custom_call_target="tpu_custom_call" | custom-call | tf_op jit(solution)/shard_map/pallas_call | solution.py:172
  3.3 0.0 copy-start.1
  3.4 18.4 %all-to-all-start = ((bf16[32,16,1024]{2,1,0:T(8,128)(2,1)}), bf16[32,16,1024]{2,1,0:T(8,128)(2,1)S(1)}, u32[]{:S(2)}, u32[]{:S(2)}) async-start(bf16[32,16,1024]{2,1,0:T(8,128)(2,1)} %shard_map.109), calls=%async_computation | async-start | bytes 2097152 | tf_op jit(solution)/shard_map/all_to_all | solution.py:155
  21.7 0.0 copy-done
  21.7 0.2 copy.12
  21.9 0.0 copy-done.1
  22.0 0.2 copy.13
  22.2 49.0 %all-to-all-done.recv_ref = bf16[32,16,1024]{2,1,0:T(8,128)(2,1)S(1)} async-done(((bf16[32,16,1024]{2,1,0:T(8,128)(2,1)}), bf16[32,16,1024]{2,1,0:T(8,128)(2,1)S(1)}, u32[]{:S(2)}, u32[]{:S(2)}) %all-to-all-start) | async-done | bytes 1048608 | tf_op jit(solution)/shard_map/all_to_all | solution.py:155
  71.2 6.1 %shard_map.110 = (bf16[32,16,1024]{2,1,0:T(8,128)(2,1)}, bf16[1024,1024]{1,0:T(8,128)(2,1)S(1)}, bf16[1024,1024]{1,0:T(8,128)(2,1)S(1)}, bf16[256,1024]{1,0:T(8,128)(2,1)S(1)}, bf16[256,1024]{1,0:T(8,128)(2,1)S(1)}) custom-call(bf16[32,16,1024]{2,1,0:T(8,128)(2,1)S(1)} %all-to-all-done.recv_ref, bf16[256,1024]{1,0:T(8,128)(2,1)S(1)} %copy-done, ...), custom_call_target="tpu_custom_call" | custom-call | tf_op jit(solution)/shard_map/pallas_call | solution.py:182
  77.2 2.1 %shard_map.111 = (bf16[512,256]{1,0:T(8,128)(2,1)}, bf16[512,256]{1,0:T(8,128)(2,1)}, bf16[512,256]{1,0:T(8,128)(2,1)}, bf16[512,256]{1,0:T(8,128)(2,1)}) custom-call(s32[1]{0:T(128)} %bitcast.2.place_ref, bf16[1024,1024]{1,0:T(8,128)(2,1)S(1)} %get-tuple-element.39.hidden_ref, bf16[1024,1024]{1,0:T(8,128)(2,1)S(1)} %get-tuple-element.40.back_pre_ref, ...), custom_call_target="tpu_custom_call" | custom-call | tf_op jit(solution)/shard_map/pallas_call | solution.py:195
  79.3 0.0 copy-start.7
  79.3 0.0 copy-start.6
  79.3 0.0 copy-start.2
  79.3 0.0 copy-start.3
  79.3 10.9 %all-to-all-start.1 = ((bf16[32,16,1024]{2,1,0:T(8,128)(2,1)}), bf16[32,16,1024]{2,1,0:T(8,128)(2,1)S(1)}, u32[]{:S(2)}, u32[]{:S(2)}) async-start(bf16[32,16,1024]{2,1,0:T(8,128)(2,1)} %get-tuple-element.47), calls=%async_computation.1 | async-start | bytes 2097152 | tf_op jit(solution)/shard_map/all_to_all | solution.py:155
  90.3 3.4 %collective-permute-start = (bf16[512,256]{1,0:T(8,128)(2,1)}, bf16[512,256]{1,0:T(8,128)(2,1)S(1)}, u32[]{:S(2)}, u32[]{:S(2)}) collective-permute-start(bf16[512,256]{1,0:T(8,128)(2,1)} %get-tuple-element.49), channel_id=1, source_target_pairs={{0,32},{32,64},{64,96},{96,0},{128,160},{160,192},{192,224},{224,1... | collective-permute-start | bytes 786440 | tf_op jit(solution)/shard_map/ppermute | solution.py:141
  93.7 4.8 %collective-permute-start.1 = (bf16[512,256]{1,0:T(8,128)(2,1)}, bf16[512,256]{1,0:T(8,128)(2,1)S(1)}, u32[]{:S(2)}, u32[]{:S(2)}) collective-permute-start(bf16[512,256]{1,0:T(8,128)(2,1)} %get-tuple-element.50), channel_id=1, source_target_pairs={{0,64},{32,96},{64,0},{96,32},{128,192},{160,224},{192,128},{224,1... | collective-permute-start | bytes 786440 | tf_op jit(solution)/shard_map/ppermute | solution.py:141
  98.6 0.0 copy-done.7
  98.6 3.3 %collective-permute-start.2 = (bf16[512,256]{1,0:T(8,128)(2,1)S(1)}, bf16[512,256]{1,0:T(8,128)(2,1)S(1)}, u32[]{:S(2)}, u32[]{:S(2)}) collective-permute-start(bf16[512,256]{1,0:T(8,128)(2,1)S(1)} %copy-done.7), channel_id=1, source_target_pairs={{0,96},{32,0},{64,32},{96,64},{128,224},{160,128},{192,160},{224,1... | collective-permute-start | bytes 786440 | tf_op jit(solution)/shard_map/ppermute | solution.py:141
  101.8 0.2 collective-permute-done.near_ref
  102.0 6.8 %collective-permute-done.1.far_ref = bf16[512,256]{1,0:T(8,128)(2,1)S(1)} collective-permute-done((bf16[512,256]{1,0:T(8,128)(2,1)}, bf16[512,256]{1,0:T(8,128)(2,1)S(1)}, u32[]{:S(2)}, u32[]{:S(2)}) %collective-permute-start.1) | collective-permute-done | bytes 262176 | tf_op jit(solution)/shard_map/ppermute | solution.py:141
  108.8 1.3 collective-permute-done.2.last_ref
  110.1 0.0 copy-done.6
  110.1 0.2 shard_map.112
  110.4 3.5 %collective-permute-start.3 = (bf16[128,256]{1,0:T(8,128)(2,1)S(1)}, bf16[128,256]{1,0:T(8,128)(2,1)S(1)}, u32[]{:S(2)}, u32[]{:S(2)}) collective-permute-start(bf16[128,256]{1,0:T(8,128)(2,1)S(1)} %get-tuple-element.53), channel_id=1, source_target_pairs={{0,128},{32,160},{64,192},{96,224},{128,256},{160,288},{192,320},{... | collective-permute-start | bytes 196616 | tf_op jit(solution)/shard_map/ppermute | solution.py:141
  113.9 3.1 %collective-permute-start.4 = (bf16[128,256]{1,0:T(8,128)(2,1)S(1)}, bf16[128,256]{1,0:T(8,128)(2,1)S(1)}, u32[]{:S(2)}, u32[]{:S(2)}) collective-permute-start(bf16[128,256]{1,0:T(8,128)(2,1)S(1)} %get-tuple-element.54), channel_id=1, source_target_pairs={{0,256},{32,288},{64,320},{96,352},{128,384},{160,416},{192,448},{... | collective-permute-start | bytes 196616 | tf_op jit(solution)/shard_map/ppermute | solution.py:141
  117.0 4.7 %collective-permute-start.5 = (bf16[128,256]{1,0:T(8,128)(2,1)S(1)}, bf16[128,256]{1,0:T(8,128)(2,1)S(1)}, u32[]{:S(2)}, u32[]{:S(2)}) collective-permute-start(bf16[128,256]{1,0:T(8,128)(2,1)S(1)} %get-tuple-element.55), channel_id=1, source_target_pairs={{0,384},{32,416},{64,448},{96,480},{128,0},{160,32},{192,64},{224,... | collective-permute-start | bytes 196616 | tf_op jit(solution)/shard_map/ppermute | solution.py:141
  121.7 0.0 collective-permute-done.3.near_ref
  121.7 14.2 %collective-permute-done.4.far_ref = bf16[128,256]{1,0:T(8,128)(2,1)S(1)} collective-permute-done((bf16[128,256]{1,0:T(8,128)(2,1)S(1)}, bf16[128,256]{1,0:T(8,128)(2,1)S(1)}, u32[]{:S(2)}, u32[]{:S(2)}) %collective-permute-start.4) | collective-permute-done | bytes 65568 | tf_op jit(solution)/shard_map/ppermute | solution.py:141
  136.0 5.1 %collective-permute-done.5.last_ref = bf16[128,256]{1,0:T(8,128)(2,1)S(1)} collective-permute-done((bf16[128,256]{1,0:T(8,128)(2,1)S(1)}, bf16[128,256]{1,0:T(8,128)(2,1)S(1)}, u32[]{:S(2)}, u32[]{:S(2)}) %collective-permute-start.5) | collective-permute-done | bytes 65568 | tf_op jit(solution)/shard_map/ppermute | solution.py:141
  141.0 0.0 all-to-all-done.1.recv_ref
  141.0 0.0 copy-done.2
  141.0 0.0 copy-done.3
  141.0 1.2 shard_map.113
  142.2 11.3 %all_to_all.25.late_ref = bf16[4,128,256]{2,1,0:T(8,128)(2,1)S(1)} all-to-all(bf16[4,128,256]{2,1,0:T(8,128)(2,1)} %bitcast.7), channel_id=1, replica_groups={{0,32,64,96},{128,160,192,224},{256,288,320,352},{384,416,448,480},{1,3..., dimensions={0} | all-to-all | bytes 524288 | tf_op jit(solution)/shard_map/all_to_all | solution.py:155
  153.5 0.9 shard_map.115
  154.4 23.3 %all_to_all.26.parts_ref = bf16[4,256,256]{2,1,0:T(8,128)(2,1)S(1)} all-to-all(bf16[4,256,256]{2,1,0:T(8,128)(2,1)} %shard_map.115), channel_id=1, replica_groups={{0,128,256,384},{32,160,288,416},{64,192,320,448},{96,224,352,480},{1,1..., dimensions={0} | all-to-all | bytes 1048576 | tf_op jit(solution)/shard_map/all_to_all | solution.py:155
  177.7 0.0 copy-start.4
  177.7 0.0 copy-start.5
  177.7 1.2 shard_map.116
  178.9 3.5 %all-to-all-start.4 = ((bf16[4,640,256]{2,1,0:T(8,128)(2,1)}), bf16[4,640,256]{2,1,0:T(8,128)(2,1)S(1)}, u32[]{:S(2)}, u32[]{:S(2)}) async-start(bf16[4,640,256]{2,1,0:T(8,128)(2,1)} %shard_map.116), calls=%async_computation.4 | async-start | bytes 2621440 | tf_op jit(solution)/shard_map/all_to_all | solution.py:155
  182.4 0.0 copy-done.4
  182.5 0.0 copy-done.5
  182.5 1.5 shard_map.114
  184.0 15.9 %all-to-all-done.4.all_ref = bf16[4,640,256]{2,1,0:T(8,128)(2,1)S(1)} async-done(((bf16[4,640,256]{2,1,0:T(8,128)(2,1)}), bf16[4,640,256]{2,1,0:T(8,128)(2,1)S(1)}, u32[]{:S(2)}, u32[]{:S(2)}) %all-to-all-start.4) | async-done | bytes 1310752 | tf_op jit(solution)/shard_map/all_to_all | solution.py:155
  199.8 1.2 shard_map.117
Async XLA Ops:
  0.6 21.1 %copy-start = (bf16[256,1024]{1,0:T(8,128)(2,1)S(1)}, bf16[256,1024]{1,0:T(8,128)(2,1)}, u32[]{:S(2)}) copy-start(bf16[256,1024]{1,0:T(8,128)(2,1)} %right_up_ref.1) | copy-start | bytes 1572868
  3.3 18.6 %copy-start.1 = (bf16[1024,256]{1,0:T(8,128)(2,1)S(1)}, bf16[1024,256]{1,0:T(8,128)(2,1)}, u32[]{:S(2)}) copy-start(bf16[1024,256]{1,0:T(8,128)(2,1)} %left_down_ref.1) | copy-start | bytes 1572868
  3.4 67.8 %all-to-all-start = ((bf16[32,16,1024]{2,1,0:T(8,128)(2,1)}), bf16[32,16,1024]{2,1,0:T(8,128)(2,1)S(1)}, u32[]{:S(2)}, u32[]{:S(2)}) async-start(bf16[32,16,1024]{2,1,0:T(8,128)(2,1)} %shard_map.109), calls=%async_computation | async-start | bytes 2097152 | tf_op jit(solution)/shard_map/all_to_all | solution.py:155
  79.3 19.2 %copy-start.7 = (bf16[512,256]{1,0:T(8,128)(2,1)S(1)}, bf16[512,256]{1,0:T(8,128)(2,1)}, u32[]{:S(2)}) copy-start(bf16[512,256]{1,0:T(8,128)(2,1)} %get-tuple-element.51) | copy-start | bytes 786436
  79.3 30.8 %copy-start.6 = (bf16[512,256]{1,0:T(8,128)(2,1)S(1)}, bf16[512,256]{1,0:T(8,128)(2,1)}, u32[]{:S(2)}) copy-start(bf16[512,256]{1,0:T(8,128)(2,1)} %get-tuple-element.48.own_ref) | copy-start | bytes 786436
  79.3 61.7 %copy-start.2 = (bf16[1024,256]{1,0:T(8,128)(2,1)S(1)}, bf16[1024,256]{1,0:T(8,128)(2,1)}, u32[]{:S(2)}) copy-start(bf16[1024,256]{1,0:T(8,128)(2,1)} %tok_ref.3) | copy-start | bytes 1572868
  79.3 61.7 %copy-start.3 = (bf16[1024,256]{1,0:T(8,128)(2,1)S(1)}, bf16[1024,256]{1,0:T(8,128)(2,1)}, u32[]{:S(2)}) copy-start(bf16[1024,256]{1,0:T(8,128)(2,1)} %grad_ref.3) | copy-start | bytes 1572868
  79.3 61.7 %all-to-all-start.1 = ((bf16[32,16,1024]{2,1,0:T(8,128)(2,1)}), bf16[32,16,1024]{2,1,0:T(8,128)(2,1)S(1)}, u32[]{:S(2)}, u32[]{:S(2)}) async-start(bf16[32,16,1024]{2,1,0:T(8,128)(2,1)} %get-tuple-element.47), calls=%async_computation.1 | async-start | bytes 2097152 | tf_op jit(solution)/shard_map/all_to_all | solution.py:155
  90.3 11.7 %collective-permute-start = (bf16[512,256]{1,0:T(8,128)(2,1)}, bf16[512,256]{1,0:T(8,128)(2,1)S(1)}, u32[]{:S(2)}, u32[]{:S(2)}) collective-permute-start(bf16[512,256]{1,0:T(8,128)(2,1)} %get-tuple-element.49), channel_id=1, source_target_pairs={{0,32},{32,64},{64,96},{96,0},{128,160},{160,192},{192,224},{224,1... | collective-permute-start | bytes 786440 | tf_op jit(solution)/shard_map/ppermute | solution.py:141
  93.7 15.0 %collective-permute-start.1 = (bf16[512,256]{1,0:T(8,128)(2,1)}, bf16[512,256]{1,0:T(8,128)(2,1)S(1)}, u32[]{:S(2)}, u32[]{:S(2)}) collective-permute-start(bf16[512,256]{1,0:T(8,128)(2,1)} %get-tuple-element.50), channel_id=1, source_target_pairs={{0,64},{32,96},{64,0},{96,32},{128,192},{160,224},{192,128},{224,1... | collective-permute-start | bytes 786440 | tf_op jit(solution)/shard_map/ppermute | solution.py:141
  98.6 11.5 %collective-permute-start.2 = (bf16[512,256]{1,0:T(8,128)(2,1)S(1)}, bf16[512,256]{1,0:T(8,128)(2,1)S(1)}, u32[]{:S(2)}, u32[]{:S(2)}) collective-permute-start(bf16[512,256]{1,0:T(8,128)(2,1)S(1)} %copy-done.7), channel_id=1, source_target_pairs={{0,96},{32,0},{64,32},{96,64},{128,224},{160,128},{192,160},{224,1... | collective-permute-start | bytes 786440 | tf_op jit(solution)/shard_map/ppermute | solution.py:141
  110.4 11.4 %collective-permute-start.3 = (bf16[128,256]{1,0:T(8,128)(2,1)S(1)}, bf16[128,256]{1,0:T(8,128)(2,1)S(1)}, u32[]{:S(2)}, u32[]{:S(2)}) collective-permute-start(bf16[128,256]{1,0:T(8,128)(2,1)S(1)} %get-tuple-element.53), channel_id=1, source_target_pairs={{0,128},{32,160},{64,192},{96,224},{128,256},{160,288},{192,320},{... | collective-permute-start | bytes 196616 | tf_op jit(solution)/shard_map/ppermute | solution.py:141
  113.9 22.1 %collective-permute-start.4 = (bf16[128,256]{1,0:T(8,128)(2,1)S(1)}, bf16[128,256]{1,0:T(8,128)(2,1)S(1)}, u32[]{:S(2)}, u32[]{:S(2)}) collective-permute-start(bf16[128,256]{1,0:T(8,128)(2,1)S(1)} %get-tuple-element.54), channel_id=1, source_target_pairs={{0,256},{32,288},{64,320},{96,352},{128,384},{160,416},{192,448},{... | collective-permute-start | bytes 196616 | tf_op jit(solution)/shard_map/ppermute | solution.py:141
  117.0 24.0 %collective-permute-start.5 = (bf16[128,256]{1,0:T(8,128)(2,1)S(1)}, bf16[128,256]{1,0:T(8,128)(2,1)S(1)}, u32[]{:S(2)}, u32[]{:S(2)}) collective-permute-start(bf16[128,256]{1,0:T(8,128)(2,1)S(1)} %get-tuple-element.55), channel_id=1, source_target_pairs={{0,384},{32,416},{64,448},{96,480},{128,0},{160,32},{192,64},{224,... | collective-permute-start | bytes 196616 | tf_op jit(solution)/shard_map/ppermute | solution.py:141
  177.7 4.7 %copy-start.4 = (bf16[256,256]{1,0:T(8,128)(2,1)S(1)}, bf16[256,256]{1,0:T(8,128)(2,1)}, u32[]{:S(2)}) copy-start(bf16[256,256]{1,0:T(8,128)(2,1)} %left_up_ref.3) | copy-start | bytes 393220
  177.7 4.7 %copy-start.5 = (bf16[256,256]{1,0:T(8,128)(2,1)S(1)}, bf16[256,256]{1,0:T(8,128)(2,1)}, u32[]{:S(2)}) copy-start(bf16[256,256]{1,0:T(8,128)(2,1)} %right_down_ref.3) | copy-start | bytes 393220
  178.9 20.9 %all-to-all-start.4 = ((bf16[4,640,256]{2,1,0:T(8,128)(2,1)}), bf16[4,640,256]{2,1,0:T(8,128)(2,1)S(1)}, u32[]{:S(2)}, u32[]{:S(2)}) async-start(bf16[4,640,256]{2,1,0:T(8,128)(2,1)} %shard_map.116), calls=%async_computation.4 | async-start | bytes 2621440 | tf_op jit(solution)/shard_map/all_to_all | solution.py:155

commit v5 on v4

--- a/solution.py
+++ b/solution.py
@@ -62,12 +62,28 @@
     send_ref[...] = weave(third, back_mixed)
 
 
-def middle_grads_kernel(place_ref, hidden_ref, back_pre_ref, mixed_ref, back_third_ref, *out_refs):
-    for step, out_ref in enumerate(out_refs):
-        start = pl.multiple_of(((place_ref[0] + step) & 3) * 256, 256)
-        block = pl.ds(start, 256)
-        out_ref[:256] = dot(hidden_ref[block, :], back_third_ref[...], NT).astype(BF16)
-        out_ref[256:] = dot(mixed_ref[...], back_pre_ref[block, :], NT).astype(BF16)
+def middle_grads_kernel(place_ref, hidden_hbm, back_pre_hbm, mixed_hbm, back_third_hbm,
+                        own_ref, near_ref, far_ref, last_ref,
+                        hidden_ref, back_pre_ref, mixed_ref, back_third_ref, sems):
+    small = [pltpu.make_async_copy(mixed_hbm, mixed_ref, sems.at[0]),
+             pltpu.make_async_copy(back_third_hbm, back_third_ref, sems.at[1])]
+    large = []
+    for step in range(4):
+        rows = pl.ds(pl.multiple_of(((place_ref[0] + step) & 3) * 256, 256), 256)
+        large.append((pltpu.make_async_copy(hidden_hbm.at[rows], hidden_ref.at[step], sems.at[2 + step]),
+                      pltpu.make_async_copy(back_pre_hbm.at[rows], back_pre_ref.at[step], sems.at[6 + step])))
+    for copy in small:
+        copy.start()
+    for pair in large:
+        for copy in pair:
+            copy.start()
+    for copy in small:
+        copy.wait()
+    for step, out_ref in enumerate((own_ref, near_ref, far_ref, last_ref)):
+        large[step][0].wait()
+        out_ref[:256] = dot(hidden_ref[step], back_third_ref[...], NT).astype(BF16)
+        large[step][1].wait()
+        out_ref[256:] = dot(mixed_ref[...], back_pre_ref[step], NT).astype(BF16)
 
 
 def fold_kernel(place_ref, own_ref, near_ref, far_ref, last_ref, *rest):
@@ -78,11 +94,18 @@
         out_ref[...] = total_ref[pl.ds(start, 128), :]
 
 
-def exit_grads_kernel(recv_ref, tok_ref, grad_ref, out_ref, mixed_ref, back_first_ref):
+def exit_grads_kernel(recv_ref, tok_hbm, grad_hbm, out_ref, mixed_ref, back_first_ref,
+                      tok_ref, grad_ref, sems):
+    grad_copy = pltpu.make_async_copy(grad_hbm, grad_ref, sems.at[0])
+    tok_copy = pltpu.make_async_copy(tok_hbm, tok_ref, sems.at[1])
+    grad_copy.start()
+    tok_copy.start()
     mixed, back_first = unweave(recv_ref[...])
     mixed_ref[...] = mixed
     back_first_ref[...] = back_first
+    grad_copy.wait()
     out_ref[:256] = dot(mixed, grad_ref[...]).astype(BF16)
+    tok_copy.wait()
     out_ref[256:] = dot(back_first, tok_ref[...]).T.astype(BF16)
 
 
@@ -96,22 +119,23 @@
     late = jnp.sum(late_ref[...].astype(F32), axis=0).astype(BF16)
     early = four_sum(own_ref[...], near_ref[...], far_ref[...], last_ref[...])
     for peer in range(4):
-        out_ref[peer, :128] = late
-        out_ref[peer, 128:] = early
+        out_ref[peer, :32] = late
+        out_ref[peer, 32:] = early
 
 
 def pack_kernel(parts_ref, out_ref):
-    late = jnp.sum(parts_ref[:, :128].astype(F32), axis=0).astype(BF16)
     for peer in range(4):
-        out_ref[peer, :128] = late
         for z_lo in range(4):
-            out_ref[peer, 128 + z_lo * 128:256 + z_lo * 128] = parts_ref[z_lo, 128:]
+            out_ref[peer, z_lo * 32:z_lo * 32 + 32] = parts_ref[z_lo, :32]
+            out_ref[peer, 128 + z_lo * 128:256 + z_lo * 128] = parts_ref[z_lo, 32:]
 
 
 def unpack_kernel(all_ref, left_up_ref, right_up_ref, left_down_ref, right_down_ref):
     for y in range(4):
-        late_ref = right_down_ref if y < 2 else left_up_ref
-        late_ref[y % 2 * 128:y % 2 * 128 + 128] = all_ref[y, :128]
+        for z_lo in range(4):
+            start = (z_lo * 4 + y) * 32
+            late_ref = right_down_ref if start < 256 else left_up_ref
+            late_ref[start % 256:start % 256 + 32] = all_ref[y, z_lo * 32:z_lo * 32 + 32]
         left_down_ref[y * 256:y * 256 + 256] = all_ref[y, 128:384]
         right_up_ref[:, y * 256:y * 256 + 256] = all_ref[y, 384:]
 
@@ -184,22 +208,26 @@
         grid=(tok // tile,),
         in_specs=[woven(tile), weight(256, 1024), weight(1024, 256), weight(1024, 256), weight(256, 1024)],
         out_specs=[woven(tile), column(1024), column(1024), column(256), column(256)],
-        out_shape=[hbm((32, 16, tok)), plain((1024, tok)), plain((1024, tok)),
-                   plain((256, tok)), plain((256, tok))],
+        out_shape=[hbm((32, 16, tok)), hbm((1024, tok)), hbm((1024, tok)),
+                   hbm((256, tok)), hbm((256, tok))],
         compiler_params=PARAMS,
     )(recv, right_up, right_up.T, left_down, left_down.T)
+    recv = exchange(send, "tensor")
+
     vmem = pl.BlockSpec(memory_space=pltpu.VMEM)
     smem = pl.BlockSpec(memory_space=pltpu.SMEM)
+    far_away = pl.BlockSpec(memory_space=pltpu.HBM)
     y_place = y.astype(jnp.int32).reshape(1)
     z_place = z_lo.astype(jnp.int32).reshape(1)
     parts = pl.pallas_call(
         middle_grads_kernel,
-        in_specs=[smem] + [vmem] * 4,
-        out_shape=[hbm((512, 256))] * 4,
-        compiler_params=PARAMS,
-    )(y_place, hidden, back_pre, mixed_up, back_third)
-    send, parts = lax.optimization_barrier((send, parts))
-    recv = exchange(send, "tensor")
+        in_specs=[smem] + [far_away] * 4,
+        out_shape=[plain((512, 256))] * 4,
+        scratch_shapes=[pltpu.VMEM((4, 256, tok), BF16), pltpu.VMEM((4, 256, tok), BF16),
+                        pltpu.VMEM((256, tok), BF16), pltpu.VMEM((256, tok), BF16),
+                        pltpu.SemaphoreType.DMA((10,))],
+        compiler_params=PARAMS,
+    )(y_place, in_hbm(hidden), in_hbm(back_pre), in_hbm(mixed_up), in_hbm(back_third))
 
     parts = pl.pallas_call(
         fold_kernel,
@@ -211,11 +239,16 @@
     pieces = send_on(parts, False)
     recv, pieces = lax.optimization_barrier((recv, pieces))
 
-    late, mixed_down, back_first = whole_call(
-        exit_grads_kernel, [hbm((512, 256)), plain((256, tok)), plain((256, tok))],
-        recv, tokens_in, out_grad)
-    late = exchange(late.reshape(4, 128, 256), "dp", ALONG_Y)
-    late = whole_call(spread_kernel, hbm((4, 256, 256)), late, *pieces)
+    late, mixed_down, back_first = pl.pallas_call(
+        exit_grads_kernel,
+        in_specs=[vmem, far_away, far_away],
+        out_shape=[hbm((512, 256)), plain((256, tok)), plain((256, tok))],
+        scratch_shapes=[pltpu.VMEM((tok, 256), BF16), pltpu.VMEM((tok, 256), BF16),
+                        pltpu.SemaphoreType.DMA((2,))],
+        compiler_params=PARAMS,
+    )(recv, in_hbm(tokens_in), in_hbm(out_grad))
+    late = exchange(late.reshape(16, 32, 256), "dp")
+    late = whole_call(spread_kernel, hbm((4, 160, 256)), late, *pieces)
     late = exchange(late, "dp", ALONG_Z)
     packed = whole_call(pack_kernel, hbm((4, 640, 256)), late)
     packed = exchange(packed, "dp", ALONG_Y)

time: 202 us -> 201 us (level); the launches traced: 201 us -> 197 us
  waiting for transfers between devices: 92.4 us -> 86.8 us
  Pallas kernels: 17 us -> 21.2 us
    pallas_call x1 -> x2, Pallas kernels: 2.07 us -> 7.76 us  [the longest x1 5.09 us: on_device(): pl.pallas_call(middle_grads_kernel, in_specs=[smem] + [far_away] * 4, out...]
    ppermute x6, waiting for transfers between devices: 27.6 us -> 24 us  [permute(): return lax.ppermute(array, 'dp', shift_pairs(inner, step))]
    all_to_all x3, waiting for transfers between devices: 64.9 us -> 62.8 us  [exchange(): lax.all_to_all(parts, axis, 0, 0, axis_index_groups=groups, tiled=True)]
    pallas_call x5 -> x4, Pallas kernels: 5.91 us -> 4.62 us  [whole_call(): return pl.pallas_call(kernel, out_shape=outs, compiler_params=PARAMS)(*args)]
  transfers between devices with their start and end apart: 9 -> 9, of which waited for: 7 -> 6; matrix products, arithmetic and copies ran while one was open for 0% -> 0% of each run, Pallas kernels for 1% -> 3%
where the time goes in v5:
time: 201 us; the launch traced here: 197 us
  waiting for transfers between devices  86.8 us (43%)
  starting transfers between devices  55.6 us (28%)
  blocking collectives  32.6 us (16%)
  Pallas kernels  21.2 us (11%)
    all_to_all x3, waiting for transfers between devices, exchange(): lax.all_to_all(parts, axis, 0, 0, axis_index_groups=groups, tiled=True)  62.8 us
    all_to_all x3, starting transfers between devices, exchange(): lax.all_to_all(parts, axis, 0, 0, axis_index_groups=groups, tiled=True)  32.7 us
    all_to_all x2, blocking collectives, exchange(): lax.all_to_all(parts, axis, 0, 0, axis_index_groups=groups, tiled=True)  32.6 us
    ppermute x6, waiting for transfers between devices, permute(): return lax.ppermute(array, 'dp', shift_pairs(inner, step))  24 us
    ppermute x6, starting transfers between devices, permute(): return lax.ppermute(array, 'dp', shift_pairs(inner, step))  22.9 us
    pallas_call x1, Pallas kernels, on_device(): pl.pallas_call(middle_kernel, grid=(tok // tile,), in_specs=[woven(tile),...  5.85 us
    pallas_call x1, Pallas kernels, on_device(): pl.pallas_call(middle_grads_kernel, in_specs=[smem] + [far_away] * 4, out...  5.09 us
    pallas_call x4, Pallas kernels, whole_call(): return pl.pallas_call(kernel, out_shape=outs, compiler_params=PARAMS)(*args)  4.62 us
  transfers between devices with their start and end apart: 9, of which 6 were waited for; matrix products, arithmetic and copies ran while one was open for 0% of the time, Pallas kernels for 3%

profile of v5, /device:TPU:6, one launch (start us, length us, event | category | flops | bytes accessed | tf_op | source)
XLA Modules:
  0.0 197.4 jit_solution(3891948484049841606)
XLA Ops:
  0.6 0.0 copy-start
  0.6 2.7 %shard_map.109 = bf16[32,16,1024]{2,1,0:T(8,128)(2,1)} custom-call(bf16[1024,256]{1,0:T(8,128)(2,1)} %tok_hbm.1, bf16[1024,256]{1,0:T(8,128)(2,1)} %grad_hbm.1, bf16[256,256]{1,0:T(8,128)(2,1)} %left_up_ref.3, bf16[256,256]{1,0:T(8,128)(2,1)} %right_down_ref.3), custom_call_target="tpu_custom_call" | custom-call | tf_op jit(solution)/shard_map/pallas_call | solution.py:196
  3.4 0.0 copy-start.1
  3.4 18.4 %all-to-all-start = ((bf16[32,16,1024]{2,1,0:T(8,128)(2,1)}), bf16[32,16,1024]{2,1,0:T(8,128)(2,1)S(1)}, u32[]{:S(2)}, u32[]{:S(2)}) async-start(bf16[32,16,1024]{2,1,0:T(8,128)(2,1)} %shard_map.109), calls=%async_computation | async-start | bytes 2097152 | tf_op jit(solution)/shard_map/all_to_all | solution.py:179
  21.7 0.0 copy-done
  21.8 0.2 copy.12
  22.0 0.0 copy-done.1
  22.0 0.2 copy.13
  22.2 49.0 %all-to-all-done.recv_ref = bf16[32,16,1024]{2,1,0:T(8,128)(2,1)S(1)} async-done(((bf16[32,16,1024]{2,1,0:T(8,128)(2,1)}), bf16[32,16,1024]{2,1,0:T(8,128)(2,1)S(1)}, u32[]{:S(2)}, u32[]{:S(2)}) %all-to-all-start) | async-done | bytes 1048608 | tf_op jit(solution)/shard_map/all_to_all | solution.py:179
  71.2 5.9 %shard_map.110 = (bf16[32,16,1024]{2,1,0:T(8,128)(2,1)}, bf16[1024,1024]{1,0:T(8,128)(2,1)}, bf16[1024,1024]{1,0:T(8,128)(2,1)}, bf16[256,1024]{1,0:T(8,128)(2,1)}, bf16[256,1024]{1,0:T(8,128)(2,1)}) custom-call(bf16[32,16,1024]{2,1,0:T(8,128)(2,1)S(1)} %all-to-all-done.recv_ref, bf16[256,1024]{1,0:T(8,128)(2,1)S(1)} %copy-done, ...), custom_call_target="tpu_custom_call" | custom-call | tf_op jit(solution)/shard_map/pallas_call | solution.py:206
  77.0 10.8 %all-to-all-start.1 = ((bf16[32,16,1024]{2,1,0:T(8,128)(2,1)}), bf16[32,16,1024]{2,1,0:T(8,128)(2,1)S(1)}, u32[]{:S(2)}, u32[]{:S(2)}) async-start(bf16[32,16,1024]{2,1,0:T(8,128)(2,1)} %get-tuple-element.33), calls=%async_computation.1 | async-start | bytes 2097152 | tf_op jit(solution)/shard_map/all_to_all | solution.py:179
  87.9 5.1 %shard_map.111 = (bf16[512,256]{1,0:T(8,128)(2,1)S(1)}, bf16[512,256]{1,0:T(8,128)(2,1)S(1)}, bf16[512,256]{1,0:T(8,128)(2,1)S(1)}, bf16[512,256]{1,0:T(8,128)(2,1)S(1)}) custom-call(s32[1]{0:T(128)} %bitcast.3.place_ref, bf16[1024,1024]{1,0:T(8,128)(2,1)} %get-tuple-element.34.hidden_hbm, bf16[1024,1024]{1,0:T(8,128)(2,1)} %get-tuple-element.35.back_pre_hbm, ...), custom_call_target="tpu_custom_call" | custom-call | tf_op jit(solution)/shard_map/pallas_call | solution.py:222
  93.0 3.5 %collective-permute-start = (bf16[512,256]{1,0:T(8,128)(2,1)S(1)}, bf16[512,256]{1,0:T(8,128)(2,1)S(1)}, u32[]{:S(2)}, u32[]{:S(2)}) collective-permute-start(bf16[512,256]{1,0:T(8,128)(2,1)S(1)} %get-tuple-element.39), channel_id=1, source_target_pairs={{0,32},{32,64},{64,96},{96,0},{128,160},{160,192},{192,224},{224,1... | collective-permute-start | bytes 786440 | tf_op jit(solution)/shard_map/ppermute | solution.py:165
  96.5 4.8 %collective-permute-start.1 = (bf16[512,256]{1,0:T(8,128)(2,1)S(1)}, bf16[512,256]{1,0:T(8,128)(2,1)S(1)}, u32[]{:S(2)}, u32[]{:S(2)}) collective-permute-start(bf16[512,256]{1,0:T(8,128)(2,1)S(1)} %get-tuple-element.40), channel_id=1, source_target_pairs={{0,64},{32,96},{64,0},{96,32},{128,192},{160,224},{192,128},{224,1... | collective-permute-start | bytes 786440 | tf_op jit(solution)/shard_map/ppermute | solution.py:165
  101.3 3.3 %collective-permute-start.2 = (bf16[512,256]{1,0:T(8,128)(2,1)S(1)}, bf16[512,256]{1,0:T(8,128)(2,1)S(1)}, u32[]{:S(2)}, u32[]{:S(2)}) collective-permute-start(bf16[512,256]{1,0:T(8,128)(2,1)S(1)} %get-tuple-element.41), channel_id=1, source_target_pairs={{0,96},{32,0},{64,32},{96,64},{128,224},{160,128},{192,160},{224,1... | collective-permute-start | bytes 786440 | tf_op jit(solution)/shard_map/ppermute | solution.py:165
  104.5 0.0 collective-permute-done.near_ref
  104.6 6.7 %collective-permute-done.1.far_ref = bf16[512,256]{1,0:T(8,128)(2,1)S(1)} collective-permute-done((bf16[512,256]{1,0:T(8,128)(2,1)S(1)}, bf16[512,256]{1,0:T(8,128)(2,1)S(1)}, u32[]{:S(2)}, u32[]{:S(2)}) %collective-permute-start.1) | collective-permute-done | bytes 262176 | tf_op jit(solution)/shard_map/ppermute | solution.py:165
  111.3 1.3 collective-permute-done.2.last_ref
  112.6 0.2 shard_map.112
  112.9 3.5 %collective-permute-start.3 = (bf16[128,256]{1,0:T(8,128)(2,1)S(1)}, bf16[128,256]{1,0:T(8,128)(2,1)S(1)}, u32[]{:S(2)}, u32[]{:S(2)}) collective-permute-start(bf16[128,256]{1,0:T(8,128)(2,1)S(1)} %get-tuple-element.43), channel_id=1, source_target_pairs={{0,128},{32,160},{64,192},{96,224},{128,256},{160,288},{192,320},{... | collective-permute-start | bytes 196616 | tf_op jit(solution)/shard_map/ppermute | solution.py:165
  116.4 3.1 %collective-permute-start.4 = (bf16[128,256]{1,0:T(8,128)(2,1)S(1)}, bf16[128,256]{1,0:T(8,128)(2,1)S(1)}, u32[]{:S(2)}, u32[]{:S(2)}) collective-permute-start(bf16[128,256]{1,0:T(8,128)(2,1)S(1)} %get-tuple-element.44), channel_id=1, source_target_pairs={{0,256},{32,288},{64,320},{96,352},{128,384},{160,416},{192,448},{... | collective-permute-start | bytes 196616 | tf_op jit(solution)/shard_map/ppermute | solution.py:165
  119.5 4.7 %collective-permute-start.5 = (bf16[128,256]{1,0:T(8,128)(2,1)S(1)}, bf16[128,256]{1,0:T(8,128)(2,1)S(1)}, u32[]{:S(2)}, u32[]{:S(2)}) collective-permute-start(bf16[128,256]{1,0:T(8,128)(2,1)S(1)} %get-tuple-element.45), channel_id=1, source_target_pairs={{0,384},{32,416},{64,448},{96,480},{128,0},{160,32},{192,64},{224,... | collective-permute-start | bytes 196616 | tf_op jit(solution)/shard_map/ppermute | solution.py:165
  124.2 0.0 collective-permute-done.3.near_ref
  124.2 14.6 %collective-permute-done.4.far_ref = bf16[128,256]{1,0:T(8,128)(2,1)S(1)} collective-permute-done((bf16[128,256]{1,0:T(8,128)(2,1)S(1)}, bf16[128,256]{1,0:T(8,128)(2,1)S(1)}, u32[]{:S(2)}, u32[]{:S(2)}) %collective-permute-start.4) | collective-permute-done | bytes 65568 | tf_op jit(solution)/shard_map/ppermute | solution.py:165
  138.8 1.3 collective-permute-done.5.last_ref
  140.1 0.0 all-to-all-done.1.recv_ref
  140.1 2.7 %shard_map.113 = (bf16[512,256]{1,0:T(8,128)(2,1)}, bf16[256,1024]{1,0:T(8,128)(2,1)S(1)}, bf16[256,1024]{1,0:T(8,128)(2,1)S(1)}) custom-call(bf16[32,16,1024]{2,1,0:T(8,128)(2,1)S(1)} %all-to-all-done.1.recv_ref, bf16[1024,256]{1,0:T(8,128)(2,1)} %tok_hbm.1, bf16[1024,256]{1,0:T(8,128)(2,1)} %grad_hbm.1), custom_call_target="tpu_custom_call" | custom-call | tf_op jit(solution)/shard_map/pallas_call | solution.py:242
  142.8 20.2 %all_to_all.25.late_ref = bf16[16,32,256]{2,1,0:T(8,128)(2,1)S(1)} all-to-all(bf16[16,32,256]{2,1,0:T(8,128)(2,1)} %bitcast.7), channel_id=1, replica_groups=mesh['dp'=16,'tensor'=32] {'dp'}, dimensions={0} | all-to-all | bytes 524288 | tf_op jit(solution)/shard_map/all_to_all | solution.py:179
  163.0 0.8 shard_map.115
  163.8 12.4 %all_to_all.26.parts_ref = bf16[4,160,256]{2,1,0:T(8,128)(2,1)S(1)} all-to-all(bf16[4,160,256]{2,1,0:T(8,128)(2,1)} %shard_map.115), channel_id=1, replica_groups={{0,128,256,384},{32,160,288,416},{64,192,320,448},{96,224,352,480},{1,1..., dimensions={0} | all-to-all | bytes 655360 | tf_op jit(solution)/shard_map/all_to_all | solution.py:179
  176.2 0.0 copy-start.2
  176.2 0.0 copy-start.3
  176.2 1.2 shard_map.116
  177.4 3.5 %all-to-all-start.4 = ((bf16[4,640,256]{2,1,0:T(8,128)(2,1)}), bf16[4,640,256]{2,1,0:T(8,128)(2,1)S(1)}, u32[]{:S(2)}, u32[]{:S(2)}) async-start(bf16[4,640,256]{2,1,0:T(8,128)(2,1)} %shard_map.116), calls=%async_computation.4 | async-start | bytes 2621440 | tf_op jit(solution)/shard_map/all_to_all | solution.py:179
  180.9 0.0 copy-done.2
  181.0 0.0 copy-done.3
  181.0 1.5 shard_map.114
  182.5 13.8 %all-to-all-done.4.all_ref = bf16[4,640,256]{2,1,0:T(8,128)(2,1)S(1)} async-done(((bf16[4,640,256]{2,1,0:T(8,128)(2,1)}), bf16[4,640,256]{2,1,0:T(8,128)(2,1)S(1)}, u32[]{:S(2)}, u32[]{:S(2)}) %all-to-all-start.4) | async-done | bytes 1310752 | tf_op jit(solution)/shard_map/all_to_all | solution.py:179
  196.3 1.2 shard_map.117
Async XLA Ops:
  0.6 21.1 %copy-start = (bf16[256,1024]{1,0:T(8,128)(2,1)S(1)}, bf16[256,1024]{1,0:T(8,128)(2,1)}, u32[]{:S(2)}) copy-start(bf16[256,1024]{1,0:T(8,128)(2,1)} %right_up_ref.1) | copy-start | bytes 1572868
  3.4 18.6 %copy-start.1 = (bf16[1024,256]{1,0:T(8,128)(2,1)S(1)}, bf16[1024,256]{1,0:T(8,128)(2,1)}, u32[]{:S(2)}) copy-start(bf16[1024,256]{1,0:T(8,128)(2,1)} %left_down_ref.1) | copy-start | bytes 1572868
  3.4 67.8 %all-to-all-start = ((bf16[32,16,1024]{2,1,0:T(8,128)(2,1)}), bf16[32,16,1024]{2,1,0:T(8,128)(2,1)S(1)}, u32[]{:S(2)}, u32[]{:S(2)}) async-start(bf16[32,16,1024]{2,1,0:T(8,128)(2,1)} %shard_map.109), calls=%async_computation | async-start | bytes 2097152 | tf_op jit(solution)/shard_map/all_to_all | solution.py:179
  77.0 63.1 %all-to-all-start.1 = ((bf16[32,16,1024]{2,1,0:T(8,128)(2,1)}), bf16[32,16,1024]{2,1,0:T(8,128)(2,1)S(1)}, u32[]{:S(2)}, u32[]{:S(2)}) async-start(bf16[32,16,1024]{2,1,0:T(8,128)(2,1)} %get-tuple-element.33), calls=%async_computation.1 | async-start | bytes 2097152 | tf_op jit(solution)/shard_map/all_to_all | solution.py:179
  93.0 11.6 %collective-permute-start = (bf16[512,256]{1,0:T(8,128)(2,1)S(1)}, bf16[512,256]{1,0:T(8,128)(2,1)S(1)}, u32[]{:S(2)}, u32[]{:S(2)}) collective-permute-start(bf16[512,256]{1,0:T(8,128)(2,1)S(1)} %get-tuple-element.39), channel_id=1, source_target_pairs={{0,32},{32,64},{64,96},{96,0},{128,160},{160,192},{192,224},{224,1... | collective-permute-start | bytes 786440 | tf_op jit(solution)/shard_map/ppermute | solution.py:165
  96.5 14.8 %collective-permute-start.1 = (bf16[512,256]{1,0:T(8,128)(2,1)S(1)}, bf16[512,256]{1,0:T(8,128)(2,1)S(1)}, u32[]{:S(2)}, u32[]{:S(2)}) collective-permute-start(bf16[512,256]{1,0:T(8,128)(2,1)S(1)} %get-tuple-element.40), channel_id=1, source_target_pairs={{0,64},{32,96},{64,0},{96,32},{128,192},{160,224},{192,128},{224,1... | collective-permute-start | bytes 786440 | tf_op jit(solution)/shard_map/ppermute | solution.py:165
  101.3 11.3 %collective-permute-start.2 = (bf16[512,256]{1,0:T(8,128)(2,1)S(1)}, bf16[512,256]{1,0:T(8,128)(2,1)S(1)}, u32[]{:S(2)}, u32[]{:S(2)}) collective-permute-start(bf16[512,256]{1,0:T(8,128)(2,1)S(1)} %get-tuple-element.41), channel_id=1, source_target_pairs={{0,96},{32,0},{64,32},{96,64},{128,224},{160,128},{192,160},{224,1... | collective-permute-start | bytes 786440 | tf_op jit(solution)/shard_map/ppermute | solution.py:165
  112.9 11.3 %collective-permute-start.3 = (bf16[128,256]{1,0:T(8,128)(2,1)S(1)}, bf16[128,256]{1,0:T(8,128)(2,1)S(1)}, u32[]{:S(2)}, u32[]{:S(2)}) collective-permute-start(bf16[128,256]{1,0:T(8,128)(2,1)S(1)} %get-tuple-element.43), channel_id=1, source_target_pairs={{0,128},{32,160},{64,192},{96,224},{128,256},{160,288},{192,320},{... | collective-permute-start | bytes 196616 | tf_op jit(solution)/shard_map/ppermute | solution.py:165
  116.4 22.4 %collective-permute-start.4 = (bf16[128,256]{1,0:T(8,128)(2,1)S(1)}, bf16[128,256]{1,0:T(8,128)(2,1)S(1)}, u32[]{:S(2)}, u32[]{:S(2)}) collective-permute-start(bf16[128,256]{1,0:T(8,128)(2,1)S(1)} %get-tuple-element.44), channel_id=1, source_target_pairs={{0,256},{32,288},{64,320},{96,352},{128,384},{160,416},{192,448},{... | collective-permute-start | bytes 196616 | tf_op jit(solution)/shard_map/ppermute | solution.py:165
  119.5 20.6 %collective-permute-start.5 = (bf16[128,256]{1,0:T(8,128)(2,1)S(1)}, bf16[128,256]{1,0:T(8,128)(2,1)S(1)}, u32[]{:S(2)}, u32[]{:S(2)}) collective-permute-start(bf16[128,256]{1,0:T(8,128)(2,1)S(1)} %get-tuple-element.45), channel_id=1, source_target_pairs={{0,384},{32,416},{64,448},{96,480},{128,0},{160,32},{192,64},{224,... | collective-permute-start | bytes 196616 | tf_op jit(solution)/shard_map/ppermute | solution.py:165
  176.2 4.7 %copy-start.2 = (bf16[256,256]{1,0:T(8,128)(2,1)S(1)}, bf16[256,256]{1,0:T(8,128)(2,1)}, u32[]{:S(2)}) copy-start(bf16[256,256]{1,0:T(8,128)(2,1)} %left_up_ref.3) | copy-start | bytes 393220
  176.2 4.7 %copy-start.3 = (bf16[256,256]{1,0:T(8,128)(2,1)S(1)}, bf16[256,256]{1,0:T(8,128)(2,1)}, u32[]{:S(2)}) copy-start(bf16[256,256]{1,0:T(8,128)(2,1)} %right_down_ref.3) | copy-start | bytes 393220
  177.4 18.9 %all-to-all-start.4 = ((bf16[4,640,256]{2,1,0:T(8,128)(2,1)}), bf16[4,640,256]{2,1,0:T(8,128)(2,1)S(1)}, u32[]{:S(2)}, u32[]{:S(2)}) async-start(bf16[4,640,256]{2,1,0:T(8,128)(2,1)} %shard_map.116), calls=%async_computation.4 | async-start | bytes 2621440 | tf_op jit(solution)/shard_map/all_to_all | solution.py:179

commit v6 on v5

--- a/solution.py
+++ b/solution.py
@@ -13,8 +13,6 @@
 NN = (((1,), (0,)), ((), ()))
 TN = (((0,), (0,)), ((), ()))
 PARAMS = pltpu.CompilerParams(vmem_limit_bytes=24 * 1024 * 1024)
-ALONG_Y = [[z_lo * 4 + y for y in range(4)] for z_lo in range(4)]
-ALONG_Z = [[z_lo * 4 + y for z_lo in range(4)] for y in range(4)]
 
 
 def dot(left, right, dims=NN):
@@ -94,18 +92,11 @@
         out_ref[...] = total_ref[pl.ds(start, 128), :]
 
 
-def exit_grads_kernel(recv_ref, tok_hbm, grad_hbm, out_ref, mixed_ref, back_first_ref,
-                      tok_ref, grad_ref, sems):
-    grad_copy = pltpu.make_async_copy(grad_hbm, grad_ref, sems.at[0])
-    tok_copy = pltpu.make_async_copy(tok_hbm, tok_ref, sems.at[1])
-    grad_copy.start()
-    tok_copy.start()
+def exit_grads_kernel(recv_ref, tok_ref, grad_ref, out_ref, mixed_ref, back_first_ref):
     mixed, back_first = unweave(recv_ref[...])
     mixed_ref[...] = mixed
     back_first_ref[...] = back_first
-    grad_copy.wait()
     out_ref[:256] = dot(mixed, grad_ref[...]).astype(BF16)
-    tok_copy.wait()
     out_ref[256:] = dot(back_first, tok_ref[...]).T.astype(BF16)
 
 
@@ -115,29 +106,22 @@
     in_grad_ref[...] = dot(back_first_ref[...], left_up_t, TN).astype(BF16)
 
 
-def spread_kernel(late_ref, own_ref, near_ref, far_ref, last_ref, out_ref):
+def spread_kernel(place_ref, late_ref, own_ref, near_ref, far_ref, last_ref, late_out_ref, early_out_ref):
     late = jnp.sum(late_ref[...].astype(F32), axis=0).astype(BF16)
-    early = four_sum(own_ref[...], near_ref[...], far_ref[...], last_ref[...])
-    for peer in range(4):
-        out_ref[peer, :32] = late
-        out_ref[peer, 32:] = early
-
-
-def pack_kernel(parts_ref, out_ref):
-    for peer in range(4):
-        for z_lo in range(4):
-            out_ref[peer, z_lo * 32:z_lo * 32 + 32] = parts_ref[z_lo, :32]
-            out_ref[peer, 128 + z_lo * 128:256 + z_lo * 128] = parts_ref[z_lo, 32:]
-
-
-def unpack_kernel(all_ref, left_up_ref, right_up_ref, left_down_ref, right_down_ref):
-    for y in range(4):
-        for z_lo in range(4):
-            start = (z_lo * 4 + y) * 32
-            late_ref = right_down_ref if start < 256 else left_up_ref
-            late_ref[start % 256:start % 256 + 32] = all_ref[y, z_lo * 32:z_lo * 32 + 32]
-        left_down_ref[y * 256:y * 256 + 256] = all_ref[y, 128:384]
-        right_up_ref[:, y * 256:y * 256 + 256] = all_ref[y, 384:]
+    late_out_ref[...] = jnp.broadcast_to(late[None], late_out_ref.shape)
+    for step, ref in enumerate((own_ref, near_ref, far_ref, last_ref)):
+        start = pl.multiple_of(((place_ref[0] + 4 - step) & 3) * 128, 128)
+        early_out_ref[pl.ds(start, 128), :] = ref[...]
+
+
+def unpack_kernel(place_ref, late_ref, own_ref, near_ref, far_ref, last_ref,
+                  left_up_ref, right_up_ref, left_down_ref, right_down_ref):
+    right_down_ref[...] = late_ref[:8].reshape(256, 256)
+    left_up_ref[...] = late_ref[8:].reshape(256, 256)
+    for step, ref in enumerate((own_ref, near_ref, far_ref, last_ref)):
+        start = pl.multiple_of(((place_ref[0] + 4 - step) & 3) * 256, 256)
+        left_down_ref[pl.ds(start, 256), :] = ref[:256]
+        right_up_ref[:, pl.ds(start, 256)] = ref[256:]
 
 
 def hbm(dims):
@@ -175,8 +159,8 @@
     return [chunks[0], near, far, permute(chunks[3], inner, 3)]
 
 
-def exchange(parts, axis, groups=None):
-    return lax.all_to_all(parts, axis, 0, 0, axis_index_groups=groups, tiled=True)
+def exchange(parts, axis):
+    return lax.all_to_all(parts, axis, 0, 0, tiled=True)
 
 
 def whole_call(kernel, outs, *args):
@@ -237,25 +221,30 @@
         compiler_params=PARAMS,
     )(z_place, *send_on(parts, True))
     pieces = send_on(parts, False)
-    recv, pieces = lax.optimization_barrier((recv, pieces))
-
-    late, mixed_down, back_first = pl.pallas_call(
-        exit_grads_kernel,
-        in_specs=[vmem, far_away, far_away],
-        out_shape=[hbm((512, 256)), plain((256, tok)), plain((256, tok))],
-        scratch_shapes=[pltpu.VMEM((tok, 256), BF16), pltpu.VMEM((tok, 256), BF16),
-                        pltpu.SemaphoreType.DMA((2,))],
-        compiler_params=PARAMS,
-    )(recv, in_hbm(tokens_in), in_hbm(out_grad))
+    part = four_sum(*pieces)
+    recv, part = lax.optimization_barrier((recv, part))
+    late, mixed_down, back_first = whole_call(
+        exit_grads_kernel, [hbm((512, 256)), plain((256, tok)), plain((256, tok))],
+        recv, tokens_in, out_grad)
+
     late = exchange(late.reshape(16, 32, 256), "dp")
-    late = whole_call(spread_kernel, hbm((4, 160, 256)), late, *pieces)
-    late = exchange(late, "dp", ALONG_Z)
-    packed = whole_call(pack_kernel, hbm((4, 640, 256)), late)
-    packed = exchange(packed, "dp", ALONG_Y)
+    pieces = send_on([part] * 4, False)
+    late, part = pl.pallas_call(
+        spread_kernel,
+        in_specs=[smem] + [vmem] * 5,
+        out_shape=[hbm((16, 32, 256)), plain((512, 256))],
+        compiler_params=PARAMS,
+    )(z_place, late, *pieces)
+    late = exchange(late, "dp")
+    pieces = send_on([part] * 4, True)
     layer_out, input_grad = whole_call(
         exit_kernel, [hbm((tok, 256)), hbm((tok, 256))], mixed_down, back_first, left_up, right_down)
-    grads = whole_call(
-        unpack_kernel, [hbm((256, 256)), hbm((256, 1024)), hbm((1024, 256)), hbm((256, 256))], packed)
+    grads = pl.pallas_call(
+        unpack_kernel,
+        in_specs=[smem] + [vmem] * 5,
+        out_shape=[hbm((256, 256)), hbm((256, 1024)), hbm((1024, 256)), hbm((256, 256))],
+        compiler_params=PARAMS,
+    )(y_place, late, *pieces)
     return (layer_out, input_grad, *grads)
 
 

time: 201 us -> 195 us (0.970)
  starting transfers between devices: 55.6 us -> 91.6 us
  blocking collectives: 32.6 us -> 0 us
  waiting for transfers between devices: 86.8 us -> 80.8 us
  Pallas kernels: 21.2 us -> 19 us
    all_to_all x2 -> x0, blocking collectives: 32.6 us -> none  [exchange(): lax.all_to_all(parts, axis, 0, 0, axis_index_groups=groups, tiled=True)]
    ppermute x6 -> x12, starting transfers between devices: 22.9 us -> 46.5 us  [permute(): return lax.ppermute(array, 'dp', shift_pairs(inner, step))]
    all_to_all x3 -> x4, waiting for transfers between devices: 62.8 us -> 49 us  [exchange(): return lax.all_to_all(parts, axis, 0, 0, tiled=True)]
    all_to_all x3 -> x4, starting transfers between devices: 32.7 us -> 45.1 us  [exchange(): return lax.all_to_all(parts, axis, 0, 0, tiled=True)]
    ppermute x6 -> x12, waiting for transfers between devices: 24 us -> 31.7 us  [permute(): return lax.ppermute(array, 'dp', shift_pairs(inner, step))]
    pallas_call x4 -> x2, Pallas kernels: 4.62 us -> 2.72 us  [whole_call(): return pl.pallas_call(kernel, out_shape=outs, compiler_params=PARAMS)(*args)]
  transfers between devices with their start and end apart: 9 -> 16, of which waited for: 6 -> 11; matrix products, arithmetic and copies ran while one was open for 0% -> 0% of each run, Pallas kernels for 3% -> 4%
where the time goes in v6:
time: 195 us; the launch traced here: 193 us
  starting transfers between devices  91.6 us (47%)
  waiting for transfers between devices  80.8 us (41%)
  Pallas kernels  19 us (10%)
    all_to_all x4, waiting for transfers between devices, exchange(): return lax.all_to_all(parts, axis, 0, 0, tiled=True)  49 us
    ppermute x12, starting transfers between devices, permute(): return lax.ppermute(array, 'dp', shift_pairs(inner, step))  46.5 us
    all_to_all x4, starting transfers between devices, exchange(): return lax.all_to_all(parts, axis, 0, 0, tiled=True)  45.1 us
    ppermute x12, waiting for transfers between devices, permute(): return lax.ppermute(array, 'dp', shift_pairs(inner, step))  31.7 us
    pallas_call x1, Pallas kernels, on_device(): pl.pallas_call(middle_kernel, grid=(tok // tile,), in_specs=[woven(tile),...  5.87 us
    pallas_call x1, Pallas kernels, on_device(): pl.pallas_call(middle_grads_kernel, in_specs=[smem] + [far_away] * 4, out...  5.51 us
  transfers between devices with their start and end apart: 16, of which 11 were waited for; matrix products, arithmetic and copies ran while one was open for 0% of the time, Pallas kernels for 4%

profile of v6, /device:TPU:6, one launch (start us, length us, event | category | flops | bytes accessed | tf_op | source)
XLA Modules:
  0.0 192.7 jit_solution(3363073217338642185)
XLA Ops:
  0.6 0.0 copy-start
  0.6 2.7 %shard_map.109 = bf16[32,16,1024]{2,1,0:T(8,128)(2,1)} custom-call(bf16[1024,256]{1,0:T(8,128)(2,1)} %tok_ref.3, bf16[1024,256]{1,0:T(8,128)(2,1)} %grad_ref.3, bf16[256,256]{1,0:T(8,128)(2,1)} %left_up_ref.3, bf16[256,256]{1,0:T(8,128)(2,1)} %right_down_ref.3), custom_call_target="tpu_custom_call" | custom-call | tf_op jit(solution)/shard_map/pallas_call | solution.py:180
  3.4 18.4 %all-to-all-start = ((bf16[32,16,1024]{2,1,0:T(8,128)(2,1)}), bf16[32,16,1024]{2,1,0:T(8,128)(2,1)S(1)}, u32[]{:S(2)}, u32[]{:S(2)}) async-start(bf16[32,16,1024]{2,1,0:T(8,128)(2,1)} %shard_map.109), calls=%async_computation | async-start | bytes 2097152 | tf_op jit(solution)/shard_map/all_to_all | solution.py:163
  21.7 0.0 copy-done
  21.7 0.2 copy.12
  21.9 0.2 copy.13
  22.2 49.0 %all-to-all-done.recv_ref = bf16[32,16,1024]{2,1,0:T(8,128)(2,1)S(1)} async-done(((bf16[32,16,1024]{2,1,0:T(8,128)(2,1)}), bf16[32,16,1024]{2,1,0:T(8,128)(2,1)S(1)}, u32[]{:S(2)}, u32[]{:S(2)}) %all-to-all-start) | async-done | bytes 1048608 | tf_op jit(solution)/shard_map/all_to_all | solution.py:163
  71.2 5.9 %shard_map.110 = (bf16[32,16,1024]{2,1,0:T(8,128)(2,1)}, bf16[1024,1024]{1,0:T(8,128)(2,1)}, bf16[1024,1024]{1,0:T(8,128)(2,1)}, bf16[256,1024]{1,0:T(8,128)(2,1)}, bf16[256,1024]{1,0:T(8,128)(2,1)}) custom-call(bf16[32,16,1024]{2,1,0:T(8,128)(2,1)S(1)} %all-to-all-done.recv_ref, bf16[256,1024]{1,0:T(8,128)(2,1)S(1)} %copy-done, ...), custom_call_target="tpu_custom_call" | custom-call | tf_op jit(solution)/shard_map/pallas_call | solution.py:190
  77.0 10.8 %all-to-all-start.1 = ((bf16[32,16,1024]{2,1,0:T(8,128)(2,1)}), bf16[32,16,1024]{2,1,0:T(8,128)(2,1)S(1)}, u32[]{:S(2)}, u32[]{:S(2)}) async-start(bf16[32,16,1024]{2,1,0:T(8,128)(2,1)} %get-tuple-element.32), calls=%async_computation.1 | async-start | bytes 2097152 | tf_op jit(solution)/shard_map/all_to_all | solution.py:163
  87.9 0.0 copy-start.2
  87.9 0.0 copy-start.3
  87.9 5.5 %shard_map.111 = (bf16[512,256]{1,0:T(8,128)(2,1)S(1)}, bf16[512,256]{1,0:T(8,128)(2,1)}, bf16[512,256]{1,0:T(8,128)(2,1)}, bf16[512,256]{1,0:T(8,128)(2,1)S(1)}) custom-call(s32[1]{0:T(128)} %bitcast.3.place_ref, bf16[1024,1024]{1,0:T(8,128)(2,1)} %get-tuple-element.33.hidden_hbm, bf16[1024,1024]{1,0:T(8,128)(2,1)} %get-tuple-element.34.back_pre_hbm, ...), custom_call_target="tpu_custom_call" | custom-call | tf_op jit(solution)/shard_map/pallas_call | solution.py:206
  93.4 3.5 %collective-permute-start = (bf16[512,256]{1,0:T(8,128)(2,1)}, bf16[512,256]{1,0:T(8,128)(2,1)S(1)}, u32[]{:S(2)}, u32[]{:S(2)}) collective-permute-start(bf16[512,256]{1,0:T(8,128)(2,1)} %get-tuple-element.38), channel_id=1, source_target_pairs={{0,32},{32,64},{64,96},{96,0},{128,160},{160,192},{192,224},{224,1... | collective-permute-start | bytes 786440 | tf_op jit(solution)/shard_map/ppermute | solution.py:149
  96.9 4.8 %collective-permute-start.1 = (bf16[512,256]{1,0:T(8,128)(2,1)}, bf16[512,256]{1,0:T(8,128)(2,1)S(1)}, u32[]{:S(2)}, u32[]{:S(2)}) collective-permute-start(bf16[512,256]{1,0:T(8,128)(2,1)} %get-tuple-element.39), channel_id=1, source_target_pairs={{0,64},{32,96},{64,0},{96,32},{128,192},{160,224},{192,128},{224,1... | collective-permute-start | bytes 786440 | tf_op jit(solution)/shard_map/ppermute | solution.py:149
  101.7 3.3 %collective-permute-start.2 = (bf16[512,256]{1,0:T(8,128)(2,1)S(1)}, bf16[512,256]{1,0:T(8,128)(2,1)S(1)}, u32[]{:S(2)}, u32[]{:S(2)}) collective-permute-start(bf16[512,256]{1,0:T(8,128)(2,1)S(1)} %get-tuple-element.40), channel_id=1, source_target_pairs={{0,96},{32,0},{64,32},{96,64},{128,224},{160,128},{192,160},{224,1... | collective-permute-start | bytes 786440 | tf_op jit(solution)/shard_map/ppermute | solution.py:149
  105.0 0.2 collective-permute-done.near_ref
  105.1 6.8 %collective-permute-done.1.far_ref = bf16[512,256]{1,0:T(8,128)(2,1)S(1)} collective-permute-done((bf16[512,256]{1,0:T(8,128)(2,1)}, bf16[512,256]{1,0:T(8,128)(2,1)S(1)}, u32[]{:S(2)}, u32[]{:S(2)}) %collective-permute-start.1) | collective-permute-done | bytes 262176 | tf_op jit(solution)/shard_map/ppermute | solution.py:149
  111.9 1.3 collective-permute-done.2.last_ref
  113.2 0.2 shard_map.112
  113.5 0.0 copy-start.4
  113.5 0.0 copy-start.5
  113.5 4.7 %collective-permute-start.3 = (bf16[128,256]{1,0:T(8,128)(2,1)S(1)}, bf16[128,256]{1,0:T(8,128)(2,1)S(1)}, u32[]{:S(2)}, u32[]{:S(2)}) collective-permute-start(bf16[128,256]{1,0:T(8,128)(2,1)S(1)} %get-tuple-element.42), channel_id=1, source_target_pairs={{0,256},{32,288},{64,320},{96,352},{128,384},{160,416},{192,448},{... | collective-permute-start | bytes 196616 | tf_op jit(solution)/shard_map/ppermute | solution.py:149
  118.2 2.0 %collective-permute-start.4 = (bf16[128,256]{1,0:T(8,128)(2,1)S(1)}, bf16[128,256]{1,0:T(8,128)(2,1)S(1)}, u32[]{:S(2)}, u32[]{:S(2)}) collective-permute-start(bf16[128,256]{1,0:T(8,128)(2,1)S(1)} %get-tuple-element.43), channel_id=1, source_target_pairs={{0,128},{32,160},{64,192},{96,224},{128,256},{160,288},{192,320},{... | collective-permute-start | bytes 196616 | tf_op jit(solution)/shard_map/ppermute | solution.py:149
  120.3 5.6 %collective-permute-start.5 = (bf16[128,256]{1,0:T(8,128)(2,1)S(1)}, bf16[128,256]{1,0:T(8,128)(2,1)S(1)}, u32[]{:S(2)}, u32[]{:S(2)}) collective-permute-start(bf16[128,256]{1,0:T(8,128)(2,1)S(1)} %get-tuple-element.44), channel_id=1, source_target_pairs={{0,384},{32,416},{64,448},{96,480},{128,0},{160,32},{192,64},{224,... | collective-permute-start | bytes 196616 | tf_op jit(solution)/shard_map/ppermute | solution.py:149
  125.9 2.7 %collective-permute-done.3 = bf16[128,256]{1,0:T(8,128)(2,1)S(1)} collective-permute-done((bf16[128,256]{1,0:T(8,128)(2,1)S(1)}, bf16[128,256]{1,0:T(8,128)(2,1)S(1)}, u32[]{:S(2)}, u32[]{:S(2)}) %collective-permute-start.3) | collective-permute-done | bytes 65568 | tf_op jit(solution)/shard_map/ppermute | solution.py:149
  128.6 11.7 %collective-permute-done.4 = bf16[128,256]{1,0:T(8,128)(2,1)S(1)} collective-permute-done((bf16[128,256]{1,0:T(8,128)(2,1)S(1)}, bf16[128,256]{1,0:T(8,128)(2,1)S(1)}, u32[]{:S(2)}, u32[]{:S(2)}) %collective-permute-start.4) | collective-permute-done | bytes 65568 | tf_op jit(solution)/shard_map/ppermute | solution.py:149
  140.3 1.1 collective-permute-done.5
  141.4 0.0 all-to-all-done.1.recv_ref
  141.5 1.2 shard_map.113
  142.7 8.9 %all-to-all-start.2 = ((bf16[16,32,256]{2,1,0:T(8,128)(2,1)}), bf16[16,32,256]{2,1,0:T(8,128)(2,1)S(1)}, u32[]{:S(2)}, u32[]{:S(2)}) async-start(bf16[16,32,256]{2,1,0:T(8,128)(2,1)} %bitcast.7), calls=%async_computation.2 | async-start | bytes 524288 | tf_op jit(solution)/shard_map/all_to_all | solution.py:163
  151.6 3.8 %collective-permute-start.6 = (bf16[128,256]{1,0:T(8,128)(2,1)S(1)}, bf16[128,256]{1,0:T(8,128)(2,1)S(1)}, u32[]{:S(2)}, u32[]{:S(2)}) collective-permute-start(bf16[128,256]{1,0:T(8,128)(2,1)S(1)} %add_convert_fusion.own_ref), channel_id=1, source_target_pairs={{0,128},{32,160},{64,192},{96,224},{128,256},{160,288},{192,320},{... | collective-permute-start | bytes 196616 | tf_op jit(solution)/shard_map/ppermute | solution.py:149
  155.4 4.3 %collective-permute-start.7 = (bf16[128,256]{1,0:T(8,128)(2,1)S(1)}, bf16[128,256]{1,0:T(8,128)(2,1)S(1)}, u32[]{:S(2)}, u32[]{:S(2)}) collective-permute-start(bf16[128,256]{1,0:T(8,128)(2,1)S(1)} %add_convert_fusion.own_ref), channel_id=1, source_target_pairs={{0,256},{32,288},{64,320},{96,352},{128,384},{160,416},{192,448},{... | collective-permute-start | bytes 196616 | tf_op jit(solution)/shard_map/ppermute | solution.py:149
  159.7 3.4 %collective-permute-start.8 = (bf16[128,256]{1,0:T(8,128)(2,1)S(1)}, bf16[128,256]{1,0:T(8,128)(2,1)S(1)}, u32[]{:S(2)}, u32[]{:S(2)}) collective-permute-start(bf16[128,256]{1,0:T(8,128)(2,1)S(1)} %add_convert_fusion.own_ref), channel_id=1, source_target_pairs={{0,384},{32,416},{64,448},{96,480},{128,0},{160,32},{192,64},{224,... | collective-permute-start | bytes 196616 | tf_op jit(solution)/shard_map/ppermute | solution.py:149
  163.1 0.0 collective-permute-done.6.near_ref
  163.1 1.1 collective-permute-done.7.far_ref
  164.2 1.7 collective-permute-done.8.last_ref
  165.8 0.0 all-to-all-done.2.late_ref
  165.8 0.8 shard_map.115
  166.6 7.0 %all-to-all-start.3 = ((bf16[16,32,256]{2,1,0:T(8,128)(2,1)}), bf16[16,32,256]{2,1,0:T(8,128)(2,1)S(1)}, u32[]{:S(2)}, u32[]{:S(2)}) async-start(bf16[16,32,256]{2,1,0:T(8,128)(2,1)} %get-tuple-element.52), calls=%async_computation.3 | async-start | bytes 524288 | tf_op jit(solution)/shard_map/all_to_all | solution.py:163
  173.7 5.3 %collective-permute-start.10 = (bf16[512,256]{1,0:T(8,128)(2,1)S(1)}, bf16[512,256]{1,0:T(8,128)(2,1)S(1)}, u32[]{:S(2)}, u32[]{:S(2)}) collective-permute-start(bf16[512,256]{1,0:T(8,128)(2,1)S(1)} %get-tuple-element.53.own_ref), channel_id=1, source_target_pairs={{0,64},{32,96},{64,0},{96,32},{128,192},{160,224},{192,128},{224,1... | collective-permute-start | bytes 786440 | tf_op jit(solution)/shard_map/ppermute | solution.py:149
  179.0 3.1 %collective-permute-start.11 = (bf16[512,256]{1,0:T(8,128)(2,1)S(1)}, bf16[512,256]{1,0:T(8,128)(2,1)S(1)}, u32[]{:S(2)}, u32[]{:S(2)}) collective-permute-start(bf16[512,256]{1,0:T(8,128)(2,1)S(1)} %get-tuple-element.53.own_ref), channel_id=1, source_target_pairs={{0,96},{32,0},{64,32},{96,64},{128,224},{160,128},{192,160},{224,1... | collective-permute-start | bytes 786440 | tf_op jit(solution)/shard_map/ppermute | solution.py:149
  182.1 2.8 %collective-permute-start.9 = (bf16[512,256]{1,0:T(8,128)(2,1)S(1)}, bf16[512,256]{1,0:T(8,128)(2,1)S(1)}, u32[]{:S(2)}, u32[]{:S(2)}) collective-permute-start(bf16[512,256]{1,0:T(8,128)(2,1)S(1)} %get-tuple-element.53.own_ref), channel_id=1, source_target_pairs={{0,32},{32,64},{64,96},{96,0},{128,160},{160,192},{192,224},{224,1... | collective-permute-start | bytes 786440 | tf_op jit(solution)/shard_map/ppermute | solution.py:149
  184.9 1.5 shard_map.114
  186.4 0.0 collective-permute-done.10.far_ref
  186.4 3.1 %collective-permute-done.11.last_ref = bf16[512,256]{1,0:T(8,128)(2,1)S(1)} collective-permute-done((bf16[512,256]{1,0:T(8,128)(2,1)S(1)}, bf16[512,256]{1,0:T(8,128)(2,1)S(1)}, u32[]{:S(2)}, u32[]{:S(2)}) %collective-permute-start.11) | collective-permute-done | bytes 262176 | tf_op jit(solution)/shard_map/ppermute | solution.py:149
  189.5 2.0 %collective-permute-done.9.near_ref = bf16[512,256]{1,0:T(8,128)(2,1)S(1)} collective-permute-done((bf16[512,256]{1,0:T(8,128)(2,1)S(1)}, bf16[512,256]{1,0:T(8,128)(2,1)S(1)}, u32[]{:S(2)}, u32[]{:S(2)}) %collective-permute-start.9) | collective-permute-done | bytes 262176 | tf_op jit(solution)/shard_map/ppermute | solution.py:149
  191.6 0.0 all-to-all-done.3.late_ref
  191.6 1.2 shard_map.116
  (7 shorter events, 0.0 us)
Async XLA Ops:
  0.6 21.1 %copy-start = (bf16[256,1024]{1,0:T(8,128)(2,1)S(1)}, bf16[256,1024]{1,0:T(8,128)(2,1)}, u32[]{:S(2)}) copy-start(bf16[256,1024]{1,0:T(8,128)(2,1)} %right_up_ref.1) | copy-start | bytes 1572868
  3.3 18.6 %copy-start.1 = (bf16[1024,256]{1,0:T(8,128)(2,1)S(1)}, bf16[1024,256]{1,0:T(8,128)(2,1)}, u32[]{:S(2)}) copy-start(bf16[1024,256]{1,0:T(8,128)(2,1)} %left_down_ref.1) | copy-start | bytes 1572868
  3.4 67.8 %all-to-all-start = ((bf16[32,16,1024]{2,1,0:T(8,128)(2,1)}), bf16[32,16,1024]{2,1,0:T(8,128)(2,1)S(1)}, u32[]{:S(2)}, u32[]{:S(2)}) async-start(bf16[32,16,1024]{2,1,0:T(8,128)(2,1)} %shard_map.109), calls=%async_computation | async-start | bytes 2097152 | tf_op jit(solution)/shard_map/all_to_all | solution.py:163
  77.0 64.4 %all-to-all-start.1 = ((bf16[32,16,1024]{2,1,0:T(8,128)(2,1)}), bf16[32,16,1024]{2,1,0:T(8,128)(2,1)S(1)}, u32[]{:S(2)}, u32[]{:S(2)}) async-start(bf16[32,16,1024]{2,1,0:T(8,128)(2,1)} %get-tuple-element.32), calls=%async_computation.1 | async-start | bytes 2097152 | tf_op jit(solution)/shard_map/all_to_all | solution.py:163
  87.9 53.6 %copy-start.2 = (bf16[1024,256]{1,0:T(8,128)(2,1)S(1)}, bf16[1024,256]{1,0:T(8,128)(2,1)}, u32[]{:S(2)}) copy-start(bf16[1024,256]{1,0:T(8,128)(2,1)} %tok_ref.3) | copy-start | bytes 1572868
  87.9 53.6 %copy-start.3 = (bf16[1024,256]{1,0:T(8,128)(2,1)S(1)}, bf16[1024,256]{1,0:T(8,128)(2,1)}, u32[]{:S(2)}) copy-start(bf16[1024,256]{1,0:T(8,128)(2,1)} %grad_ref.3) | copy-start | bytes 1572868
  93.4 11.7 %collective-permute-start = (bf16[512,256]{1,0:T(8,128)(2,1)}, bf16[512,256]{1,0:T(8,128)(2,1)S(1)}, u32[]{:S(2)}, u32[]{:S(2)}) collective-permute-start(bf16[512,256]{1,0:T(8,128)(2,1)} %get-tuple-element.38), channel_id=1, source_target_pairs={{0,32},{32,64},{64,96},{96,0},{128,160},{160,192},{192,224},{224,1... | collective-permute-start | bytes 786440 | tf_op jit(solution)/shard_map/ppermute | solution.py:149
  96.9 15.0 %collective-permute-start.1 = (bf16[512,256]{1,0:T(8,128)(2,1)}, bf16[512,256]{1,0:T(8,128)(2,1)S(1)}, u32[]{:S(2)}, u32[]{:S(2)}) collective-permute-start(bf16[512,256]{1,0:T(8,128)(2,1)} %get-tuple-element.39), channel_id=1, source_target_pairs={{0,64},{32,96},{64,0},{96,32},{128,192},{160,224},{192,128},{224,1... | collective-permute-start | bytes 786440 | tf_op jit(solution)/shard_map/ppermute | solution.py:149
  101.7 11.5 %collective-permute-start.2 = (bf16[512,256]{1,0:T(8,128)(2,1)S(1)}, bf16[512,256]{1,0:T(8,128)(2,1)S(1)}, u32[]{:S(2)}, u32[]{:S(2)}) collective-permute-start(bf16[512,256]{1,0:T(8,128)(2,1)S(1)} %get-tuple-element.40), channel_id=1, source_target_pairs={{0,96},{32,0},{64,32},{96,64},{128,224},{160,128},{192,160},{224,1... | collective-permute-start | bytes 786440 | tf_op jit(solution)/shard_map/ppermute | solution.py:149
  113.5 71.4 %copy-start.4 = (bf16[256,256]{1,0:T(8,128)(2,1)S(1)}, bf16[256,256]{1,0:T(8,128)(2,1)}, u32[]{:S(2)}) copy-start(bf16[256,256]{1,0:T(8,128)(2,1)} %left_up_ref.3) | copy-start | bytes 393220
  113.5 71.4 %copy-start.5 = (bf16[256,256]{1,0:T(8,128)(2,1)S(1)}, bf16[256,256]{1,0:T(8,128)(2,1)}, u32[]{:S(2)}) copy-start(bf16[256,256]{1,0:T(8,128)(2,1)} %right_down_ref.3) | copy-start | bytes 393220
  113.5 15.1 %collective-permute-start.3 = (bf16[128,256]{1,0:T(8,128)(2,1)S(1)}, bf16[128,256]{1,0:T(8,128)(2,1)S(1)}, u32[]{:S(2)}, u32[]{:S(2)}) collective-permute-start(bf16[128,256]{1,0:T(8,128)(2,1)S(1)} %get-tuple-element.42), channel_id=1, source_target_pairs={{0,256},{32,288},{64,320},{96,352},{128,384},{160,416},{192,448},{... | collective-permute-start | bytes 196616 | tf_op jit(solution)/shard_map/ppermute | solution.py:149
  118.2 22.0 %collective-permute-start.4 = (bf16[128,256]{1,0:T(8,128)(2,1)S(1)}, bf16[128,256]{1,0:T(8,128)(2,1)S(1)}, u32[]{:S(2)}, u32[]{:S(2)}) collective-permute-start(bf16[128,256]{1,0:T(8,128)(2,1)S(1)} %get-tuple-element.43), channel_id=1, source_target_pairs={{0,128},{32,160},{64,192},{96,224},{128,256},{160,288},{192,320},{... | collective-permute-start | bytes 196616 | tf_op jit(solution)/shard_map/ppermute | solution.py:149
  120.3 21.1 %collective-permute-start.5 = (bf16[128,256]{1,0:T(8,128)(2,1)S(1)}, bf16[128,256]{1,0:T(8,128)(2,1)S(1)}, u32[]{:S(2)}, u32[]{:S(2)}) collective-permute-start(bf16[128,256]{1,0:T(8,128)(2,1)S(1)} %get-tuple-element.44), channel_id=1, source_target_pairs={{0,384},{32,416},{64,448},{96,480},{128,0},{160,32},{192,64},{224,... | collective-permute-start | bytes 196616 | tf_op jit(solution)/shard_map/ppermute | solution.py:149
  142.7 23.1 %all-to-all-start.2 = ((bf16[16,32,256]{2,1,0:T(8,128)(2,1)}), bf16[16,32,256]{2,1,0:T(8,128)(2,1)S(1)}, u32[]{:S(2)}, u32[]{:S(2)}) async-start(bf16[16,32,256]{2,1,0:T(8,128)(2,1)} %bitcast.7), calls=%async_computation.2 | async-start | bytes 524288 | tf_op jit(solution)/shard_map/all_to_all | solution.py:163
  151.6 11.5 %collective-permute-start.6 = (bf16[128,256]{1,0:T(8,128)(2,1)S(1)}, bf16[128,256]{1,0:T(8,128)(2,1)S(1)}, u32[]{:S(2)}, u32[]{:S(2)}) collective-permute-start(bf16[128,256]{1,0:T(8,128)(2,1)S(1)} %add_convert_fusion.own_ref), channel_id=1, source_target_pairs={{0,128},{32,160},{64,192},{96,224},{128,256},{160,288},{192,320},{... | collective-permute-start | bytes 196616 | tf_op jit(solution)/shard_map/ppermute | solution.py:149
  155.4 8.8 %collective-permute-start.7 = (bf16[128,256]{1,0:T(8,128)(2,1)S(1)}, bf16[128,256]{1,0:T(8,128)(2,1)S(1)}, u32[]{:S(2)}, u32[]{:S(2)}) collective-permute-start(bf16[128,256]{1,0:T(8,128)(2,1)S(1)} %add_convert_fusion.own_ref), channel_id=1, source_target_pairs={{0,256},{32,288},{64,320},{96,352},{128,384},{160,416},{192,448},{... | collective-permute-start | bytes 196616 | tf_op jit(solution)/shard_map/ppermute | solution.py:149
  159.7 6.2 %collective-permute-start.8 = (bf16[128,256]{1,0:T(8,128)(2,1)S(1)}, bf16[128,256]{1,0:T(8,128)(2,1)S(1)}, u32[]{:S(2)}, u32[]{:S(2)}) collective-permute-start(bf16[128,256]{1,0:T(8,128)(2,1)S(1)} %add_convert_fusion.own_ref), channel_id=1, source_target_pairs={{0,384},{32,416},{64,448},{96,480},{128,0},{160,32},{192,64},{224,... | collective-permute-start | bytes 196616 | tf_op jit(solution)/shard_map/ppermute | solution.py:149
  166.6 24.9 %all-to-all-start.3 = ((bf16[16,32,256]{2,1,0:T(8,128)(2,1)}), bf16[16,32,256]{2,1,0:T(8,128)(2,1)S(1)}, u32[]{:S(2)}, u32[]{:S(2)}) async-start(bf16[16,32,256]{2,1,0:T(8,128)(2,1)} %get-tuple-element.52), calls=%async_computation.3 | async-start | bytes 524288 | tf_op jit(solution)/shard_map/all_to_all | solution.py:163
  173.7 12.7 %collective-permute-start.10 = (bf16[512,256]{1,0:T(8,128)(2,1)S(1)}, bf16[512,256]{1,0:T(8,128)(2,1)S(1)}, u32[]{:S(2)}, u32[]{:S(2)}) collective-permute-start(bf16[512,256]{1,0:T(8,128)(2,1)S(1)} %get-tuple-element.53.own_ref), channel_id=1, source_target_pairs={{0,64},{32,96},{64,0},{96,32},{128,192},{160,224},{192,128},{224,1... | collective-permute-start | bytes 786440 | tf_op jit(solution)/shard_map/ppermute | solution.py:149
  179.0 10.5 %collective-permute-start.11 = (bf16[512,256]{1,0:T(8,128)(2,1)S(1)}, bf16[512,256]{1,0:T(8,128)(2,1)S(1)}, u32[]{:S(2)}, u32[]{:S(2)}) collective-permute-start(bf16[512,256]{1,0:T(8,128)(2,1)S(1)} %get-tuple-element.53.own_ref), channel_id=1, source_target_pairs={{0,96},{32,0},{64,32},{96,64},{128,224},{160,128},{192,160},{224,1... | collective-permute-start | bytes 786440 | tf_op jit(solution)/shard_map/ppermute | solution.py:149
  182.1 9.5 %collective-permute-start.9 = (bf16[512,256]{1,0:T(8,128)(2,1)S(1)}, bf16[512,256]{1,0:T(8,128)(2,1)S(1)}, u32[]{:S(2)}, u32[]{:S(2)}) collective-permute-start(bf16[512,256]{1,0:T(8,128)(2,1)S(1)} %get-tuple-element.53.own_ref), channel_id=1, source_target_pairs={{0,32},{32,64},{64,96},{96,0},{128,160},{160,192},{192,224},{224,1... | collective-permute-start | bytes 786440 | tf_op jit(solution)/shard_map/ppermute | solution.py:149

commit v7 on v6

--- a/solution.py
+++ b/solution.py
@@ -48,10 +48,9 @@
     pre = dot(right_up_t_ref[...], mixed)
     back_hidden = dot(left_down_ref[...], back_third)
     square = pre * pre
-    tanh = jnp.tanh(GELU_C * (pre + GELU_A * (pre * square)))
-    cdf = 0.5 * (1.0 + tanh)
-    hidden = (pre * cdf).astype(BF16)
-    slope = cdf + (0.5 * pre) * (1.0 - tanh * tanh) * (GELU_C * (1.0 + (3.0 * GELU_A) * square))
+    half = 0.5 + 0.5 * jnp.tanh(pre * (GELU_C + (GELU_C * GELU_A) * square))
+    hidden = (pre * half).astype(BF16)
+    slope = half + (half - half * half) * (pre * (2.0 * GELU_C + (6.0 * GELU_C * GELU_A) * square))
     back_pre = (back_hidden * slope).astype(BF16)
     hidden_ref[...] = hidden
     back_pre_ref[...] = back_pre
@@ -84,12 +83,11 @@
         out_ref[256:] = dot(mixed_ref[...], back_pre_ref[step], NT).astype(BF16)
 
 
-def fold_kernel(place_ref, own_ref, near_ref, far_ref, last_ref, *rest):
-    total_ref = rest[-1]
+def fold_kernel(place_ref, own_ref, near_ref, far_ref, last_ref, keep_ref, give_ref, total_ref):
     total_ref[...] = four_sum(own_ref[...], near_ref[...], far_ref[...], last_ref[...])
-    for step, out_ref in enumerate(rest[:-1]):
-        start = pl.multiple_of(((place_ref[0] + step) & 3) * 128, 128)
-        out_ref[...] = total_ref[pl.ds(start, 128), :]
+    parity = place_ref[0] & 1
+    keep_ref[...] = total_ref[pl.ds(pl.multiple_of(parity * 256, 256), 256), :]
+    give_ref[...] = total_ref[pl.ds(pl.multiple_of((1 - parity) * 256, 256), 256), :]
 
 
 def exit_grads_kernel(recv_ref, tok_ref, grad_ref, out_ref, mixed_ref, back_first_ref):
@@ -106,12 +104,12 @@
     in_grad_ref[...] = dot(back_first_ref[...], left_up_t, TN).astype(BF16)
 
 
-def spread_kernel(place_ref, late_ref, own_ref, near_ref, far_ref, last_ref, late_out_ref, early_out_ref):
+def spread_kernel(place_ref, late_ref, own_ref, other_ref, late_out_ref, early_out_ref):
     late = jnp.sum(late_ref[...].astype(F32), axis=0).astype(BF16)
     late_out_ref[...] = jnp.broadcast_to(late[None], late_out_ref.shape)
-    for step, ref in enumerate((own_ref, near_ref, far_ref, last_ref)):
-        start = pl.multiple_of(((place_ref[0] + 4 - step) & 3) * 128, 128)
-        early_out_ref[pl.ds(start, 128), :] = ref[...]
+    parity = place_ref[0] & 1
+    early_out_ref[pl.ds(pl.multiple_of(parity * 256, 256), 256), :] = own_ref[...]
+    early_out_ref[pl.ds(pl.multiple_of((1 - parity) * 256, 256), 256), :] = other_ref[...]
 
 
 def unpack_kernel(place_ref, late_ref, own_ref, near_ref, far_ref, last_ref,
@@ -136,27 +134,28 @@
     return pltpu.with_memory_space_constraint(array, pltpu.HBM)
 
 
-def shift_pairs(inner, step):
-    pairs = []
-    for z_lo in range(4):
-        for y in range(4):
-            to = (z_lo * 4 + (y + step) % 4) if inner else (((z_lo + step) % 4) * 4 + y)
-            pairs.append((z_lo * 4 + y, to))
-    return pairs
-
-
-def permute(array, inner, step):
-    return lax.ppermute(array, "dp", shift_pairs(inner, step))
+def along_y(array, step):
+    pairs = [(z_lo * 4 + y, z_lo * 4 + (y + step) % 4) for z_lo in range(4) for y in range(4)]
+    return lax.ppermute(array, "dp", pairs)
+
+
+def swap_z(array, bit):
+    pairs = [(z_lo * 4 + y, (z_lo ^ bit) * 4 + y) for z_lo in range(4) for y in range(4)]
+    return lax.ppermute(array, "dp", pairs)
+
+
+def two_sum(own, other):
+    return (own.astype(F32) + other.astype(F32)).astype(BF16)
 
 
 def four_sum(own, near, far, last):
     return ((own.astype(F32) + far.astype(F32)) + (near.astype(F32) + last.astype(F32))).astype(BF16)
 
 
-def send_on(chunks, inner):
-    far = permute(chunks[2], inner, 2)
-    near = permute(chunks[1], inner, 1)
-    return [chunks[0], near, far, permute(chunks[3], inner, 3)]
+def send_on(chunks):
+    far = along_y(chunks[2], 2)
+    near = along_y(chunks[1], 1)
+    return [chunks[0], near, far, along_y(chunks[3], 3)]
 
 
 def exchange(parts, axis):
@@ -213,30 +212,29 @@
         compiler_params=PARAMS,
     )(y_place, in_hbm(hidden), in_hbm(back_pre), in_hbm(mixed_up), in_hbm(back_third))
 
-    parts = pl.pallas_call(
+    keep, give = pl.pallas_call(
         fold_kernel,
         in_specs=[smem] + [vmem] * 4,
-        out_shape=[plain((128, 256))] * 4,
+        out_shape=[plain((256, 256))] * 2,
         scratch_shapes=[pltpu.VMEM((512, 256), BF16)],
         compiler_params=PARAMS,
-    )(z_place, *send_on(parts, True))
-    pieces = send_on(parts, False)
-    part = four_sum(*pieces)
+    )(z_place, *send_on(parts))
+    part = two_sum(keep, swap_z(give, 1))
+    part = two_sum(part, swap_z(part, 2))
     recv, part = lax.optimization_barrier((recv, part))
     late, mixed_down, back_first = whole_call(
         exit_grads_kernel, [hbm((512, 256)), plain((256, tok)), plain((256, tok))],
         recv, tokens_in, out_grad)
 
     late = exchange(late.reshape(16, 32, 256), "dp")
-    pieces = send_on([part] * 4, False)
     late, part = pl.pallas_call(
         spread_kernel,
-        in_specs=[smem] + [vmem] * 5,
+        in_specs=[smem] + [vmem] * 3,
         out_shape=[hbm((16, 32, 256)), plain((512, 256))],
         compiler_params=PARAMS,
-    )(z_place, late, *pieces)
+    )(z_place, late, part, swap_z(part, 1))
     late = exchange(late, "dp")
-    pieces = send_on([part] * 4, True)
+    pieces = send_on([part] * 4)
     layer_out, input_grad = whole_call(
         exit_kernel, [hbm((tok, 256)), hbm((tok, 256))], mixed_down, back_first, left_up, right_down)
     grads = pl.pallas_call(

time: 195 us -> 194 us (level)
  starting transfers between devices: 91.6 us -> 71.9 us
  waiting for transfers between devices: 80.8 us -> 100 us
    ppermute x12 -> x9, waiting for transfers between devices: 31.7 us -> 48.9 us  [the longest x3 35.2 us: swap_z(): return lax.ppermute(array, 'dp', pairs)]
    ppermute x12 -> x9, starting transfers between devices: 46.5 us -> 33.8 us  [the longest x6 23.4 us: along_y(): return lax.ppermute(array, 'dp', pairs)]
    all_to_all x4, starting transfers between devices: 45.1 us -> 38.1 us  [exchange(): return lax.all_to_all(parts, axis, 0, 0, tiled=True)]
    all_to_all x4, waiting for transfers between devices: 49 us -> 51.4 us  [exchange(): return lax.all_to_all(parts, axis, 0, 0, tiled=True)]
  transfers between devices with their start and end apart: 16 -> 13, of which waited for: 11 -> 10; matrix products, arithmetic and copies ran while one was open for 0% -> 0% of each run, Pallas kernels for 4% -> 4%
where the time goes in v7:
time: 194 us; the launch traced here: 192 us
  waiting for transfers between devices  100 us (52%)
  starting transfers between devices  71.9 us (37%)
  Pallas kernels  18.3 us (9%)
    all_to_all x4, waiting for transfers between devices, exchange(): return lax.all_to_all(parts, axis, 0, 0, tiled=True)  51.4 us
    all_to_all x4, starting transfers between devices, exchange(): return lax.all_to_all(parts, axis, 0, 0, tiled=True)  38.1 us
    ppermute x3, waiting for transfers between devices, swap_z(): return lax.ppermute(array, 'dp', pairs)  35.2 us
    ppermute x6, starting transfers between devices, along_y(): return lax.ppermute(array, 'dp', pairs)  23.4 us
    ppermute x6, waiting for transfers between devices, along_y(): return lax.ppermute(array, 'dp', pairs)  13.7 us
    ppermute x3, starting transfers between devices, swap_z(): return lax.ppermute(array, 'dp', pairs)  10.5 us
    pallas_call x1, Pallas kernels, on_device(): pl.pallas_call(middle_grads_kernel, in_specs=[smem] + [far_away] * 4, out...  5.42 us
    pallas_call x1, Pallas kernels, on_device(): pl.pallas_call(middle_kernel, grid=(tok // tile,), in_specs=[woven(tile),...  5.31 us
  transfers between devices with their start and end apart: 13, of which 10 were waited for; matrix products, arithmetic and copies ran while one was open for 0% of the time, Pallas kernels for 4%

profile of v7, /device:TPU:6, one launch (start us, length us, event | category | flops | bytes accessed | tf_op | source)
XLA Modules:
  0.0 192.0 jit_solution(14968918610971696759)
XLA Ops:
  0.6 0.0 copy-start
  0.6 2.7 %shard_map.109 = bf16[32,16,1024]{2,1,0:T(8,128)(2,1)} custom-call(bf16[1024,256]{1,0:T(8,128)(2,1)} %tok_ref.3, bf16[1024,256]{1,0:T(8,128)(2,1)} %grad_ref.3, bf16[256,256]{1,0:T(8,128)(2,1)} %left_up_ref.3, bf16[256,256]{1,0:T(8,128)(2,1)} %right_down_ref.3), custom_call_target="tpu_custom_call" | custom-call | tf_op jit(solution)/shard_map/pallas_call | solution.py:179
  3.3 0.0 copy-start.1
  3.3 18.4 %all-to-all-start = ((bf16[32,16,1024]{2,1,0:T(8,128)(2,1)}), bf16[32,16,1024]{2,1,0:T(8,128)(2,1)S(1)}, u32[]{:S(2)}, u32[]{:S(2)}) async-start(bf16[32,16,1024]{2,1,0:T(8,128)(2,1)} %shard_map.109), calls=%async_computation | async-start | bytes 2097152 | tf_op jit(solution)/shard_map/all_to_all | solution.py:162
  21.7 0.0 copy-done
  21.7 0.2 copy.12
  21.9 0.0 copy-done.1
  21.9 0.2 copy.13
  22.1 49.0 %all-to-all-done.recv_ref = bf16[32,16,1024]{2,1,0:T(8,128)(2,1)S(1)} async-done(((bf16[32,16,1024]{2,1,0:T(8,128)(2,1)}), bf16[32,16,1024]{2,1,0:T(8,128)(2,1)S(1)}, u32[]{:S(2)}, u32[]{:S(2)}) %all-to-all-start) | async-done | bytes 1048608 | tf_op jit(solution)/shard_map/all_to_all | solution.py:162
  71.2 5.3 %shard_map.110 = (bf16[32,16,1024]{2,1,0:T(8,128)(2,1)}, bf16[1024,1024]{1,0:T(8,128)(2,1)}, bf16[1024,1024]{1,0:T(8,128)(2,1)}, bf16[256,1024]{1,0:T(8,128)(2,1)}, bf16[256,1024]{1,0:T(8,128)(2,1)}) custom-call(bf16[32,16,1024]{2,1,0:T(8,128)(2,1)S(1)} %all-to-all-done.recv_ref, bf16[256,1024]{1,0:T(8,128)(2,1)S(1)} %copy-done, ...), custom_call_target="tpu_custom_call" | custom-call | tf_op jit(solution)/shard_map/pallas_call | solution.py:189
  76.5 10.8 %all-to-all-start.1 = ((bf16[32,16,1024]{2,1,0:T(8,128)(2,1)}), bf16[32,16,1024]{2,1,0:T(8,128)(2,1)S(1)}, u32[]{:S(2)}, u32[]{:S(2)}) async-start(bf16[32,16,1024]{2,1,0:T(8,128)(2,1)} %get-tuple-element.30), calls=%async_computation.1 | async-start | bytes 2097152 | tf_op jit(solution)/shard_map/all_to_all | solution.py:162
  87.3 5.4 %shard_map.111 = (bf16[512,256]{1,0:T(8,128)(2,1)S(1)}, bf16[512,256]{1,0:T(8,128)(2,1)}, bf16[512,256]{1,0:T(8,128)(2,1)}, bf16[512,256]{1,0:T(8,128)(2,1)S(1)}) custom-call(s32[1]{0:T(128)} %bitcast.3.place_ref, bf16[1024,1024]{1,0:T(8,128)(2,1)} %get-tuple-element.31.hidden_hbm, bf16[1024,1024]{1,0:T(8,128)(2,1)} %get-tuple-element.32.back_pre_hbm, ...), custom_call_target="tpu_custom_call" | custom-call | tf_op jit(solution)/shard_map/pallas_call | solution.py:205
  92.7 0.0 copy-start.2
  92.7 0.0 copy-start.3
  92.8 3.6 %collective-permute-start = (bf16[512,256]{1,0:T(8,128)(2,1)}, bf16[512,256]{1,0:T(8,128)(2,1)S(1)}, u32[]{:S(2)}, u32[]{:S(2)}) collective-permute-start(bf16[512,256]{1,0:T(8,128)(2,1)} %get-tuple-element.36), channel_id=1, source_target_pairs={{0,32},{32,64},{64,96},{96,0},{128,160},{160,192},{192,224},{224,1... | collective-permute-start | bytes 786440 | tf_op jit(solution)/shard_map/ppermute | solution.py:139
  96.4 4.8 %collective-permute-start.1 = (bf16[512,256]{1,0:T(8,128)(2,1)}, bf16[512,256]{1,0:T(8,128)(2,1)S(1)}, u32[]{:S(2)}, u32[]{:S(2)}) collective-permute-start(bf16[512,256]{1,0:T(8,128)(2,1)} %get-tuple-element.37), channel_id=1, source_target_pairs={{0,64},{32,96},{64,0},{96,32},{128,192},{160,224},{192,128},{224,1... | collective-permute-start | bytes 786440 | tf_op jit(solution)/shard_map/ppermute | solution.py:139
  101.2 3.3 %collective-permute-start.2 = (bf16[512,256]{1,0:T(8,128)(2,1)S(1)}, bf16[512,256]{1,0:T(8,128)(2,1)S(1)}, u32[]{:S(2)}, u32[]{:S(2)}) collective-permute-start(bf16[512,256]{1,0:T(8,128)(2,1)S(1)} %get-tuple-element.38), channel_id=1, source_target_pairs={{0,96},{32,0},{64,32},{96,64},{128,224},{160,128},{192,160},{224,1... | collective-permute-start | bytes 786440 | tf_op jit(solution)/shard_map/ppermute | solution.py:139
  104.4 0.2 collective-permute-done.near_ref
  104.6 6.8 %collective-permute-done.1.far_ref = bf16[512,256]{1,0:T(8,128)(2,1)S(1)} collective-permute-done((bf16[512,256]{1,0:T(8,128)(2,1)}, bf16[512,256]{1,0:T(8,128)(2,1)S(1)}, u32[]{:S(2)}, u32[]{:S(2)}) %collective-permute-start.1) | collective-permute-done | bytes 262176 | tf_op jit(solution)/shard_map/ppermute | solution.py:139
  111.4 1.3 collective-permute-done.2.last_ref
  112.7 0.2 shard_map.112
  113.0 3.5 %collective-permute-start.3 = (bf16[256,256]{1,0:T(8,128)(2,1)S(1)}, bf16[256,256]{1,0:T(8,128)(2,1)S(1)}, u32[]{:S(2)}, u32[]{:S(2)}) collective-permute-start(bf16[256,256]{1,0:T(8,128)(2,1)S(1)} %get-tuple-element.40), channel_id=1, source_target_pairs={{0,128},{32,160},{64,192},{96,224},{128,0},{160,32},{192,64},{224,... | collective-permute-start | bytes 393224 | tf_op jit(solution)/shard_map/ppermute | solution.py:144
  116.5 21.8 %collective-permute-done.3 = bf16[256,256]{1,0:T(8,128)(2,1)S(1)} collective-permute-done((bf16[256,256]{1,0:T(8,128)(2,1)S(1)}, bf16[256,256]{1,0:T(8,128)(2,1)S(1)}, u32[]{:S(2)}, u32[]{:S(2)}) %collective-permute-start.3) | collective-permute-done | bytes 131104 | tf_op jit(solution)/shard_map/ppermute | solution.py:144
  138.3 0.0 copy-start.4
  138.4 0.0 copy-start.5
  138.4 3.1 %collective-permute-start.4 = (bf16[256,256]{1,0:T(8,128)(2,1)S(1)}, bf16[256,256]{1,0:T(8,128)(2,1)S(1)}, u32[]{:S(2)}, u32[]{:S(2)}) collective-permute-start(bf16[256,256]{1,0:T(8,128)(2,1)S(1)} %add_convert_fusion.1), channel_id=1, source_target_pairs={{0,256},{32,288},{64,320},{96,352},{128,384},{160,416},{192,448},{... | collective-permute-start | bytes 393224 | tf_op jit(solution)/shard_map/ppermute | solution.py:144
  141.5 7.5 %collective-permute-done.4 = bf16[256,256]{1,0:T(8,128)(2,1)S(1)} collective-permute-done((bf16[256,256]{1,0:T(8,128)(2,1)S(1)}, bf16[256,256]{1,0:T(8,128)(2,1)S(1)}, u32[]{:S(2)}, u32[]{:S(2)}) %collective-permute-start.4) | collective-permute-done | bytes 131104 | tf_op jit(solution)/shard_map/ppermute | solution.py:144
  149.1 0.0 all-to-all-done.1.recv_ref
  149.1 0.0 copy-done.2
  149.1 0.0 copy-done.3
  149.1 1.2 shard_map.113
  150.4 5.4 %all-to-all-start.2 = ((bf16[16,32,256]{2,1,0:T(8,128)(2,1)}), bf16[16,32,256]{2,1,0:T(8,128)(2,1)S(1)}, u32[]{:S(2)}, u32[]{:S(2)}) async-start(bf16[16,32,256]{2,1,0:T(8,128)(2,1)} %bitcast.7), calls=%async_computation.2 | async-start | bytes 524288 | tf_op jit(solution)/shard_map/all_to_all | solution.py:162
  155.8 3.8 %collective-permute-start.5 = (bf16[256,256]{1,0:T(8,128)(2,1)S(1)}, bf16[256,256]{1,0:T(8,128)(2,1)S(1)}, u32[]{:S(2)}, u32[]{:S(2)}) collective-permute-start(bf16[256,256]{1,0:T(8,128)(2,1)S(1)} %add_convert_fusion.own_ref), channel_id=1, source_target_pairs={{0,128},{32,160},{64,192},{96,224},{128,0},{160,32},{192,64},{224,... | collective-permute-start | bytes 393224 | tf_op jit(solution)/shard_map/ppermute | solution.py:144
  159.6 5.8 %collective-permute-done.5.other_ref = bf16[256,256]{1,0:T(8,128)(2,1)S(1)} collective-permute-done((bf16[256,256]{1,0:T(8,128)(2,1)S(1)}, bf16[256,256]{1,0:T(8,128)(2,1)S(1)}, u32[]{:S(2)}, u32[]{:S(2)}) %collective-permute-start.5) | collective-permute-done | bytes 131104 | tf_op jit(solution)/shard_map/ppermute | solution.py:144
  165.4 2.4 %all-to-all-done.2.late_ref = bf16[16,32,256]{2,1,0:T(8,128)(2,1)S(1)} async-done(((bf16[16,32,256]{2,1,0:T(8,128)(2,1)}), bf16[16,32,256]{2,1,0:T(8,128)(2,1)S(1)}, u32[]{:S(2)}, u32[]{:S(2)}) %all-to-all-start.2) | async-done | bytes 262176 | tf_op jit(solution)/shard_map/all_to_all | solution.py:162
  167.8 0.8 shard_map.115
  168.6 3.5 %all-to-all-start.3 = ((bf16[16,32,256]{2,1,0:T(8,128)(2,1)}), bf16[16,32,256]{2,1,0:T(8,128)(2,1)S(1)}, u32[]{:S(2)}, u32[]{:S(2)}) async-start(bf16[16,32,256]{2,1,0:T(8,128)(2,1)} %get-tuple-element.48), calls=%async_computation.3 | async-start | bytes 524288 | tf_op jit(solution)/shard_map/all_to_all | solution.py:162
  172.1 3.7 %collective-permute-start.6 = (bf16[512,256]{1,0:T(8,128)(2,1)S(1)}, bf16[512,256]{1,0:T(8,128)(2,1)S(1)}, u32[]{:S(2)}, u32[]{:S(2)}) collective-permute-start(bf16[512,256]{1,0:T(8,128)(2,1)S(1)} %get-tuple-element.49.own_ref), channel_id=1, source_target_pairs={{0,32},{32,64},{64,96},{96,0},{128,160},{160,192},{192,224},{224,1... | collective-permute-start | bytes 786440 | tf_op jit(solution)/shard_map/ppermute | solution.py:139
  175.8 4.6 %collective-permute-start.7 = (bf16[512,256]{1,0:T(8,128)(2,1)S(1)}, bf16[512,256]{1,0:T(8,128)(2,1)S(1)}, u32[]{:S(2)}, u32[]{:S(2)}) collective-permute-start(bf16[512,256]{1,0:T(8,128)(2,1)S(1)} %get-tuple-element.49.own_ref), channel_id=1, source_target_pairs={{0,64},{32,96},{64,0},{96,32},{128,192},{160,224},{192,128},{224,1... | collective-permute-start | bytes 786440 | tf_op jit(solution)/shard_map/ppermute | solution.py:139
  180.4 3.4 %collective-permute-start.8 = (bf16[512,256]{1,0:T(8,128)(2,1)S(1)}, bf16[512,256]{1,0:T(8,128)(2,1)S(1)}, u32[]{:S(2)}, u32[]{:S(2)}) collective-permute-start(bf16[512,256]{1,0:T(8,128)(2,1)S(1)} %get-tuple-element.49.own_ref), channel_id=1, source_target_pairs={{0,96},{32,0},{64,32},{96,64},{128,224},{160,128},{192,160},{224,1... | collective-permute-start | bytes 786440 | tf_op jit(solution)/shard_map/ppermute | solution.py:139
  183.8 0.0 copy-done.4
  183.8 0.0 copy-done.5
  183.8 1.5 shard_map.114
  185.3 0.0 collective-permute-done.6.near_ref
  185.3 5.1 %collective-permute-done.7.far_ref = bf16[512,256]{1,0:T(8,128)(2,1)S(1)} collective-permute-done((bf16[512,256]{1,0:T(8,128)(2,1)S(1)}, bf16[512,256]{1,0:T(8,128)(2,1)S(1)}, u32[]{:S(2)}, u32[]{:S(2)}) %collective-permute-start.7) | collective-permute-done | bytes 262176 | tf_op jit(solution)/shard_map/ppermute | solution.py:139
  190.5 0.3 collective-permute-done.8.last_ref
  190.8 0.0 all-to-all-done.3.late_ref
  190.8 1.2 shard_map.116
  (2 shorter events, 0.1 us)
Async XLA Ops:
  0.6 21.1 %copy-start = (bf16[256,1024]{1,0:T(8,128)(2,1)S(1)}, bf16[256,1024]{1,0:T(8,128)(2,1)}, u32[]{:S(2)}) copy-start(bf16[256,1024]{1,0:T(8,128)(2,1)} %right_up_ref.1) | copy-start | bytes 1572868
  3.3 18.6 %copy-start.1 = (bf16[1024,256]{1,0:T(8,128)(2,1)S(1)}, bf16[1024,256]{1,0:T(8,128)(2,1)}, u32[]{:S(2)}) copy-start(bf16[1024,256]{1,0:T(8,128)(2,1)} %left_down_ref.1) | copy-start | bytes 1572868
  3.3 67.8 %all-to-all-start = ((bf16[32,16,1024]{2,1,0:T(8,128)(2,1)}), bf16[32,16,1024]{2,1,0:T(8,128)(2,1)S(1)}, u32[]{:S(2)}, u32[]{:S(2)}) async-start(bf16[32,16,1024]{2,1,0:T(8,128)(2,1)} %shard_map.109), calls=%async_computation | async-start | bytes 2097152 | tf_op jit(solution)/shard_map/all_to_all | solution.py:162
  76.5 72.6 %all-to-all-start.1 = ((bf16[32,16,1024]{2,1,0:T(8,128)(2,1)}), bf16[32,16,1024]{2,1,0:T(8,128)(2,1)S(1)}, u32[]{:S(2)}, u32[]{:S(2)}) async-start(bf16[32,16,1024]{2,1,0:T(8,128)(2,1)} %get-tuple-element.30), calls=%async_computation.1 | async-start | bytes 2097152 | tf_op jit(solution)/shard_map/all_to_all | solution.py:162
  92.7 56.4 %copy-start.2 = (bf16[1024,256]{1,0:T(8,128)(2,1)S(1)}, bf16[1024,256]{1,0:T(8,128)(2,1)}, u32[]{:S(2)}) copy-start(bf16[1024,256]{1,0:T(8,128)(2,1)} %tok_ref.3) | copy-start | bytes 1572868
  92.7 56.4 %copy-start.3 = (bf16[1024,256]{1,0:T(8,128)(2,1)S(1)}, bf16[1024,256]{1,0:T(8,128)(2,1)}, u32[]{:S(2)}) copy-start(bf16[1024,256]{1,0:T(8,128)(2,1)} %grad_ref.3) | copy-start | bytes 1572868
  92.8 11.9 %collective-permute-start = (bf16[512,256]{1,0:T(8,128)(2,1)}, bf16[512,256]{1,0:T(8,128)(2,1)S(1)}, u32[]{:S(2)}, u32[]{:S(2)}) collective-permute-start(bf16[512,256]{1,0:T(8,128)(2,1)} %get-tuple-element.36), channel_id=1, source_target_pairs={{0,32},{32,64},{64,96},{96,0},{128,160},{160,192},{192,224},{224,1... | collective-permute-start | bytes 786440 | tf_op jit(solution)/shard_map/ppermute | solution.py:139
  96.4 15.0 %collective-permute-start.1 = (bf16[512,256]{1,0:T(8,128)(2,1)}, bf16[512,256]{1,0:T(8,128)(2,1)S(1)}, u32[]{:S(2)}, u32[]{:S(2)}) collective-permute-start(bf16[512,256]{1,0:T(8,128)(2,1)} %get-tuple-element.37), channel_id=1, source_target_pairs={{0,64},{32,96},{64,0},{96,32},{128,192},{160,224},{192,128},{224,1... | collective-permute-start | bytes 786440 | tf_op jit(solution)/shard_map/ppermute | solution.py:139
  101.2 11.5 %collective-permute-start.2 = (bf16[512,256]{1,0:T(8,128)(2,1)S(1)}, bf16[512,256]{1,0:T(8,128)(2,1)S(1)}, u32[]{:S(2)}, u32[]{:S(2)}) collective-permute-start(bf16[512,256]{1,0:T(8,128)(2,1)S(1)} %get-tuple-element.38), channel_id=1, source_target_pairs={{0,96},{32,0},{64,32},{96,64},{128,224},{160,128},{192,160},{224,1... | collective-permute-start | bytes 786440 | tf_op jit(solution)/shard_map/ppermute | solution.py:139
  113.0 25.3 %collective-permute-start.3 = (bf16[256,256]{1,0:T(8,128)(2,1)S(1)}, bf16[256,256]{1,0:T(8,128)(2,1)S(1)}, u32[]{:S(2)}, u32[]{:S(2)}) collective-permute-start(bf16[256,256]{1,0:T(8,128)(2,1)S(1)} %get-tuple-element.40), channel_id=1, source_target_pairs={{0,128},{32,160},{64,192},{96,224},{128,0},{160,32},{192,64},{224,... | collective-permute-start | bytes 393224 | tf_op jit(solution)/shard_map/ppermute | solution.py:144
  138.3 45.5 %copy-start.4 = (bf16[256,256]{1,0:T(8,128)(2,1)S(1)}, bf16[256,256]{1,0:T(8,128)(2,1)}, u32[]{:S(2)}) copy-start(bf16[256,256]{1,0:T(8,128)(2,1)} %left_up_ref.3) | copy-start | bytes 393220
  138.4 45.5 %copy-start.5 = (bf16[256,256]{1,0:T(8,128)(2,1)S(1)}, bf16[256,256]{1,0:T(8,128)(2,1)}, u32[]{:S(2)}) copy-start(bf16[256,256]{1,0:T(8,128)(2,1)} %right_down_ref.3) | copy-start | bytes 393220
  138.4 10.7 %collective-permute-start.4 = (bf16[256,256]{1,0:T(8,128)(2,1)S(1)}, bf16[256,256]{1,0:T(8,128)(2,1)S(1)}, u32[]{:S(2)}, u32[]{:S(2)}) collective-permute-start(bf16[256,256]{1,0:T(8,128)(2,1)S(1)} %add_convert_fusion.1), channel_id=1, source_target_pairs={{0,256},{32,288},{64,320},{96,352},{128,384},{160,416},{192,448},{... | collective-permute-start | bytes 393224 | tf_op jit(solution)/shard_map/ppermute | solution.py:144
  150.4 17.4 %all-to-all-start.2 = ((bf16[16,32,256]{2,1,0:T(8,128)(2,1)}), bf16[16,32,256]{2,1,0:T(8,128)(2,1)S(1)}, u32[]{:S(2)}, u32[]{:S(2)}) async-start(bf16[16,32,256]{2,1,0:T(8,128)(2,1)} %bitcast.7), calls=%async_computation.2 | async-start | bytes 524288 | tf_op jit(solution)/shard_map/all_to_all | solution.py:162
  155.8 9.6 %collective-permute-start.5 = (bf16[256,256]{1,0:T(8,128)(2,1)S(1)}, bf16[256,256]{1,0:T(8,128)(2,1)S(1)}, u32[]{:S(2)}, u32[]{:S(2)}) collective-permute-start(bf16[256,256]{1,0:T(8,128)(2,1)S(1)} %add_convert_fusion.own_ref), channel_id=1, source_target_pairs={{0,128},{32,160},{64,192},{96,224},{128,0},{160,32},{192,64},{224,... | collective-permute-start | bytes 393224 | tf_op jit(solution)/shard_map/ppermute | solution.py:144
  168.6 22.2 %all-to-all-start.3 = ((bf16[16,32,256]{2,1,0:T(8,128)(2,1)}), bf16[16,32,256]{2,1,0:T(8,128)(2,1)S(1)}, u32[]{:S(2)}, u32[]{:S(2)}) async-start(bf16[16,32,256]{2,1,0:T(8,128)(2,1)} %get-tuple-element.48), calls=%async_computation.3 | async-start | bytes 524288 | tf_op jit(solution)/shard_map/all_to_all | solution.py:162
  172.1 13.2 %collective-permute-start.6 = (bf16[512,256]{1,0:T(8,128)(2,1)S(1)}, bf16[512,256]{1,0:T(8,128)(2,1)S(1)}, u32[]{:S(2)}, u32[]{:S(2)}) collective-permute-start(bf16[512,256]{1,0:T(8,128)(2,1)S(1)} %get-tuple-element.49.own_ref), channel_id=1, source_target_pairs={{0,32},{32,64},{64,96},{96,0},{128,160},{160,192},{192,224},{224,1... | collective-permute-start | bytes 786440 | tf_op jit(solution)/shard_map/ppermute | solution.py:139
  175.8 14.6 %collective-permute-start.7 = (bf16[512,256]{1,0:T(8,128)(2,1)S(1)}, bf16[512,256]{1,0:T(8,128)(2,1)S(1)}, u32[]{:S(2)}, u32[]{:S(2)}) collective-permute-start(bf16[512,256]{1,0:T(8,128)(2,1)S(1)} %get-tuple-element.49.own_ref), channel_id=1, source_target_pairs={{0,64},{32,96},{64,0},{96,32},{128,192},{160,224},{192,128},{224,1... | collective-permute-start | bytes 786440 | tf_op jit(solution)/shard_map/ppermute | solution.py:139
  180.4 10.4 %collective-permute-start.8 = (bf16[512,256]{1,0:T(8,128)(2,1)S(1)}, bf16[512,256]{1,0:T(8,128)(2,1)S(1)}, u32[]{:S(2)}, u32[]{:S(2)}) collective-permute-start(bf16[512,256]{1,0:T(8,128)(2,1)S(1)} %get-tuple-element.49.own_ref), channel_id=1, source_target_pairs={{0,96},{32,0},{64,32},{96,64},{128,224},{160,128},{192,160},{224,1... | collective-permute-start | bytes 786440 | tf_op jit(solution)/shard_map/ppermute | solution.py:139

commit v8 on v7

--- a/solution.py
+++ b/solution.py
@@ -83,13 +83,6 @@
         out_ref[256:] = dot(mixed_ref[...], back_pre_ref[step], NT).astype(BF16)
 
 
-def fold_kernel(place_ref, own_ref, near_ref, far_ref, last_ref, keep_ref, give_ref, total_ref):
-    total_ref[...] = four_sum(own_ref[...], near_ref[...], far_ref[...], last_ref[...])
-    parity = place_ref[0] & 1
-    keep_ref[...] = total_ref[pl.ds(pl.multiple_of(parity * 256, 256), 256), :]
-    give_ref[...] = total_ref[pl.ds(pl.multiple_of((1 - parity) * 256, 256), 256), :]
-
-
 def exit_grads_kernel(recv_ref, tok_ref, grad_ref, out_ref, mixed_ref, back_first_ref):
     mixed, back_first = unweave(recv_ref[...])
     mixed_ref[...] = mixed
@@ -104,12 +97,10 @@
     in_grad_ref[...] = dot(back_first_ref[...], left_up_t, TN).astype(BF16)
 
 
-def spread_kernel(place_ref, late_ref, own_ref, other_ref, late_out_ref, early_out_ref):
+def spread_kernel(late_ref, own_ref, other_ref, late_out_ref, early_out_ref):
     late = jnp.sum(late_ref[...].astype(F32), axis=0).astype(BF16)
     late_out_ref[...] = jnp.broadcast_to(late[None], late_out_ref.shape)
-    parity = place_ref[0] & 1
-    early_out_ref[pl.ds(pl.multiple_of(parity * 256, 256), 256), :] = own_ref[...]
-    early_out_ref[pl.ds(pl.multiple_of((1 - parity) * 256, 256), 256), :] = other_ref[...]
+    early_out_ref[...] = two_sum(own_ref[...], other_ref[...])
 
 
 def unpack_kernel(place_ref, late_ref, own_ref, near_ref, far_ref, last_ref,
@@ -170,7 +161,7 @@
     tok = tokens_in.shape[0]
     tile = 256
     dp_index = lax.axis_index("dp")
-    y, z_lo = dp_index & 3, dp_index >> 2
+    y = dp_index & 3
 
     weight = lambda rows, cols: pl.BlockSpec((rows, cols), lambda i: (0, 0))
     column = lambda rows: pl.BlockSpec((rows, tile), lambda i: (0, i))
@@ -201,7 +192,6 @@
     smem = pl.BlockSpec(memory_space=pltpu.SMEM)
     far_away = pl.BlockSpec(memory_space=pltpu.HBM)
     y_place = y.astype(jnp.int32).reshape(1)
-    z_place = z_lo.astype(jnp.int32).reshape(1)
     parts = pl.pallas_call(
         middle_grads_kernel,
         in_specs=[smem] + [far_away] * 4,
@@ -212,27 +202,16 @@
         compiler_params=PARAMS,
     )(y_place, in_hbm(hidden), in_hbm(back_pre), in_hbm(mixed_up), in_hbm(back_third))
 
-    keep, give = pl.pallas_call(
-        fold_kernel,
-        in_specs=[smem] + [vmem] * 4,
-        out_shape=[plain((256, 256))] * 2,
-        scratch_shapes=[pltpu.VMEM((512, 256), BF16)],
-        compiler_params=PARAMS,
-    )(z_place, *send_on(parts))
-    part = two_sum(keep, swap_z(give, 1))
-    part = two_sum(part, swap_z(part, 2))
+    part = four_sum(*send_on(parts))
+    part = two_sum(part, swap_z(part, 1))
     recv, part = lax.optimization_barrier((recv, part))
     late, mixed_down, back_first = whole_call(
-        exit_grads_kernel, [hbm((512, 256)), plain((256, tok)), plain((256, tok))],
+        exit_grads_kernel, [hbm((512, 256)), hbm((256, tok)), hbm((256, tok))],
         recv, tokens_in, out_grad)
 
     late = exchange(late.reshape(16, 32, 256), "dp")
-    late, part = pl.pallas_call(
-        spread_kernel,
-        in_specs=[smem] + [vmem] * 3,
-        out_shape=[hbm((16, 32, 256)), plain((512, 256))],
-        compiler_params=PARAMS,
-    )(z_place, late, part, swap_z(part, 1))
+    late, part = whole_call(
+        spread_kernel, [hbm((16, 32, 256)), plain((512, 256))], late, part, swap_z(part, 2))
     late = exchange(late, "dp")
     pieces = send_on([part] * 4)
     layer_out, input_grad = whole_call(

time: 194 us -> 199 us (1.026)
  starting transfers between devices: 71.9 us -> 75 us
  waiting for transfers between devices: 100 us -> 102 us
    ppermute x3 -> x2, waiting for transfers between devices: 35.2 us -> 41.6 us  [swap_z(): return lax.ppermute(array, 'dp', pairs)]
    all_to_all x4, starting transfers between devices: 38.1 us -> 42.7 us  [exchange(): return lax.all_to_all(parts, axis, 0, 0, tiled=True)]
    ppermute x6, waiting for transfers between devices: 13.7 us -> 11.3 us  [along_y(): return lax.ppermute(array, 'dp', pairs)]
    all_to_all x4, waiting for transfers between devices: 51.4 us -> 49 us  [exchange(): return lax.all_to_all(parts, axis, 0, 0, tiled=True)]
    ppermute x3 -> x2, starting transfers between devices: 10.5 us -> 8.24 us  [swap_z(): return lax.ppermute(array, 'dp', pairs)]
  transfers between devices with their start and end apart: 13 -> 12, of which waited for: 10 -> 8; matrix products, arithmetic and copies ran while one was open for 0% -> 0% of each run, Pallas kernels for 4% -> 3%
where the time goes in v8:
time: 199 us; the launch traced here: 196 us
  waiting for transfers between devices  102 us (51%)
  starting transfers between devices  75 us (38%)
  Pallas kernels  17.8 us (9%)
    all_to_all x4, waiting for transfers between devices, exchange(): return lax.all_to_all(parts, axis, 0, 0, tiled=True)  49 us
    all_to_all x4, starting transfers between devices, exchange(): return lax.all_to_all(parts, axis, 0, 0, tiled=True)  42.7 us
    ppermute x2, waiting for transfers between devices, swap_z(): return lax.ppermute(array, 'dp', pairs)  41.6 us
    ppermute x6, starting transfers between devices, along_y(): return lax.ppermute(array, 'dp', pairs)  24 us
    ppermute x6, waiting for transfers between devices, along_y(): return lax.ppermute(array, 'dp', pairs)  11.3 us
    ppermute x2, starting transfers between devices, swap_z(): return lax.ppermute(array, 'dp', pairs)  8.24 us
    pallas_call x1, Pallas kernels, on_device(): pl.pallas_call(middle_kernel, grid=(tok // tile,), in_specs=[woven(tile),...  5.31 us
    pallas_call x1, Pallas kernels, on_device(): pl.pallas_call(middle_grads_kernel, in_specs=[smem] + [far_away] * 4, out...  5.09 us
  transfers between devices with their start and end apart: 12, of which 8 were waited for; matrix products, arithmetic and copies ran while one was open for 0% of the time, Pallas kernels for 3%

profile of v8, /device:TPU:6, one launch (start us, length us, event | category | flops | bytes accessed | tf_op | source)
XLA Modules:
  0.0 196.3 jit_solution(9161565697787115269)
XLA Ops:
  0.6 0.0 copy-start
  0.6 2.7 %shard_map.109 = bf16[32,16,1024]{2,1,0:T(8,128)(2,1)} custom-call(bf16[1024,256]{1,0:T(8,128)(2,1)} %tok_ref.3, bf16[1024,256]{1,0:T(8,128)(2,1)} %grad_ref.3, bf16[256,256]{1,0:T(8,128)(2,1)} %left_up_ref.3, bf16[256,256]{1,0:T(8,128)(2,1)} %right_down_ref.3), custom_call_target="tpu_custom_call" | custom-call | tf_op jit(solution)/shard_map/pallas_call | solution.py:170
  3.3 18.4 %all-to-all-start = ((bf16[32,16,1024]{2,1,0:T(8,128)(2,1)}), bf16[32,16,1024]{2,1,0:T(8,128)(2,1)S(1)}, u32[]{:S(2)}, u32[]{:S(2)}) async-start(bf16[32,16,1024]{2,1,0:T(8,128)(2,1)} %shard_map.109), calls=%async_computation | async-start | bytes 2097152 | tf_op jit(solution)/shard_map/all_to_all | solution.py:153
  21.7 0.0 copy-done
  21.7 0.2 copy.12
  21.9 0.0 copy-done.1
  21.9 0.2 copy.13
  22.1 49.0 %all-to-all-done.recv_ref = bf16[32,16,1024]{2,1,0:T(8,128)(2,1)S(1)} async-done(((bf16[32,16,1024]{2,1,0:T(8,128)(2,1)}), bf16[32,16,1024]{2,1,0:T(8,128)(2,1)S(1)}, u32[]{:S(2)}, u32[]{:S(2)}) %all-to-all-start) | async-done | bytes 1048608 | tf_op jit(solution)/shard_map/all_to_all | solution.py:153
  71.2 5.3 %shard_map.110 = (bf16[32,16,1024]{2,1,0:T(8,128)(2,1)}, bf16[1024,1024]{1,0:T(8,128)(2,1)}, bf16[1024,1024]{1,0:T(8,128)(2,1)}, bf16[256,1024]{1,0:T(8,128)(2,1)}, bf16[256,1024]{1,0:T(8,128)(2,1)}) custom-call(bf16[32,16,1024]{2,1,0:T(8,128)(2,1)S(1)} %all-to-all-done.recv_ref, bf16[256,1024]{1,0:T(8,128)(2,1)S(1)} %copy-done, ...), custom_call_target="tpu_custom_call" | custom-call | tf_op jit(solution)/shard_map/pallas_call | solution.py:180
  76.5 10.8 %all-to-all-start.1 = ((bf16[32,16,1024]{2,1,0:T(8,128)(2,1)}), bf16[32,16,1024]{2,1,0:T(8,128)(2,1)S(1)}, u32[]{:S(2)}, u32[]{:S(2)}) async-start(bf16[32,16,1024]{2,1,0:T(8,128)(2,1)} %get-tuple-element.28), calls=%async_computation.1 | async-start | bytes 2097152 | tf_op jit(solution)/shard_map/all_to_all | solution.py:153
  87.3 5.1 %shard_map.111 = (bf16[512,256]{1,0:T(8,128)(2,1)S(1)}, bf16[512,256]{1,0:T(8,128)(2,1)S(1)}, bf16[512,256]{1,0:T(8,128)(2,1)S(1)}, bf16[512,256]{1,0:T(8,128)(2,1)S(1)}) custom-call(s32[1]{0:T(128)} %bitcast.2.place_ref, bf16[1024,1024]{1,0:T(8,128)(2,1)} %get-tuple-element.29.hidden_hbm, bf16[1024,1024]{1,0:T(8,128)(2,1)} %get-tuple-element.30.back_pre_hbm, ...), custom_call_target="tpu_custom_call" | custom-call | tf_op jit(solution)/shard_map/pallas_call | solution.py:195
  92.4 0.0 copy-start.2
  92.4 0.0 copy-start.3
  92.4 5.2 %collective-permute-start = (bf16[512,256]{1,0:T(8,128)(2,1)S(1)}, bf16[512,256]{1,0:T(8,128)(2,1)S(1)}, u32[]{:S(2)}, u32[]{:S(2)}) collective-permute-start(bf16[512,256]{1,0:T(8,128)(2,1)S(1)} %get-tuple-element.34), channel_id=1, source_target_pairs={{0,64},{32,96},{64,0},{96,32},{128,192},{160,224},{192,128},{224,1... | collective-permute-start | bytes 786440 | tf_op jit(solution)/shard_map/ppermute | solution.py:130
  97.6 2.6 %collective-permute-start.1 = (bf16[512,256]{1,0:T(8,128)(2,1)S(1)}, bf16[512,256]{1,0:T(8,128)(2,1)S(1)}, u32[]{:S(2)}, u32[]{:S(2)}) collective-permute-start(bf16[512,256]{1,0:T(8,128)(2,1)S(1)} %get-tuple-element.35), channel_id=1, source_target_pairs={{0,32},{32,64},{64,96},{96,0},{128,160},{160,192},{192,224},{224,1... | collective-permute-start | bytes 786440 | tf_op jit(solution)/shard_map/ppermute | solution.py:130
  100.2 4.5 %collective-permute-start.2 = (bf16[512,256]{1,0:T(8,128)(2,1)S(1)}, bf16[512,256]{1,0:T(8,128)(2,1)S(1)}, u32[]{:S(2)}, u32[]{:S(2)}) collective-permute-start(bf16[512,256]{1,0:T(8,128)(2,1)S(1)} %get-tuple-element.36), channel_id=1, source_target_pairs={{0,96},{32,0},{64,32},{96,64},{128,224},{160,128},{192,160},{224,1... | collective-permute-start | bytes 786440 | tf_op jit(solution)/shard_map/ppermute | solution.py:130
  104.7 0.4 collective-permute-done
  105.1 4.8 %collective-permute-done.1 = bf16[512,256]{1,0:T(8,128)(2,1)S(1)} collective-permute-done((bf16[512,256]{1,0:T(8,128)(2,1)S(1)}, bf16[512,256]{1,0:T(8,128)(2,1)S(1)}, u32[]{:S(2)}, u32[]{:S(2)}) %collective-permute-start.1) | collective-permute-done | bytes 262176 | tf_op jit(solution)/shard_map/ppermute | solution.py:130
  109.9 0.3 collective-permute-done.2
  110.3 0.1 add_convert_fusion.1
  110.4 3.5 %collective-permute-start.3 = (bf16[512,256]{1,0:T(8,128)(2,1)S(1)}, bf16[512,256]{1,0:T(8,128)(2,1)S(1)}, u32[]{:S(2)}, u32[]{:S(2)}) collective-permute-start(bf16[512,256]{1,0:T(8,128)(2,1)S(1)} %add_convert_fusion.1), channel_id=1, source_target_pairs={{0,128},{32,160},{64,192},{96,224},{128,0},{160,32},{192,64},{224,... | collective-permute-start | bytes 786440 | tf_op jit(solution)/shard_map/ppermute | solution.py:135
  113.9 26.8 %collective-permute-done.3 = bf16[512,256]{1,0:T(8,128)(2,1)S(1)} collective-permute-done((bf16[512,256]{1,0:T(8,128)(2,1)S(1)}, bf16[512,256]{1,0:T(8,128)(2,1)S(1)}, u32[]{:S(2)}, u32[]{:S(2)}) %collective-permute-start.3) | collective-permute-done | bytes 262176 | tf_op jit(solution)/shard_map/ppermute | solution.py:135
  140.7 0.1 add_convert_fusion.own_ref
  140.8 0.0 copy-start.4
  140.8 0.0 copy-start.5
  140.8 0.0 all-to-all-done.1.recv_ref
  140.8 0.0 copy-done.2
  140.8 0.0 copy-done.3
  140.8 1.3 shard_map.112
  142.1 8.3 %all-to-all-start.2 = ((bf16[16,32,256]{2,1,0:T(8,128)(2,1)}), bf16[16,32,256]{2,1,0:T(8,128)(2,1)S(1)}, u32[]{:S(2)}, u32[]{:S(2)}) async-start(bf16[16,32,256]{2,1,0:T(8,128)(2,1)} %bitcast.6), calls=%async_computation.2 | async-start | bytes 524288 | tf_op jit(solution)/shard_map/all_to_all | solution.py:153
  150.4 4.7 %collective-permute-start.4 = (bf16[512,256]{1,0:T(8,128)(2,1)S(1)}, bf16[512,256]{1,0:T(8,128)(2,1)S(1)}, u32[]{:S(2)}, u32[]{:S(2)}) collective-permute-start(bf16[512,256]{1,0:T(8,128)(2,1)S(1)} %add_convert_fusion.own_ref), channel_id=1, source_target_pairs={{0,256},{32,288},{64,320},{96,352},{128,384},{160,416},{192,448},{... | collective-permute-start | bytes 786440 | tf_op jit(solution)/shard_map/ppermute | solution.py:135
  155.2 14.8 %collective-permute-done.4.other_ref = bf16[512,256]{1,0:T(8,128)(2,1)S(1)} collective-permute-done((bf16[512,256]{1,0:T(8,128)(2,1)S(1)}, bf16[512,256]{1,0:T(8,128)(2,1)S(1)}, u32[]{:S(2)}, u32[]{:S(2)}) %collective-permute-start.4) | collective-permute-done | bytes 262176 | tf_op jit(solution)/shard_map/ppermute | solution.py:135
  170.0 0.0 all-to-all-done.2.late_ref
  170.0 0.8 shard_map.114
  170.7 5.2 %all-to-all-start.3 = ((bf16[16,32,256]{2,1,0:T(8,128)(2,1)}), bf16[16,32,256]{2,1,0:T(8,128)(2,1)S(1)}, u32[]{:S(2)}, u32[]{:S(2)}) async-start(bf16[16,32,256]{2,1,0:T(8,128)(2,1)} %get-tuple-element.44), calls=%async_computation.3 | async-start | bytes 524288 | tf_op jit(solution)/shard_map/all_to_all | solution.py:153
  176.0 3.8 %collective-permute-start.5 = (bf16[512,256]{1,0:T(8,128)(2,1)S(1)}, bf16[512,256]{1,0:T(8,128)(2,1)S(1)}, u32[]{:S(2)}, u32[]{:S(2)}) collective-permute-start(bf16[512,256]{1,0:T(8,128)(2,1)S(1)} %get-tuple-element.45.own_ref), channel_id=1, source_target_pairs={{0,32},{32,64},{64,96},{96,0},{128,160},{160,192},{192,224},{224,1... | collective-permute-start | bytes 786440 | tf_op jit(solution)/shard_map/ppermute | solution.py:130
  179.8 4.6 %collective-permute-start.6 = (bf16[512,256]{1,0:T(8,128)(2,1)S(1)}, bf16[512,256]{1,0:T(8,128)(2,1)S(1)}, u32[]{:S(2)}, u32[]{:S(2)}) collective-permute-start(bf16[512,256]{1,0:T(8,128)(2,1)S(1)} %get-tuple-element.45.own_ref), channel_id=1, source_target_pairs={{0,64},{32,96},{64,0},{96,32},{128,192},{160,224},{192,128},{224,1... | collective-permute-start | bytes 786440 | tf_op jit(solution)/shard_map/ppermute | solution.py:130
  184.4 3.4 %collective-permute-start.7 = (bf16[512,256]{1,0:T(8,128)(2,1)S(1)}, bf16[512,256]{1,0:T(8,128)(2,1)S(1)}, u32[]{:S(2)}, u32[]{:S(2)}) collective-permute-start(bf16[512,256]{1,0:T(8,128)(2,1)S(1)} %get-tuple-element.45.own_ref), channel_id=1, source_target_pairs={{0,96},{32,0},{64,32},{96,64},{128,224},{160,128},{192,160},{224,1... | collective-permute-start | bytes 786440 | tf_op jit(solution)/shard_map/ppermute | solution.py:130
  187.8 0.0 copy-done.4
  187.8 0.0 copy-done.5
  187.8 0.0 copy-done.6
  187.8 0.0 copy-done.7
  187.8 1.5 shard_map.113
  189.3 0.0 collective-permute-done.5.near_ref
  189.3 5.5 %collective-permute-done.6.far_ref = bf16[512,256]{1,0:T(8,128)(2,1)S(1)} collective-permute-done((bf16[512,256]{1,0:T(8,128)(2,1)S(1)}, bf16[512,256]{1,0:T(8,128)(2,1)S(1)}, u32[]{:S(2)}, u32[]{:S(2)}) %collective-permute-start.6) | collective-permute-done | bytes 262176 | tf_op jit(solution)/shard_map/ppermute | solution.py:130
  194.8 0.3 collective-permute-done.7.last_ref
  195.1 0.0 all-to-all-done.3.late_ref
  195.1 1.2 shard_map.115
  (3 shorter events, 0.0 us)
Async XLA Ops:
  0.6 21.1 %copy-start = (bf16[256,1024]{1,0:T(8,128)(2,1)S(1)}, bf16[256,1024]{1,0:T(8,128)(2,1)}, u32[]{:S(2)}) copy-start(bf16[256,1024]{1,0:T(8,128)(2,1)} %right_up_ref.1) | copy-start | bytes 1572868
  3.3 18.6 %copy-start.1 = (bf16[1024,256]{1,0:T(8,128)(2,1)S(1)}, bf16[1024,256]{1,0:T(8,128)(2,1)}, u32[]{:S(2)}) copy-start(bf16[1024,256]{1,0:T(8,128)(2,1)} %left_down_ref.1) | copy-start | bytes 1572868
  3.3 67.8 %all-to-all-start = ((bf16[32,16,1024]{2,1,0:T(8,128)(2,1)}), bf16[32,16,1024]{2,1,0:T(8,128)(2,1)S(1)}, u32[]{:S(2)}, u32[]{:S(2)}) async-start(bf16[32,16,1024]{2,1,0:T(8,128)(2,1)} %shard_map.109), calls=%async_computation | async-start | bytes 2097152 | tf_op jit(solution)/shard_map/all_to_all | solution.py:153
  76.5 64.3 %all-to-all-start.1 = ((bf16[32,16,1024]{2,1,0:T(8,128)(2,1)}), bf16[32,16,1024]{2,1,0:T(8,128)(2,1)S(1)}, u32[]{:S(2)}, u32[]{:S(2)}) async-start(bf16[32,16,1024]{2,1,0:T(8,128)(2,1)} %get-tuple-element.28), calls=%async_computation.1 | async-start | bytes 2097152 | tf_op jit(solution)/shard_map/all_to_all | solution.py:153
  92.4 48.4 %copy-start.2 = (bf16[1024,256]{1,0:T(8,128)(2,1)S(1)}, bf16[1024,256]{1,0:T(8,128)(2,1)}, u32[]{:S(2)}) copy-start(bf16[1024,256]{1,0:T(8,128)(2,1)} %tok_ref.3) | copy-start | bytes 1572868
  92.4 48.4 %copy-start.3 = (bf16[1024,256]{1,0:T(8,128)(2,1)S(1)}, bf16[1024,256]{1,0:T(8,128)(2,1)}, u32[]{:S(2)}) copy-start(bf16[1024,256]{1,0:T(8,128)(2,1)} %grad_ref.3) | copy-start | bytes 1572868
  92.4 12.7 %collective-permute-start = (bf16[512,256]{1,0:T(8,128)(2,1)S(1)}, bf16[512,256]{1,0:T(8,128)(2,1)S(1)}, u32[]{:S(2)}, u32[]{:S(2)}) collective-permute-start(bf16[512,256]{1,0:T(8,128)(2,1)S(1)} %get-tuple-element.34), channel_id=1, source_target_pairs={{0,64},{32,96},{64,0},{96,32},{128,192},{160,224},{192,128},{224,1... | collective-permute-start | bytes 786440 | tf_op jit(solution)/shard_map/ppermute | solution.py:130
  97.6 12.3 %collective-permute-start.1 = (bf16[512,256]{1,0:T(8,128)(2,1)S(1)}, bf16[512,256]{1,0:T(8,128)(2,1)S(1)}, u32[]{:S(2)}, u32[]{:S(2)}) collective-permute-start(bf16[512,256]{1,0:T(8,128)(2,1)S(1)} %get-tuple-element.35), channel_id=1, source_target_pairs={{0,32},{32,64},{64,96},{96,0},{128,160},{160,192},{192,224},{224,1... | collective-permute-start | bytes 786440 | tf_op jit(solution)/shard_map/ppermute | solution.py:130
  100.2 10.0 %collective-permute-start.2 = (bf16[512,256]{1,0:T(8,128)(2,1)S(1)}, bf16[512,256]{1,0:T(8,128)(2,1)S(1)}, u32[]{:S(2)}, u32[]{:S(2)}) collective-permute-start(bf16[512,256]{1,0:T(8,128)(2,1)S(1)} %get-tuple-element.36), channel_id=1, source_target_pairs={{0,96},{32,0},{64,32},{96,64},{128,224},{160,128},{192,160},{224,1... | collective-permute-start | bytes 786440 | tf_op jit(solution)/shard_map/ppermute | solution.py:130
  110.4 30.3 %collective-permute-start.3 = (bf16[512,256]{1,0:T(8,128)(2,1)S(1)}, bf16[512,256]{1,0:T(8,128)(2,1)S(1)}, u32[]{:S(2)}, u32[]{:S(2)}) collective-permute-start(bf16[512,256]{1,0:T(8,128)(2,1)S(1)} %add_convert_fusion.1), channel_id=1, source_target_pairs={{0,128},{32,160},{64,192},{96,224},{128,0},{160,32},{192,64},{224,... | collective-permute-start | bytes 786440 | tf_op jit(solution)/shard_map/ppermute | solution.py:135
  140.8 47.0 %copy-start.4 = (bf16[256,256]{1,0:T(8,128)(2,1)S(1)}, bf16[256,256]{1,0:T(8,128)(2,1)}, u32[]{:S(2)}) copy-start(bf16[256,256]{1,0:T(8,128)(2,1)} %left_up_ref.3) | copy-start | bytes 393220
  140.8 47.0 %copy-start.5 = (bf16[256,256]{1,0:T(8,128)(2,1)S(1)}, bf16[256,256]{1,0:T(8,128)(2,1)}, u32[]{:S(2)}) copy-start(bf16[256,256]{1,0:T(8,128)(2,1)} %right_down_ref.3) | copy-start | bytes 393220
  142.1 45.7 %copy-start.6 = (bf16[256,1024]{1,0:T(8,128)(2,1)S(1)}, bf16[256,1024]{1,0:T(8,128)(2,1)}, u32[]{:S(2)}) copy-start(bf16[256,1024]{1,0:T(8,128)(2,1)} %get-tuple-element.38.mixed_ref) | copy-start | bytes 1572868
  142.1 45.7 %copy-start.7 = (bf16[256,1024]{1,0:T(8,128)(2,1)S(1)}, bf16[256,1024]{1,0:T(8,128)(2,1)}, u32[]{:S(2)}) copy-start(bf16[256,1024]{1,0:T(8,128)(2,1)} %get-tuple-element.39.back_first_ref) | copy-start | bytes 1572868
  142.1 27.8 %all-to-all-start.2 = ((bf16[16,32,256]{2,1,0:T(8,128)(2,1)}), bf16[16,32,256]{2,1,0:T(8,128)(2,1)S(1)}, u32[]{:S(2)}, u32[]{:S(2)}) async-start(bf16[16,32,256]{2,1,0:T(8,128)(2,1)} %bitcast.6), calls=%async_computation.2 | async-start | bytes 524288 | tf_op jit(solution)/shard_map/all_to_all | solution.py:153
  150.4 19.5 %collective-permute-start.4 = (bf16[512,256]{1,0:T(8,128)(2,1)S(1)}, bf16[512,256]{1,0:T(8,128)(2,1)S(1)}, u32[]{:S(2)}, u32[]{:S(2)}) collective-permute-start(bf16[512,256]{1,0:T(8,128)(2,1)S(1)} %add_convert_fusion.own_ref), channel_id=1, source_target_pairs={{0,256},{32,288},{64,320},{96,352},{128,384},{160,416},{192,448},{... | collective-permute-start | bytes 786440 | tf_op jit(solution)/shard_map/ppermute | solution.py:135
  170.7 24.4 %all-to-all-start.3 = ((bf16[16,32,256]{2,1,0:T(8,128)(2,1)}), bf16[16,32,256]{2,1,0:T(8,128)(2,1)S(1)}, u32[]{:S(2)}, u32[]{:S(2)}) async-start(bf16[16,32,256]{2,1,0:T(8,128)(2,1)} %get-tuple-element.44), calls=%async_computation.3 | async-start | bytes 524288 | tf_op jit(solution)/shard_map/all_to_all | solution.py:153
  176.0 13.3 %collective-permute-start.5 = (bf16[512,256]{1,0:T(8,128)(2,1)S(1)}, bf16[512,256]{1,0:T(8,128)(2,1)S(1)}, u32[]{:S(2)}, u32[]{:S(2)}) collective-permute-start(bf16[512,256]{1,0:T(8,128)(2,1)S(1)} %get-tuple-element.45.own_ref), channel_id=1, source_target_pairs={{0,32},{32,64},{64,96},{96,0},{128,160},{160,192},{192,224},{224,1... | collective-permute-start | bytes 786440 | tf_op jit(solution)/shard_map/ppermute | solution.py:130
  179.8 15.0 %collective-permute-start.6 = (bf16[512,256]{1,0:T(8,128)(2,1)S(1)}, bf16[512,256]{1,0:T(8,128)(2,1)S(1)}, u32[]{:S(2)}, u32[]{:S(2)}) collective-permute-start(bf16[512,256]{1,0:T(8,128)(2,1)S(1)} %get-tuple-element.45.own_ref), channel_id=1, source_target_pairs={{0,64},{32,96},{64,0},{96,32},{128,192},{160,224},{192,128},{224,1... | collective-permute-start | bytes 786440 | tf_op jit(solution)/shard_map/ppermute | solution.py:130
  184.4 10.7 %collective-permute-start.7 = (bf16[512,256]{1,0:T(8,128)(2,1)S(1)}, bf16[512,256]{1,0:T(8,128)(2,1)S(1)}, u32[]{:S(2)}, u32[]{:S(2)}) collective-permute-start(bf16[512,256]{1,0:T(8,128)(2,1)S(1)} %get-tuple-element.45.own_ref), channel_id=1, source_target_pairs={{0,96},{32,0},{64,32},{96,64},{128,224},{160,128},{192,160},{224,1... | collective-permute-start | bytes 786440 | tf_op jit(solution)/shard_map/ppermute | solution.py:130

commit v9 on v7

--- a/solution.py
+++ b/solution.py
@@ -85,9 +85,9 @@
 
 def fold_kernel(place_ref, own_ref, near_ref, far_ref, last_ref, keep_ref, give_ref, total_ref):
     total_ref[...] = four_sum(own_ref[...], near_ref[...], far_ref[...], last_ref[...])
-    parity = place_ref[0] & 1
-    keep_ref[...] = total_ref[pl.ds(pl.multiple_of(parity * 256, 256), 256), :]
-    give_ref[...] = total_ref[pl.ds(pl.multiple_of((1 - parity) * 256, 256), 256), :]
+    half = place_ref[0] & 1
+    keep_ref[...] = total_ref[pl.ds(pl.multiple_of(half * 256, 256), 256), :]
+    give_ref[...] = total_ref[pl.ds(pl.multiple_of((1 - half) * 256, 256), 256), :]
 
 
 def exit_grads_kernel(recv_ref, tok_ref, grad_ref, out_ref, mixed_ref, back_first_ref):
@@ -107,9 +107,9 @@
 def spread_kernel(place_ref, late_ref, own_ref, other_ref, late_out_ref, early_out_ref):
     late = jnp.sum(late_ref[...].astype(F32), axis=0).astype(BF16)
     late_out_ref[...] = jnp.broadcast_to(late[None], late_out_ref.shape)
-    parity = place_ref[0] & 1
-    early_out_ref[pl.ds(pl.multiple_of(parity * 256, 256), 256), :] = own_ref[...]
-    early_out_ref[pl.ds(pl.multiple_of((1 - parity) * 256, 256), 256), :] = other_ref[...]
+    half = place_ref[0] & 1
+    early_out_ref[pl.ds(pl.multiple_of(half * 256, 256), 256), :] = own_ref[...]
+    early_out_ref[pl.ds(pl.multiple_of((1 - half) * 256, 256), 256), :] = other_ref[...]
 
 
 def unpack_kernel(place_ref, late_ref, own_ref, near_ref, far_ref, last_ref,
@@ -201,7 +201,7 @@
     smem = pl.BlockSpec(memory_space=pltpu.SMEM)
     far_away = pl.BlockSpec(memory_space=pltpu.HBM)
     y_place = y.astype(jnp.int32).reshape(1)
-    z_place = z_lo.astype(jnp.int32).reshape(1)
+    z_half = (z_lo >> 1).astype(jnp.int32).reshape(1)
     parts = pl.pallas_call(
         middle_grads_kernel,
         in_specs=[smem] + [far_away] * 4,
@@ -218,9 +218,9 @@
         out_shape=[plain((256, 256))] * 2,
         scratch_shapes=[pltpu.VMEM((512, 256), BF16)],
         compiler_params=PARAMS,
-    )(z_place, *send_on(parts))
-    part = two_sum(keep, swap_z(give, 1))
-    part = two_sum(part, swap_z(part, 2))
+    )(z_half, *send_on(parts))
+    part = two_sum(keep, swap_z(give, 2))
+    part = two_sum(part, swap_z(part, 1))
     recv, part = lax.optimization_barrier((recv, part))
     late, mixed_down, back_first = whole_call(
         exit_grads_kernel, [hbm((512, 256)), plain((256, tok)), plain((256, tok))],
@@ -232,7 +232,7 @@
         in_specs=[smem] + [vmem] * 3,
         out_shape=[hbm((16, 32, 256)), plain((512, 256))],
         compiler_params=PARAMS,
-    )(z_place, late, part, swap_z(part, 1))
+    )(z_half, late, part, swap_z(part, 2))
     late = exchange(late, "dp")
     pieces = send_on([part] * 4)
     layer_out, input_grad = whole_call(

time: 194 us -> 195 us (level)
  starting transfers between devices: 71.9 us -> 75.9 us
  waiting for transfers between devices: 100 us -> 96.6 us
    all_to_all x4, starting transfers between devices: 38.1 us -> 41.1 us  [exchange(): return lax.all_to_all(parts, axis, 0, 0, tiled=True)]
    all_to_all x4, waiting for transfers between devices: 51.4 us -> 49 us  [exchange(): return lax.all_to_all(parts, axis, 0, 0, tiled=True)]
  transfers between devices with their start and end apart: 13 -> 13, of which waited for: 10 -> 9; matrix products, arithmetic and copies ran while one was open for 0% -> 0% of each run, Pallas kernels for 4% -> 4%
where the time goes in v9:
time: 195 us; the launch traced here: 192 us
  waiting for transfers between devices  96.6 us (50%)
  starting transfers between devices  75.9 us (39%)
  Pallas kernels  18.3 us (9%)
    all_to_all x4, waiting for transfers between devices, exchange(): return lax.all_to_all(parts, axis, 0, 0, tiled=True)  49 us
    all_to_all x4, starting transfers between devices, exchange(): return lax.all_to_all(parts, axis, 0, 0, tiled=True)  41.1 us
    ppermute x3, waiting for transfers between devices, swap_z(): return lax.ppermute(array, 'dp', pairs)  33.5 us
    ppermute x6, starting transfers between devices, along_y(): return lax.ppermute(array, 'dp', pairs)  23.4 us
    ppermute x6, waiting for transfers between devices, along_y(): return lax.ppermute(array, 'dp', pairs)  14.1 us
    ppermute x3, starting transfers between devices, swap_z(): return lax.ppermute(array, 'dp', pairs)  11.3 us
    pallas_call x1, Pallas kernels, on_device(): pl.pallas_call(middle_grads_kernel, in_specs=[smem] + [far_away] * 4, out...  5.42 us
    pallas_call x1, Pallas kernels, on_device(): pl.pallas_call(middle_kernel, grid=(tok // tile,), in_specs=[woven(tile),...  5.31 us
  transfers between devices with their start and end apart: 13, of which 9 were waited for; matrix products, arithmetic and copies ran while one was open for 0% of the time, Pallas kernels for 4%

profile of v9, /device:TPU:6, one launch (start us, length us, event | category | flops | bytes accessed | tf_op | source)
XLA Modules:
  0.0 192.2 jit_solution(17460627058177068096)
XLA Ops:
  0.6 0.0 copy-start
  0.6 2.7 %shard_map.109 = bf16[32,16,1024]{2,1,0:T(8,128)(2,1)} custom-call(bf16[1024,256]{1,0:T(8,128)(2,1)} %tok_ref.3, bf16[1024,256]{1,0:T(8,128)(2,1)} %grad_ref.3, bf16[256,256]{1,0:T(8,128)(2,1)} %left_up_ref.3, bf16[256,256]{1,0:T(8,128)(2,1)} %right_down_ref.3), custom_call_target="tpu_custom_call" | custom-call | tf_op jit(solution)/shard_map/pallas_call | solution.py:179
  3.3 0.0 copy-start.1
  3.3 18.4 %all-to-all-start = ((bf16[32,16,1024]{2,1,0:T(8,128)(2,1)}), bf16[32,16,1024]{2,1,0:T(8,128)(2,1)S(1)}, u32[]{:S(2)}, u32[]{:S(2)}) async-start(bf16[32,16,1024]{2,1,0:T(8,128)(2,1)} %shard_map.109), calls=%async_computation | async-start | bytes 2097152 | tf_op jit(solution)/shard_map/all_to_all | solution.py:162
  21.7 0.0 copy-done
  21.7 0.2 copy.12
  21.9 0.0 copy-done.1
  21.9 0.2 copy.13
  22.1 49.0 %all-to-all-done.recv_ref = bf16[32,16,1024]{2,1,0:T(8,128)(2,1)S(1)} async-done(((bf16[32,16,1024]{2,1,0:T(8,128)(2,1)}), bf16[32,16,1024]{2,1,0:T(8,128)(2,1)S(1)}, u32[]{:S(2)}, u32[]{:S(2)}) %all-to-all-start) | async-done | bytes 1048608 | tf_op jit(solution)/shard_map/all_to_all | solution.py:162
  71.2 5.3 %shard_map.110 = (bf16[32,16,1024]{2,1,0:T(8,128)(2,1)}, bf16[1024,1024]{1,0:T(8,128)(2,1)}, bf16[1024,1024]{1,0:T(8,128)(2,1)}, bf16[256,1024]{1,0:T(8,128)(2,1)}, bf16[256,1024]{1,0:T(8,128)(2,1)}) custom-call(bf16[32,16,1024]{2,1,0:T(8,128)(2,1)S(1)} %all-to-all-done.recv_ref, bf16[256,1024]{1,0:T(8,128)(2,1)S(1)} %copy-done, ...), custom_call_target="tpu_custom_call" | custom-call | tf_op jit(solution)/shard_map/pallas_call | solution.py:189
  76.5 10.8 %all-to-all-start.1 = ((bf16[32,16,1024]{2,1,0:T(8,128)(2,1)}), bf16[32,16,1024]{2,1,0:T(8,128)(2,1)S(1)}, u32[]{:S(2)}, u32[]{:S(2)}) async-start(bf16[32,16,1024]{2,1,0:T(8,128)(2,1)} %get-tuple-element.30), calls=%async_computation.1 | async-start | bytes 2097152 | tf_op jit(solution)/shard_map/all_to_all | solution.py:162
  87.3 5.4 %shard_map.111 = (bf16[512,256]{1,0:T(8,128)(2,1)S(1)}, bf16[512,256]{1,0:T(8,128)(2,1)}, bf16[512,256]{1,0:T(8,128)(2,1)}, bf16[512,256]{1,0:T(8,128)(2,1)S(1)}) custom-call(s32[1]{0:T(128)} %bitcast.3.place_ref, bf16[1024,1024]{1,0:T(8,128)(2,1)} %get-tuple-element.31.hidden_hbm, bf16[1024,1024]{1,0:T(8,128)(2,1)} %get-tuple-element.32.back_pre_hbm, ...), custom_call_target="tpu_custom_call" | custom-call | tf_op jit(solution)/shard_map/pallas_call | solution.py:205
  92.7 0.0 copy-start.2
  92.7 0.0 copy-start.3
  92.8 3.6 %collective-permute-start = (bf16[512,256]{1,0:T(8,128)(2,1)}, bf16[512,256]{1,0:T(8,128)(2,1)S(1)}, u32[]{:S(2)}, u32[]{:S(2)}) collective-permute-start(bf16[512,256]{1,0:T(8,128)(2,1)} %get-tuple-element.36), channel_id=1, source_target_pairs={{0,32},{32,64},{64,96},{96,0},{128,160},{160,192},{192,224},{224,1... | collective-permute-start | bytes 786440 | tf_op jit(solution)/shard_map/ppermute | solution.py:139
  96.4 4.8 %collective-permute-start.1 = (bf16[512,256]{1,0:T(8,128)(2,1)}, bf16[512,256]{1,0:T(8,128)(2,1)S(1)}, u32[]{:S(2)}, u32[]{:S(2)}) collective-permute-start(bf16[512,256]{1,0:T(8,128)(2,1)} %get-tuple-element.37), channel_id=1, source_target_pairs={{0,64},{32,96},{64,0},{96,32},{128,192},{160,224},{192,128},{224,1... | collective-permute-start | bytes 786440 | tf_op jit(solution)/shard_map/ppermute | solution.py:139
  101.2 3.3 %collective-permute-start.2 = (bf16[512,256]{1,0:T(8,128)(2,1)S(1)}, bf16[512,256]{1,0:T(8,128)(2,1)S(1)}, u32[]{:S(2)}, u32[]{:S(2)}) collective-permute-start(bf16[512,256]{1,0:T(8,128)(2,1)S(1)} %get-tuple-element.38), channel_id=1, source_target_pairs={{0,96},{32,0},{64,32},{96,64},{128,224},{160,128},{192,160},{224,1... | collective-permute-start | bytes 786440 | tf_op jit(solution)/shard_map/ppermute | solution.py:139
  104.4 0.2 collective-permute-done.near_ref
  104.6 6.8 %collective-permute-done.1.far_ref = bf16[512,256]{1,0:T(8,128)(2,1)S(1)} collective-permute-done((bf16[512,256]{1,0:T(8,128)(2,1)}, bf16[512,256]{1,0:T(8,128)(2,1)S(1)}, u32[]{:S(2)}, u32[]{:S(2)}) %collective-permute-start.1) | collective-permute-done | bytes 262176 | tf_op jit(solution)/shard_map/ppermute | solution.py:139
  111.4 1.3 collective-permute-done.2.last_ref
  112.7 0.2 shard_map.112
  113.0 4.6 %collective-permute-start.3 = (bf16[256,256]{1,0:T(8,128)(2,1)S(1)}, bf16[256,256]{1,0:T(8,128)(2,1)S(1)}, u32[]{:S(2)}, u32[]{:S(2)}) collective-permute-start(bf16[256,256]{1,0:T(8,128)(2,1)S(1)} %get-tuple-element.40), channel_id=1, source_target_pairs={{0,256},{32,288},{64,320},{96,352},{128,384},{160,416},{192,448},{... | collective-permute-start | bytes 393224 | tf_op jit(solution)/shard_map/ppermute | solution.py:144
  117.6 18.0 %collective-permute-done.3 = bf16[256,256]{1,0:T(8,128)(2,1)S(1)} collective-permute-done((bf16[256,256]{1,0:T(8,128)(2,1)S(1)}, bf16[256,256]{1,0:T(8,128)(2,1)S(1)}, u32[]{:S(2)}, u32[]{:S(2)}) %collective-permute-start.3) | collective-permute-done | bytes 131104 | tf_op jit(solution)/shard_map/ppermute | solution.py:144
  135.6 0.0 copy-start.4
  135.6 0.0 copy-start.5
  135.6 2.1 %collective-permute-start.4 = (bf16[256,256]{1,0:T(8,128)(2,1)S(1)}, bf16[256,256]{1,0:T(8,128)(2,1)S(1)}, u32[]{:S(2)}, u32[]{:S(2)}) collective-permute-start(bf16[256,256]{1,0:T(8,128)(2,1)S(1)} %add_convert_fusion.1), channel_id=1, source_target_pairs={{0,128},{32,160},{64,192},{96,224},{128,0},{160,32},{192,64},{224,... | collective-permute-start | bytes 393224 | tf_op jit(solution)/shard_map/ppermute | solution.py:144
  137.6 5.9 %collective-permute-done.4 = bf16[256,256]{1,0:T(8,128)(2,1)S(1)} collective-permute-done((bf16[256,256]{1,0:T(8,128)(2,1)S(1)}, bf16[256,256]{1,0:T(8,128)(2,1)S(1)}, u32[]{:S(2)}, u32[]{:S(2)}) %collective-permute-start.4) | collective-permute-done | bytes 131104 | tf_op jit(solution)/shard_map/ppermute | solution.py:144
  143.6 0.0 all-to-all-done.1.recv_ref
  143.6 0.0 copy-done.2
  143.6 0.0 copy-done.3
  143.6 1.2 shard_map.113
  144.8 6.6 %all-to-all-start.2 = ((bf16[16,32,256]{2,1,0:T(8,128)(2,1)}), bf16[16,32,256]{2,1,0:T(8,128)(2,1)S(1)}, u32[]{:S(2)}, u32[]{:S(2)}) async-start(bf16[16,32,256]{2,1,0:T(8,128)(2,1)} %bitcast.7), calls=%async_computation.2 | async-start | bytes 524288 | tf_op jit(solution)/shard_map/all_to_all | solution.py:162
  151.5 4.7 %collective-permute-start.5 = (bf16[256,256]{1,0:T(8,128)(2,1)S(1)}, bf16[256,256]{1,0:T(8,128)(2,1)S(1)}, u32[]{:S(2)}, u32[]{:S(2)}) collective-permute-start(bf16[256,256]{1,0:T(8,128)(2,1)S(1)} %add_convert_fusion.own_ref), channel_id=1, source_target_pairs={{0,256},{32,288},{64,320},{96,352},{128,384},{160,416},{192,448},{... | collective-permute-start | bytes 393224 | tf_op jit(solution)/shard_map/ppermute | solution.py:144
  156.2 9.6 %collective-permute-done.5.other_ref = bf16[256,256]{1,0:T(8,128)(2,1)S(1)} collective-permute-done((bf16[256,256]{1,0:T(8,128)(2,1)S(1)}, bf16[256,256]{1,0:T(8,128)(2,1)S(1)}, u32[]{:S(2)}, u32[]{:S(2)}) %collective-permute-start.5) | collective-permute-done | bytes 131104 | tf_op jit(solution)/shard_map/ppermute | solution.py:144
  165.9 0.0 all-to-all-done.2.late_ref
  165.9 0.8 shard_map.115
  166.6 5.2 %all-to-all-start.3 = ((bf16[16,32,256]{2,1,0:T(8,128)(2,1)}), bf16[16,32,256]{2,1,0:T(8,128)(2,1)S(1)}, u32[]{:S(2)}, u32[]{:S(2)}) async-start(bf16[16,32,256]{2,1,0:T(8,128)(2,1)} %get-tuple-element.48), calls=%async_computation.3 | async-start | bytes 524288 | tf_op jit(solution)/shard_map/all_to_all | solution.py:162
  171.9 3.8 %collective-permute-start.6 = (bf16[512,256]{1,0:T(8,128)(2,1)S(1)}, bf16[512,256]{1,0:T(8,128)(2,1)S(1)}, u32[]{:S(2)}, u32[]{:S(2)}) collective-permute-start(bf16[512,256]{1,0:T(8,128)(2,1)S(1)} %get-tuple-element.49.own_ref), channel_id=1, source_target_pairs={{0,32},{32,64},{64,96},{96,0},{128,160},{160,192},{192,224},{224,1... | collective-permute-start | bytes 786440 | tf_op jit(solution)/shard_map/ppermute | solution.py:139
  175.7 4.6 %collective-permute-start.7 = (bf16[512,256]{1,0:T(8,128)(2,1)S(1)}, bf16[512,256]{1,0:T(8,128)(2,1)S(1)}, u32[]{:S(2)}, u32[]{:S(2)}) collective-permute-start(bf16[512,256]{1,0:T(8,128)(2,1)S(1)} %get-tuple-element.49.own_ref), channel_id=1, source_target_pairs={{0,64},{32,96},{64,0},{96,32},{128,192},{160,224},{192,128},{224,1... | collective-permute-start | bytes 786440 | tf_op jit(solution)/shard_map/ppermute | solution.py:139
  180.3 3.4 %collective-permute-start.8 = (bf16[512,256]{1,0:T(8,128)(2,1)S(1)}, bf16[512,256]{1,0:T(8,128)(2,1)S(1)}, u32[]{:S(2)}, u32[]{:S(2)}) collective-permute-start(bf16[512,256]{1,0:T(8,128)(2,1)S(1)} %get-tuple-element.49.own_ref), channel_id=1, source_target_pairs={{0,96},{32,0},{64,32},{96,64},{128,224},{160,128},{192,160},{224,1... | collective-permute-start | bytes 786440 | tf_op jit(solution)/shard_map/ppermute | solution.py:139
  183.7 0.0 copy-done.4
  183.7 0.0 copy-done.5
  183.7 1.5 shard_map.114
  185.2 0.0 collective-permute-done.6.near_ref
  185.2 5.5 %collective-permute-done.7.far_ref = bf16[512,256]{1,0:T(8,128)(2,1)S(1)} collective-permute-done((bf16[512,256]{1,0:T(8,128)(2,1)S(1)}, bf16[512,256]{1,0:T(8,128)(2,1)S(1)}, u32[]{:S(2)}, u32[]{:S(2)}) %collective-permute-start.7) | collective-permute-done | bytes 262176 | tf_op jit(solution)/shard_map/ppermute | solution.py:139
  190.7 0.3 collective-permute-done.8.last_ref
  191.0 0.0 all-to-all-done.3.late_ref
  191.0 1.2 shard_map.116
  (2 shorter events, 0.1 us)
Async XLA Ops:
  0.6 21.1 %copy-start = (bf16[256,1024]{1,0:T(8,128)(2,1)S(1)}, bf16[256,1024]{1,0:T(8,128)(2,1)}, u32[]{:S(2)}) copy-start(bf16[256,1024]{1,0:T(8,128)(2,1)} %right_up_ref.1) | copy-start | bytes 1572868
  3.3 18.6 %copy-start.1 = (bf16[1024,256]{1,0:T(8,128)(2,1)S(1)}, bf16[1024,256]{1,0:T(8,128)(2,1)}, u32[]{:S(2)}) copy-start(bf16[1024,256]{1,0:T(8,128)(2,1)} %left_down_ref.1) | copy-start | bytes 1572868
  3.3 67.8 %all-to-all-start = ((bf16[32,16,1024]{2,1,0:T(8,128)(2,1)}), bf16[32,16,1024]{2,1,0:T(8,128)(2,1)S(1)}, u32[]{:S(2)}, u32[]{:S(2)}) async-start(bf16[32,16,1024]{2,1,0:T(8,128)(2,1)} %shard_map.109), calls=%async_computation | async-start | bytes 2097152 | tf_op jit(solution)/shard_map/all_to_all | solution.py:162
  76.5 67.1 %all-to-all-start.1 = ((bf16[32,16,1024]{2,1,0:T(8,128)(2,1)}), bf16[32,16,1024]{2,1,0:T(8,128)(2,1)S(1)}, u32[]{:S(2)}, u32[]{:S(2)}) async-start(bf16[32,16,1024]{2,1,0:T(8,128)(2,1)} %get-tuple-element.30), calls=%async_computation.1 | async-start | bytes 2097152 | tf_op jit(solution)/shard_map/all_to_all | solution.py:162
  92.7 50.9 %copy-start.2 = (bf16[1024,256]{1,0:T(8,128)(2,1)S(1)}, bf16[1024,256]{1,0:T(8,128)(2,1)}, u32[]{:S(2)}) copy-start(bf16[1024,256]{1,0:T(8,128)(2,1)} %tok_ref.3) | copy-start | bytes 1572868
  92.7 50.9 %copy-start.3 = (bf16[1024,256]{1,0:T(8,128)(2,1)S(1)}, bf16[1024,256]{1,0:T(8,128)(2,1)}, u32[]{:S(2)}) copy-start(bf16[1024,256]{1,0:T(8,128)(2,1)} %grad_ref.3) | copy-start | bytes 1572868
  92.8 11.9 %collective-permute-start = (bf16[512,256]{1,0:T(8,128)(2,1)}, bf16[512,256]{1,0:T(8,128)(2,1)S(1)}, u32[]{:S(2)}, u32[]{:S(2)}) collective-permute-start(bf16[512,256]{1,0:T(8,128)(2,1)} %get-tuple-element.36), channel_id=1, source_target_pairs={{0,32},{32,64},{64,96},{96,0},{128,160},{160,192},{192,224},{224,1... | collective-permute-start | bytes 786440 | tf_op jit(solution)/shard_map/ppermute | solution.py:139
  96.4 15.0 %collective-permute-start.1 = (bf16[512,256]{1,0:T(8,128)(2,1)}, bf16[512,256]{1,0:T(8,128)(2,1)S(1)}, u32[]{:S(2)}, u32[]{:S(2)}) collective-permute-start(bf16[512,256]{1,0:T(8,128)(2,1)} %get-tuple-element.37), channel_id=1, source_target_pairs={{0,64},{32,96},{64,0},{96,32},{128,192},{160,224},{192,128},{224,1... | collective-permute-start | bytes 786440 | tf_op jit(solution)/shard_map/ppermute | solution.py:139
  101.2 11.5 %collective-permute-start.2 = (bf16[512,256]{1,0:T(8,128)(2,1)S(1)}, bf16[512,256]{1,0:T(8,128)(2,1)S(1)}, u32[]{:S(2)}, u32[]{:S(2)}) collective-permute-start(bf16[512,256]{1,0:T(8,128)(2,1)S(1)} %get-tuple-element.38), channel_id=1, source_target_pairs={{0,96},{32,0},{64,32},{96,64},{128,224},{160,128},{192,160},{224,1... | collective-permute-start | bytes 786440 | tf_op jit(solution)/shard_map/ppermute | solution.py:139
  113.0 22.5 %collective-permute-start.3 = (bf16[256,256]{1,0:T(8,128)(2,1)S(1)}, bf16[256,256]{1,0:T(8,128)(2,1)S(1)}, u32[]{:S(2)}, u32[]{:S(2)}) collective-permute-start(bf16[256,256]{1,0:T(8,128)(2,1)S(1)} %get-tuple-element.40), channel_id=1, source_target_pairs={{0,256},{32,288},{64,320},{96,352},{128,384},{160,416},{192,448},{... | collective-permute-start | bytes 393224 | tf_op jit(solution)/shard_map/ppermute | solution.py:144
  135.6 48.1 %copy-start.4 = (bf16[256,256]{1,0:T(8,128)(2,1)S(1)}, bf16[256,256]{1,0:T(8,128)(2,1)}, u32[]{:S(2)}) copy-start(bf16[256,256]{1,0:T(8,128)(2,1)} %left_up_ref.3) | copy-start | bytes 393220
  135.6 48.1 %copy-start.5 = (bf16[256,256]{1,0:T(8,128)(2,1)S(1)}, bf16[256,256]{1,0:T(8,128)(2,1)}, u32[]{:S(2)}) copy-start(bf16[256,256]{1,0:T(8,128)(2,1)} %right_down_ref.3) | copy-start | bytes 393220
  135.6 8.0 %collective-permute-start.4 = (bf16[256,256]{1,0:T(8,128)(2,1)S(1)}, bf16[256,256]{1,0:T(8,128)(2,1)S(1)}, u32[]{:S(2)}, u32[]{:S(2)}) collective-permute-start(bf16[256,256]{1,0:T(8,128)(2,1)S(1)} %add_convert_fusion.1), channel_id=1, source_target_pairs={{0,128},{32,160},{64,192},{96,224},{128,0},{160,32},{192,64},{224,... | collective-permute-start | bytes 393224 | tf_op jit(solution)/shard_map/ppermute | solution.py:144
  144.8 21.0 %all-to-all-start.2 = ((bf16[16,32,256]{2,1,0:T(8,128)(2,1)}), bf16[16,32,256]{2,1,0:T(8,128)(2,1)S(1)}, u32[]{:S(2)}, u32[]{:S(2)}) async-start(bf16[16,32,256]{2,1,0:T(8,128)(2,1)} %bitcast.7), calls=%async_computation.2 | async-start | bytes 524288 | tf_op jit(solution)/shard_map/all_to_all | solution.py:162
  151.5 14.4 %collective-permute-start.5 = (bf16[256,256]{1,0:T(8,128)(2,1)S(1)}, bf16[256,256]{1,0:T(8,128)(2,1)S(1)}, u32[]{:S(2)}, u32[]{:S(2)}) collective-permute-start(bf16[256,256]{1,0:T(8,128)(2,1)S(1)} %add_convert_fusion.own_ref), channel_id=1, source_target_pairs={{0,256},{32,288},{64,320},{96,352},{128,384},{160,416},{192,448},{... | collective-permute-start | bytes 393224 | tf_op jit(solution)/shard_map/ppermute | solution.py:144
  166.6 24.4 %all-to-all-start.3 = ((bf16[16,32,256]{2,1,0:T(8,128)(2,1)}), bf16[16,32,256]{2,1,0:T(8,128)(2,1)S(1)}, u32[]{:S(2)}, u32[]{:S(2)}) async-start(bf16[16,32,256]{2,1,0:T(8,128)(2,1)} %get-tuple-element.48), calls=%async_computation.3 | async-start | bytes 524288 | tf_op jit(solution)/shard_map/all_to_all | solution.py:162
  171.9 13.3 %collective-permute-start.6 = (bf16[512,256]{1,0:T(8,128)(2,1)S(1)}, bf16[512,256]{1,0:T(8,128)(2,1)S(1)}, u32[]{:S(2)}, u32[]{:S(2)}) collective-permute-start(bf16[512,256]{1,0:T(8,128)(2,1)S(1)} %get-tuple-element.49.own_ref), channel_id=1, source_target_pairs={{0,32},{32,64},{64,96},{96,0},{128,160},{160,192},{192,224},{224,1... | collective-permute-start | bytes 786440 | tf_op jit(solution)/shard_map/ppermute | solution.py:139
  175.7 15.0 %collective-permute-start.7 = (bf16[512,256]{1,0:T(8,128)(2,1)S(1)}, bf16[512,256]{1,0:T(8,128)(2,1)S(1)}, u32[]{:S(2)}, u32[]{:S(2)}) collective-permute-start(bf16[512,256]{1,0:T(8,128)(2,1)S(1)} %get-tuple-element.49.own_ref), channel_id=1, source_target_pairs={{0,64},{32,96},{64,0},{96,32},{128,192},{160,224},{192,128},{224,1... | collective-permute-start | bytes 786440 | tf_op jit(solution)/shard_map/ppermute | solution.py:139
  180.3 10.7 %collective-permute-start.8 = (bf16[512,256]{1,0:T(8,128)(2,1)S(1)}, bf16[512,256]{1,0:T(8,128)(2,1)S(1)}, u32[]{:S(2)}, u32[]{:S(2)}) collective-permute-start(bf16[512,256]{1,0:T(8,128)(2,1)S(1)} %get-tuple-element.49.own_ref), channel_id=1, source_target_pairs={{0,96},{32,0},{64,32},{96,64},{128,224},{160,128},{192,160},{224,1... | collective-permute-start | bytes 786440 | tf_op jit(solution)/shard_map/ppermute | solution.py:139
